TPU v7x, 32 devices: a whole 2x2x4 slice. The times are simulated.
32 devices in a mesh: dp: 8 (over y, x, core), mp: 4 (over z).
Axes of the slice: x: 2, y: 2, z: 4, core: 2. Of those that a mesh axis runs over, the one named last changes fastest.
Arguments:
- tokens: bfloat16 [16, 1024, 768], P('dp'), may hold values from -6 to 6
- lengths: int32 [16], P('dp'), may hold values from 256 to 1024, as said below
- qkv_weight: bfloat16 [3, 768, 768], P(None, None, 'mp'), may hold values from -0.5 to 0.5
- out_weight: bfloat16 [768, 768], P('mp'), may hold values from -0.3125 to 0.3125
- conv_taps: float32 [12, 33], P('mp'), may hold values from -0.36 to 0.36
- norm1_gain: float32 [768], replicated, may hold values from 0.1 to 1.9
- norm1_bias: float32 [768], replicated, may hold values from -0.5 to 0.5
- norm2_gain: float32 [768], replicated, may hold values from 0.1 to 1.9
- norm2_bias: float32 [768], replicated, may hold values from -0.5 to 0.5
- up_weight: bfloat16 [768, 3072], P(None, 'mp'), may hold values from -0.21875 to 0.21875
- down_weight: bfloat16 [3072, 768], P('mp'), may hold values from -0.109375 to 0.109375
- cotangent: bfloat16 [16, 1024, 768], P('dp'), may hold values from -6 to 6
Outputs:
- output: bfloat16 [16, 1024, 768], P('dp')
- input_grad: bfloat16 [16, 1024, 768], P('dp')
- qkv_grad: float32 [3, 768, 768], P(None, None, 'mp')
- out_grad: float32 [768, 768], P('mp')
- taps_grad: float32 [12, 33], P('mp')
- norm1_gain_grad: float32 [768], replicated
- norm1_bias_grad: float32 [768], replicated
- norm2_gain_grad: float32 [768], replicated
- norm2_bias_grad: float32 [768], replicated
- up_grad: float32 [768, 3072], P(None, 'mp')
- down_grad: float32 [3072, 768], P('mp')
Inputs may be any that keep to these rules, and one draw needn't show every extreme that they name: Each entry of lengths is the document's true length, and at least one document in every draw has length exactly 1024.
All inputs are finite; a program needn't handle non-finite values.
Results may differ from a plain program's by a relative error of at most 0.024.
The roundings to bfloat16 on the way count: a program that leaves them out, or rounds other values in their place, can miss the bound.
Values may be sent and summed in bfloat16 or wider, within the bound.
A program may use at most 256 MiB of HBM per device.

v0:
```python
import jax
import jax.numpy as jnp
from jax import lax
from jax.sharding import PartitionSpec as P

HEAD_DIM = 64
LANDMARKS = 64
KSIZE = 33
NS_ITERS = 6


EPSILON = 1e-05
FULL_PRECISION = lax.Precision.HIGHEST


def layer_norm(values, gain_vec, shift_vec):
    average = jnp.mean(values, axis=-1, keepdims=True)
    centered = values - average
    variance = jnp.mean(centered * centered, axis=-1, keepdims=True)
    return centered * lax.rsqrt(variance + EPSILON) * gain_vec + shift_vec


def newton_schulz(kernel):
    identity_m = jnp.eye(kernel.shape[-1], dtype=kernel.dtype)
    total_sq = jnp.sum(kernel * kernel, axis=(1, 2), keepdims=True)
    kernel_inverse = jnp.swapaxes(kernel, 1, 2) / total_sq
    for sweep_no in range(NS_ITERS):
        product = jnp.einsum("hij,hjk->hik", kernel, kernel_inverse, precision=FULL_PRECISION)
        inner_term = 7.0 * identity_m - product
        inner_term = 15.0 * identity_m - jnp.einsum(
            "hij,hjk->hik", product, inner_term, precision=FULL_PRECISION
        )
        inner_term = 13.0 * identity_m - jnp.einsum(
            "hij,hjk->hik", product, inner_term, precision=FULL_PRECISION
        )
        kernel_inverse = 0.25 * jnp.einsum(
            "hij,hjk->hik", kernel_inverse, inner_term, precision=FULL_PRECISION
        )
    return kernel_inverse


def pinv_from(landmark_queries, landmark_keys):
    scores_scale_factor = HEAD_DIM ** (-0.5)
    second_scores = (
        jnp.einsum("ble,gle->lbg", landmark_queries, landmark_keys, precision=FULL_PRECISION)
        * scores_scale_factor
    )
    return newton_schulz(jax.nn.softmax(second_scores, axis=-1))


def depthwise(values, tap_weights):
    half_span = (KSIZE - 1) // 2
    seq_len = values.shape[0]
    padded = jnp.pad(values, ((half_span, half_span), (0, 0), (0, 0)))
    running = jnp.zeros_like(values)
    for offset in range(KSIZE):
        running = (
            running + padded[offset : offset + seq_len] * tap_weights[:, offset][None, :, None]
        )
    return running


def gelu_exact(values):
    return jax.nn.gelu(values, approximate=False)


def landmark_table(length, seq_len):
    places = jnp.arange(seq_len, dtype=jnp.int32)
    live_flag = places < length
    segment = places * LANDMARKS // length
    segment_membership = (
        (segment[None, :] == jnp.arange(LANDMARKS, dtype=jnp.int32)[:, None]) & live_flag[None, :]
    ).astype(jnp.float32)
    landmark_counts = jnp.sum(segment_membership, axis=1)
    return (segment_membership, landmark_counts, live_flag)


def masked_scores(landmark_queries, key_matrix, live_flag):
    scores_scale_factor = HEAD_DIM ** (-0.5)
    third_scores = (
        jnp.einsum("xyk,pyk->yxp", landmark_queries, key_matrix, preferred_element_type=jnp.float32)
        * scores_scale_factor
    )
    return jnp.where(live_flag[None, None, :], third_scores, -1e30)


def attend_forward(query_matrix, key_matrix, value_matrix, length, tap_weights):
    scores_scale_factor = HEAD_DIM ** (-0.5)
    seq_len = query_matrix.shape[0]
    segment_membership, landmark_counts, live_flag = landmark_table(length, seq_len)
    live_f = live_flag.astype(jnp.float32)
    membership_batch = segment_membership.astype(jnp.bfloat16)
    landmark_queries = (
        jnp.einsum(
            "ov,vaf->oaf", membership_batch, query_matrix, preferred_element_type=jnp.float32
        )
        / landmark_counts[:, None, None]
    ).astype(jnp.bfloat16)
    landmark_keys = (
        jnp.einsum("ov,vaf->oaf", membership_batch, key_matrix, preferred_element_type=jnp.float32)
        / landmark_counts[:, None, None]
    ).astype(jnp.bfloat16)
    first_scores = (
        jnp.einsum("wxe,pxe->xwp", query_matrix, landmark_keys, preferred_element_type=jnp.float32)
        * scores_scale_factor
    )
    lse_one = jax.nn.logsumexp(first_scores, axis=-1)
    first_kernel = jnp.exp(first_scores - lse_one[..., None]).astype(jnp.bfloat16)
    kernel_inverse = pinv_from(
        landmark_queries.astype(jnp.float32), landmark_keys.astype(jnp.float32)
    )
    third_scores = masked_scores(landmark_queries, key_matrix, live_flag)
    lse_three = jax.nn.logsumexp(third_scores, axis=-1)
    third_kernel = jnp.exp(third_scores - lse_three[..., None]).astype(jnp.bfloat16)
    landmark_summary = jnp.einsum(
        "olp,pon->oln", third_kernel, value_matrix, preferred_element_type=jnp.float32
    )
    mixing_matrix = jnp.einsum(
        "lcb,lbf->lcf", kernel_inverse, landmark_summary, precision=FULL_PRECISION
    ).astype(jnp.bfloat16)
    landmark_approximation = jnp.einsum(
        "wpb,wbi->pwi", first_kernel, mixing_matrix, preferred_element_type=jnp.float32
    )
    masked_v = value_matrix.astype(jnp.float32) * live_f[:, None, None]
    local_term = depthwise(masked_v, tap_weights)
    context = ((landmark_approximation + local_term) * live_f[:, None, None]).astype(jnp.bfloat16)
    return (
        context,
        (
            landmark_queries,
            landmark_keys,
            lse_one,
            lse_three,
            kernel_inverse,
            landmark_summary,
            mixing_matrix,
        ),
    )


def attend_backward(
    query_matrix, key_matrix, value_matrix, length, tap_weights, kept_state, grad_context
):
    (
        landmark_queries,
        landmark_keys,
        lse_one,
        lse_three,
        kernel_inverse,
        landmark_summary,
        mixing_matrix,
    ) = kept_state
    scores_scale_factor = HEAD_DIM ** (-0.5)
    seq_len = query_matrix.shape[0]
    segment_membership, landmark_counts, live_flag = landmark_table(length, seq_len)
    live_f = live_flag.astype(jnp.float32)
    grad_local = grad_context.astype(jnp.float32) * live_f[:, None, None]
    local_branch_gradient = grad_local.astype(jnp.bfloat16)
    masked_v = value_matrix.astype(jnp.float32) * live_f[:, None, None]
    unused, conv_pull = jax.vjp(depthwise, masked_v, tap_weights)
    grad_masked, grad_taps = conv_pull(grad_local)
    first_scores = (
        jnp.einsum("wxe,pxe->xwp", query_matrix, landmark_keys, preferred_element_type=jnp.float32)
        * scores_scale_factor
    )
    first_kernel = jnp.exp(first_scores - lse_one[..., None])
    mixing_gradient = jnp.einsum(
        "paj,ape->pje",
        first_kernel.astype(jnp.bfloat16),
        local_branch_gradient,
        preferred_element_type=jnp.float32,
    )
    grad_kernel_one = jnp.einsum(
        "upn,pyn->puy", local_branch_gradient, mixing_matrix, preferred_element_type=jnp.float32
    )
    first_scores_gradient = (
        first_kernel
        * (grad_kernel_one - jnp.sum(grad_kernel_one * first_kernel, axis=-1, keepdims=True))
    ).astype(jnp.bfloat16)
    inverse_gradient = jnp.einsum(
        "xfe,xge->xfg", mixing_gradient, landmark_summary, precision=FULL_PRECISION
    )
    summary_gradient = jnp.einsum(
        "exa,exu->eau", kernel_inverse, mixing_gradient, precision=FULL_PRECISION
    ).astype(jnp.bfloat16)
    third_scores = masked_scores(landmark_queries, key_matrix, live_flag)
    third_kernel = jnp.exp(third_scores - lse_three[..., None])
    grad_kernel_three = jnp.einsum(
        "jbq,kjq->jbk", summary_gradient, value_matrix, preferred_element_type=jnp.float32
    )
    third_scores_gradient = (
        third_kernel
        * (grad_kernel_three - jnp.sum(grad_kernel_three * third_kernel, axis=-1, keepdims=True))
    ).astype(jnp.bfloat16)
    unused_inv, pinv_pull = jax.vjp(
        pinv_from, landmark_queries.astype(jnp.float32), landmark_keys.astype(jnp.float32)
    )
    landmark_query_gradient, landmark_key_gradient = pinv_pull(inverse_gradient)
    landmark_query_gradient = (
        landmark_query_gradient
        + jnp.einsum(
            "tni,itu->ntu", third_scores_gradient, key_matrix, preferred_element_type=jnp.float32
        )
        * scores_scale_factor
    )
    landmark_key_gradient = (
        landmark_key_gradient
        + jnp.einsum(
            "nxc,xnk->cnk", first_scores_gradient, query_matrix, preferred_element_type=jnp.float32
        )
        * scores_scale_factor
    )
    spread_q = jnp.einsum(
        "bq,brw->qrw",
        segment_membership,
        landmark_query_gradient / landmark_counts[:, None, None],
        precision=FULL_PRECISION,
    )
    spread_k = jnp.einsum(
        "bq,brw->qrw",
        segment_membership,
        landmark_key_gradient / landmark_counts[:, None, None],
        precision=FULL_PRECISION,
    )
    grad_query = (
        jnp.einsum(
            "nfc,cnk->fnk", first_scores_gradient, landmark_keys, preferred_element_type=jnp.float32
        )
        * scores_scale_factor
        + spread_q
    )
    grad_key = (
        jnp.einsum(
            "zpw,pzv->wzv",
            third_scores_gradient,
            landmark_queries,
            preferred_element_type=jnp.float32,
        )
        * scores_scale_factor
        + spread_k
    )
    grad_value = (
        jnp.einsum(
            "zrb,zrc->bzc",
            third_kernel.astype(jnp.bfloat16),
            summary_gradient,
            preferred_element_type=jnp.float32,
        )
        + grad_masked * live_f[:, None, None]
    )
    return (
        grad_query.astype(jnp.bfloat16),
        grad_key.astype(jnp.bfloat16),
        grad_value.astype(jnp.bfloat16),
        grad_taps,
    )


def body(
    tokens,
    lengths,
    qkv_weight,
    out_weight,
    conv_taps,
    norm1_gain,
    norm1_bias,
    norm2_gain,
    norm2_bias,
    up_weight,
    down_weight,
    cotangent,
):
    slot_count, seq_len, model_width = tokens.shape
    row_count = slot_count * seq_len
    local_heads = conv_taps.shape[0]
    local_width = local_heads * HEAD_DIM
    flat = tokens.reshape(row_count, model_width)
    places = jnp.arange(seq_len, dtype=jnp.int32)
    live_rows = (places[None, :] < lengths[:, None]).astype(jnp.float32).reshape(row_count)
    projected = jnp.einsum(
        "rd,tdc->trc", flat, qkv_weight, preferred_element_type=jnp.float32
    ).astype(jnp.bfloat16)
    per_head = projected.reshape(3, slot_count, seq_len, local_heads, HEAD_DIM)
    attend_all = jax.vmap(attend_forward, in_axes=(0, 0, 0, 0, None))
    context, kept_state = attend_all(per_head[0], per_head[1], per_head[2], lengths, conv_taps)
    context_flat = context.reshape(row_count, local_width)
    attn_part = jnp.einsum(
        "rc,cd->rd", context_flat, out_weight, preferred_element_type=jnp.float32
    )
    attn_out = lax.psum(attn_part.astype(jnp.bfloat16), "mp").astype(jnp.float32)
    mixed = flat.astype(jnp.float32) + attn_out
    normed, ln_one_pull = jax.vjp(layer_norm, mixed, norm1_gain, norm1_bias)
    normed_b = normed.astype(jnp.bfloat16)
    hidden_pre = jnp.einsum("rd,df->rf", normed_b, up_weight, preferred_element_type=jnp.float32)
    activated, gelu_pull = jax.vjp(gelu_exact, hidden_pre)
    activated_b = activated.astype(jnp.bfloat16)
    branch_part = jnp.einsum(
        "rf,fd->rd", activated_b, down_weight, preferred_element_type=jnp.float32
    )
    branch = lax.psum(branch_part.astype(jnp.bfloat16), "mp").astype(jnp.float32)
    final_norm, ln_two_pull = jax.vjp(layer_norm, normed + branch, norm2_gain, norm2_bias)
    output = (
        (final_norm * live_rows[:, None])
        .astype(jnp.bfloat16)
        .reshape(slot_count, seq_len, model_width)
    )
    grad_out = cotangent.reshape(row_count, model_width).astype(jnp.float32) * live_rows[:, None]
    grad_resid, grad_gain_two, grad_bias_two = ln_two_pull(grad_out)
    grad_branch_b = grad_resid.astype(jnp.bfloat16)
    grad_down = jnp.einsum(
        "rf,rd->fd", activated_b, grad_branch_b, preferred_element_type=jnp.float32
    )
    grad_act = jnp.einsum(
        "rd,fd->rf", grad_branch_b, down_weight, preferred_element_type=jnp.float32
    )
    grad_pre = gelu_pull(grad_act)[0].astype(jnp.bfloat16)
    grad_up = jnp.einsum("rd,rf->df", normed_b, grad_pre, preferred_element_type=jnp.float32)
    normed_part = jnp.einsum("rf,df->rd", grad_pre, up_weight, preferred_element_type=jnp.float32)
    grad_normed = grad_resid + lax.psum(normed_part.astype(jnp.bfloat16), "mp").astype(jnp.float32)
    grad_mixed, grad_gain_one, grad_bias_one = ln_one_pull(grad_normed)
    small_grads = jnp.stack([grad_gain_one, grad_bias_one, grad_gain_two, grad_bias_two])
    grad_attn_b = grad_mixed.astype(jnp.bfloat16)
    grad_outw = jnp.einsum(
        "rc,rd->cd", context_flat, grad_attn_b, preferred_element_type=jnp.float32
    )
    grad_context = jnp.einsum(
        "rd,cd->rc", grad_attn_b, out_weight, preferred_element_type=jnp.float32
    ).astype(jnp.bfloat16)
    grad_context = grad_context.reshape(slot_count, seq_len, local_heads, HEAD_DIM)
    back_all = jax.vmap(attend_backward, in_axes=(0, 0, 0, 0, None, 0, 0))
    grad_query, grad_key, grad_value, grad_taps = back_all(
        per_head[0], per_head[1], per_head[2], lengths, conv_taps, kept_state, grad_context
    )
    grad_proj = jnp.stack([grad_query, grad_key, grad_value]).reshape(3, row_count, local_width)
    grad_qkv = jnp.einsum("rd,trc->tdc", flat, grad_proj, preferred_element_type=jnp.float32)
    input_part = jnp.einsum(
        "trc,tdc->rd", grad_proj, qkv_weight, preferred_element_type=jnp.float32
    )
    input_grad = (
        grad_mixed + lax.psum(input_part.astype(jnp.bfloat16), "mp").astype(jnp.float32)
    ).astype(jnp.bfloat16)
    input_grad = input_grad.reshape(slot_count, seq_len, model_width)
    taps_pad = jnp.pad(jnp.sum(grad_taps, axis=0), ((0, 0), (0, model_width - KSIZE)))
    shares = (
        lax.psum_scatter(grad_qkv, "dp", scatter_dimension=1, tiled=True),
        lax.psum_scatter(grad_outw, "dp", scatter_dimension=1, tiled=True),
        lax.psum_scatter(taps_pad, "dp", scatter_dimension=1, tiled=True),
        lax.psum_scatter(grad_up, "dp", scatter_dimension=0, tiled=True),
        lax.psum_scatter(grad_down, "dp", scatter_dimension=1, tiled=True),
        lax.psum_scatter(small_grads, "dp", scatter_dimension=1, tiled=True),
    )
    sync_qkv, sync_outw, sync_taps, sync_up, sync_down, sync_small = (
        lax.all_gather(shares[0].astype(jnp.bfloat16), "dp", axis=1, tiled=True).astype(
            jnp.float32
        ),
        lax.all_gather(shares[1].astype(jnp.bfloat16), "dp", axis=1, tiled=True).astype(
            jnp.float32
        ),
        lax.all_gather(shares[2].astype(jnp.bfloat16), "dp", axis=1, tiled=True).astype(
            jnp.float32
        ),
        lax.all_gather(shares[3].astype(jnp.bfloat16), "dp", axis=0, tiled=True).astype(
            jnp.float32
        ),
        lax.all_gather(shares[4].astype(jnp.bfloat16), "dp", axis=1, tiled=True).astype(
            jnp.float32
        ),
        lax.all_gather(shares[5].astype(jnp.bfloat16), "dp", axis=1, tiled=True).astype(
            jnp.float32
        ),
    )
    return (
        output,
        input_grad,
        sync_qkv,
        sync_outw,
        sync_taps[:, :KSIZE],
        sync_small[0],
        sync_small[1],
        sync_small[2],
        sync_small[3],
        sync_up,
        sync_down,
    )


def solution(mesh):
    return jax.shard_map(
        body,
        mesh=mesh,
        in_specs=(
            P("dp", None, None),
            P("dp"),
            P(None, None, "mp"),
            P("mp", None),
            P("mp", None),
            P(),
            P(),
            P(),
            P(),
            P(None, "mp"),
            P("mp", None),
            P("dp", None, None),
        ),
        out_specs=(
            P("dp", None, None),
            P("dp", None, None),
            P(None, None, "mp"),
            P("mp", None),
            P("mp", None),
            P(),
            P(),
            P(),
            P(),
            P(None, "mp"),
            P("mp", None),
        ),
        check_vma=False,
    )
```

profile of v0, /device:TPU:4, one launch (start us, length us, event | category | flops | bytes accessed | tf_op | source)
XLA Modules:
  0.0 949.9 jit_solution(3927351751233964447)
XLA Ops:
  7.8 2.2 slice_reduce_fusion.35
  10.0 2.5 slice_reduce_fusion.36
  16.2 4.2 fusion.10
  21.5 1.5 squeeze.15
  28.3 2.2 fusion.132
  30.5 2.7 squeeze.16
  51.0 36.9 %fusion.18 = bf16[2,1024,3,64]{1,3,2,0:T(8,128)(2,1)} fusion(f32[2,1024,3,64]{1,3,2,0:T(8,128)} %convert_multiply_fusion, bf16[2,3,64,64]{3,2,1,0:T(8,128)(2,1)} %convolution_convert_fusion.6, f32[3]{0:T(128)} %get-tuple-element.140, f32[3]{0:T(128)} %get-tuple-element.141, f32[3]{0:T(128)} %get-tuple-element.110, f32[3]{0:T(128)} %get-tuple-element.111, ...), kind=kOutput, calls=%fused_computation.63 | convolution fusion | flops 77856768 | bytes 4014476 | tf_op jit(solution)/shard_map/vmap(wpb,wbi->pwi)/dot_general | solution.py:121
  87.9 2.0 copy.226
  91.0 2.7 convolution_convert_fusion.2
  93.8 122.4 %all-reduce.73.cloned.1.call-done = bf16[2048,768]{1,0:T(8,128)(2,1)} async-done(((bf16[2048,768]{1,0:T(8,128)(2,1)}), bf16[2048,768]{1,0:T(8,128)(2,1)}) %all-reduce.73.cloned.1.call-update) | async-done | bytes 3145744 | tf_op jit(solution)/shard_map/psum | solution.py:290
  216.2 3.9 fusion.7
  220.9 2.2 multiply_reduce_fusion.6
  223.2 17.7 %multiply_convert_fusion.1 = (bf16[2048,768]{1,0:T(8,128)(2,1)S(1)}, f32[2048,768]{1,0:T(8,128)}, f32[2048,768]{1,0:T(8,128)}) fusion(bf16[768,768]{1,0:T(8,128)(2,1)S(1)} %copy-done, f32[2048,768]{1,0:T(8,128)S(1)} %get-tuple-element.151, f32[768]{0:T(1024)S(1)} %copy-done.118, f32[768]{0:T(1024)S(1)} %copy-done.106, f32[2048]{0:T(1024)S(1)} %fusion.107), kind=kOutput, calls=%fused_computation.17 | convolution fusion | flops 2524446720 | bytes 23214080 | tf_op jit(solution)/shard_map/rd,df->rf/dot_general | solution.py:294
  240.9 1.8 copy-done.162
  242.7 3.9 convolution_convert_fusion.1
  247.3 119.6 %all-reduce.75.cloned.1.call-done = bf16[2048,768]{1,0:T(8,128)(2,1)} async-done(((bf16[2048,768]{1,0:T(8,128)(2,1)}), bf16[2048,768]{1,0:T(8,128)(2,1)}) %all-reduce.75.cloned.1.call-update) | async-done | bytes 3145744 | tf_op jit(solution)/shard_map/psum | solution.py:300
  366.9 4.6 fusion.126
  373.4 2.6 multiply_reduce_fusion.1
  376.1 4.9 fusion.125
  381.0 4.6 add_convert_fusion.1
  385.7 1.7 copy-done.160
  387.4 4.0 convolution_convert_fusion
  391.6 7.9 fusion.112
  399.6 2.7 multiply_reduce_fusion
  403.5 7.1 fusion.114
  410.7 101.0 %all-reduce.77.cloned.1.call-done = bf16[2048,768]{1,0:T(8,128)(2,1)} async-done(((bf16[2048,768]{1,0:T(8,128)(2,1)}), bf16[2048,768]{1,0:T(8,128)(2,1)}) %all-reduce.77.cloned.1.call-update) | async-done | bytes 3145744 | tf_op jit(solution)/shard_map/psum | solution.py:319
  511.6 7.0 multiply_reduce_fusion.2
  518.7 6.6 fusion.124
  525.3 2.6 copy-done.6
  528.0 2.5 fusion.11
  530.5 2.8 reshape.458
  533.4 2.2 fusion.58
  561.5 7.8 multiply_reduce_fusion.39
  569.3 8.2 multiply_reduce_fusion.38
  579.8 2.2 multiply_reduce_fusion.40
  584.7 1.9 multiply_reduce_fusion.41
  586.7 2.6 convolution_bitcast_fusion.1
  591.2 1.9 fusion.56
  593.2 2.4 multiply_convert_fusion.3
  598.1 8.6 broadcast_multiply_fusion.1
  606.9 1.6 convert_element_type.249
  609.4 9.5 %broadcast_multiply_fusion = (f32[2,1024,3,64]{1,3,2,0:T(8,128)}, f32[2,1024,3,64]{1,3,2,0:T(8,128)}, f32[2,1024,3,64]{1,3,2,0:T(8,128)}, f32[2,1024,3,64]{1,3,2...) fusion(f32[3]{0:T(128)S(1)} %copy-done.142, ...), kind=kLoop, calls=%fused_computation.230 | loop fusion | flops 7077888 | bytes 28319948 | tf_op jit(solution)/shard_map/vmap(transpose(jvp()))/mul | solution.py:58
  619.0 20.5 %pad_add_fusion = f32[2,1056,3,64]{1,3,2,0:T(8,128)} fusion(f32[2,1024,3,64]{1,3,2,0:T(8,128)} %get-tuple-element.160, f32[2,1024,3,64]{1,3,2,0:T(8,128)} %get-tuple-element.161, f32[2,1024,3,64]{1,3,2,0:T(8,128)} %get-tuple-element.162, f32[2,1024,3,64]{1,3,2,0:T(8,128)} %get-tuple-element.163, f32[2,1024,3,64]{1,3,2,0:T(8,128)} %get-tuple-element.164, ...), kind=kLoop, calls=%fused_computation.47 | loop fusion | flops 10543104 | bytes 44089344 | tf_op jit(solution)/shard_map/vmap(transpose(jvp()))/add_any | solution.py:58
  639.6 1.6 convert_element_type.247
  643.7 1.5 fusion.15
  646.1 1.5 stack.20
  647.6 7.5 fusion.14
  659.1 2.0 convolution_bitcast_fusion
  661.1 2.7 copy.302
  663.8 4.8 reshape.471
  669.8 4.0 bitcast_convert_fusion
  674.8 8.8 all-gather
  685.2 7.9 all-gather.1
  693.8 22.2 %reduce-scatter.21.cloned.1.call-done = f32[96,192]{1,0:T(8,128)} async-done(((f32[768,192]{1,0:T(8,128)}), f32[96,192]{1,0:T(8,128)}) %reduce-scatter.21.cloned.1.call-update) | async-done | bytes 73744
  717.1 8.7 all_gather.19
  726.7 15.3 %all-gather.7.cloned.1.call-done = bf16[768,768]{0,1:T(8,128)(2,1)} async-done(((bf16[768,96]{0,1:T(8,128)(2,1)}), bf16[768,768]{0,1:T(8,128)(2,1)}) %all-gather.7.cloned.1.call-update) | async-done | bytes 1179664 | tf_op jit(solution)/shard_map/all_gather | solution.py:365
  742.0 2.7 copy.268
  744.7 23.7 %all-gather.5.cloned.1.call-done = bf16[768,768]{1,0:T(8,128)(2,1)} async-done(((bf16[96,768]{1,0:T(8,128)(2,1)}), bf16[768,768]{1,0:T(8,128)(2,1)}) %all-gather.5.cloned.1.call-update) | async-done | bytes 1179664 | tf_op jit(solution)/shard_map/all_gather | solution.py:362
  768.4 2.8 convert_element_type.248
  771.2 40.9 %reduce-scatter.19.cloned.1.call-done = f32[96,576]{1,0:T(8,128)} async-done(((f32[768,576]{1,0:T(8,128)}), f32[96,576]{1,0:T(8,128)}) %reduce-scatter.19.cloned.1.call-update) | async-done | bytes 221200
  813.6 12.2 %all_gather.18 = bf16[3,768,192]{2,0,1:T(4,128)(2,1)S(1)} all-gather(bf16[3,96,192]{2,0,1:T(4,128)(2,1)S(1)} %copy.261), channel_id=1, replica_groups=mesh['dp'=8,'mp'=4] {'dp'}, dimensions={1}, use_global_device_ids=true | all-gather | bytes 995328 | tf_op jit(solution)/shard_map/all_gather | solution.py:353
  825.8 2.2 copy.266
  828.0 108.3 %all-reduce.79.cloned.1.call-done = bf16[2048,768]{1,0:T(8,128)(2,1)} async-done(((bf16[2048,768]{1,0:T(8,128)(2,1)}), bf16[2048,768]{1,0:T(8,128)(2,1)}) %all-reduce.79.cloned.1.call-update) | async-done | bytes 3145744 | tf_op jit(solution)/shard_map/psum | solution.py:340
  936.2 6.3 add_convert_fusion
  (518 shorter events, 84.2 us)
Async XLA Ops:
  7.2 216.0 %copy-start = (bf16[768,768]{1,0:T(8,128)(2,1)S(1)}, bf16[768,768]{1,0:T(8,128)(2,1)}, u32[]{:S(2)}) copy-start(bf16[768,768]{1,0:T(8,128)(2,1)} %param.23) | copy-start | bytes 3538948
  7.2 209.0 %all-reduce.73.cloned.1.call-start = ((), (), s32[]{:S(2)}) async-start(), calls=%async_computation.6 | async-start | bytes 6291456 | tf_op jit(solution)/shard_map/psum | solution.py:290
  15.0 11.0 %copy-start.99 = (pred[2,1024]{1,0:T(4,128)(4,1)}, pred[2,1024]{1,0:T(4,128)(4,1)S(1)}, u32[]{:S(2)}) copy-start(pred[2,1024]{1,0:T(4,128)(4,1)S(1)} %get-tuple-element.191) | copy-start | bytes 6148
  23.5 4.8 copy-start.36
  25.5 2.8 copy-start.85
  26.7 3.8 copy-start.83
  27.3 18.0 %copy-start.104 = (f32[2,3,64]{2,1,0:T(4,128)}, f32[2,3,64]{2,1,0:T(4,128)S(1)}, u32[]{:S(2)}) copy-start(f32[2,3,64]{2,1,0:T(4,128)S(1)} %get-tuple-element.194) | copy-start | bytes 4612
  27.3 20.5 %copy-start.3 = (f32[2,3,64,1024]{3,2,1,0:T(8,128)}, f32[2,3,64,1024]{3,2,1,0:T(8,128)S(1)}, u32[]{:S(2)}) copy-start(f32[2,3,64,1024]{3,2,1,0:T(8,128)S(1)} %get-tuple-element.195) | copy-start | bytes 4718596
  34.4 9.3 copy-start.17
  35.1 2.6 copy-start.19
  45.3 4.7 copy-start.77
  48.3 2.7 copy-start.9
  87.9 3.1 copy-start.82
  93.8 273.1 %all-reduce.75.cloned.1.call-start = ((), (), s32[]{:S(2)}) async-start(), calls=%async_computation.7 | async-start | bytes 6291456 | tf_op jit(solution)/shard_map/psum | solution.py:300
  216.2 3.9 copy-start.14
  216.2 4.7 copy-start.16
  223.1 17.8 %copy-start.2 = (f32[2048,768]{1,0:T(8,128)}, f32[2048,768]{1,0:T(8,128)S(1)}, u32[]{:S(2)}) copy-start(f32[2048,768]{1,0:T(8,128)S(1)} %get-tuple-element.151) | copy-start | bytes 18874372
  223.2 19.5 %copy-start.155 = (bf16[768,768]{1,0:T(8,128)(2,1)S(1)}, bf16[768,768]{1,0:T(8,128)(2,1)}, u32[]{:S(2)}) copy-start(bf16[768,768]{1,0:T(8,128)(2,1)} %param.24) | copy-start | bytes 3538948
  246.6 265.0 %all-reduce.77.cloned.1.call-start = ((), (), s32[]{:S(2)}) async-start(), calls=%async_computation.8 | async-start | bytes 6291456 | tf_op jit(solution)/shard_map/psum | solution.py:319
  373.4 2.7 copy-start.117
  373.4 7.6 slice-start.2
  373.4 7.6 slice-start.4
  376.1 4.9 slice-start.3
  376.1 4.9 slice-start.5
  381.0 4.7 copy-start.7
  391.4 215.5 %reduce-scatter.17.cloned.1.call-start = ((), (), s32[]{:S(2)}) async-start(), calls=%async_computation.12 | async-start | bytes 2654208 | tf_op jit(solution)/shard_map/reduce_scatter | solution.py:349
  399.5 3.4 copy-start.114
  399.5 240.0 %reduce-scatter.15.cloned.1.call-start = ((), (), s32[]{:S(2)}) async-start(), calls=%async_computation.10 | async-start | bytes 2654208 | tf_op jit(solution)/shard_map/reduce_scatter | solution.py:348
  399.6 3.9 copy-start.161
  410.6 263.3 %reduce-scatter.23.cloned.1.call-start = ((), (), s32[]{:S(2)}) async-start(), calls=%async_computation.16 | async-start | bytes 442368
  511.6 7.0 copy-start.13
  525.3 2.7 copy-start.6
  525.3 5.1 copy-start.101
  530.5 2.9 copy-start.91
  533.3 2.7 copy-start.74
  533.4 3.2 copy-start.49
  548.8 2.7 copy-start.22
  561.5 7.8 copy-start.151
  569.3 9.0 copy-start.66
  577.6 4.9 copy-start.41
  579.8 6.8 slice-start
  582.0 4.6 slice-start.1
  586.6 2.7 copy-start.86
  586.6 2.7 copy-start.115
  586.6 2.7 copy-start.153
  586.7 2.7 copy-start.158
  589.3 95.0 %reduce-scatter.25.cloned.1.call-start = ((), (), s32[]{:S(2)}) async-start(), calls=%async_computation.17 | async-start | bytes 442368
  591.1 124.9 %reduce-scatter.21.cloned.1.call-start = ((), (), s32[]{:S(2)}) async-start(), calls=%async_computation.15 | async-start | bytes 884736
  593.1 148.9 %all-gather.7.cloned.1.call-start = ((), (), s32[]{:S(2)}) async-start(), calls=%async_computation.13 | async-start | bytes 1327104 | tf_op jit(solution)/shard_map/all_gather | solution.py:365
  598.1 10.8 %copy-start.84 = (bf16[2,64,3,64]{3,1,2,0:T(8,128)(2,1)S(1)}, bf16[2,64,3,64]{3,1,2,0:T(8,128)(2,1)}, u32[]{:S(2)}) copy-start(bf16[2,64,3,64]{3,1,2,0:T(8,128)(2,1)} %copy-done.83) | copy-start | bytes 147460
  598.1 10.8 %copy-start.116 = (f32[2,3,64]{2,1,0:T(4,128)S(1)}, f32[2,3,64]{2,1,0:T(4,128)}, u32[]{:S(2)}) copy-start(f32[2,3,64]{2,1,0:T(4,128)} %neg.102) | copy-start | bytes 4612
  598.1 10.8 %copy-start.154 = (f32[2,64]{1,0:T(2,128)S(1)}, f32[2,64]{1,0:T(2,128)}, u32[]{:S(2)}) copy-start(f32[2,64]{1,0:T(2,128)} %copy-done.152) | copy-start | bytes 1540
  598.1 10.8 %copy-start.157 = (f32[2,64,3,64]{3,1,2,0:T(8,128)S(1)}, f32[2,64,3,64]{3,1,2,0:T(8,128)}, u32[]{:S(2)}) copy-start(f32[2,64,3,64]{3,1,2,0:T(8,128)} %fusion.40) | copy-start | bytes 294916
  598.1 10.8 %copy-start.159 = (f32[2,3,64,64]{2,3,1,0:T(8,128)S(1)}, f32[2,3,64,64]{2,3,1,0:T(8,128)}, u32[]{:S(2)}) copy-start(f32[2,3,64,64]{2,3,1,0:T(8,128)} %get-tuple-element.204) | copy-start | bytes 294916
  606.7 2.6 copy-start.137
  606.8 2.6 copy-start.138
  606.8 2.6 copy-start.139
  608.6 159.8 %all-gather.5.cloned.1.call-start = ((), (), s32[]{:S(2)}) async-start(), calls=%async_computation.11 | async-start | bytes 1327104 | tf_op jit(solution)/shard_map/all_gather | solution.py:362
  641.2 170.9 %reduce-scatter.19.cloned.1.call-start = ((), (), s32[]{:S(2)}) async-start(), calls=%async_computation.14 | async-start | bytes 2211840
  656.5 2.6 copy-start.15
  663.8 5.2 copy-start.96
  668.7 267.6 %all-reduce.79.cloned.1.call-start = ((), (), s32[]{:S(2)}) async-start(), calls=%async_computation.9 | async-start | bytes 6291456 | tf_op jit(solution)/shard_map/psum | solution.py:340
  825.8 110.5 %copy-start.103 = (f32[2048]{0:T(1024)S(1)}, f32[2048]{0:T(1024)}, u32[]{:S(2)}) copy-start(f32[2048]{0:T(1024)} %copy-done.101) | copy-start | bytes 24580
  936.2 6.3 copy-start.1
  (117 other events, 203.1 us)
Sparse Core Ops, SparseCore 0:
  93.9 122.2 all-reduce.72
  246.8 120.0 all-reduce.74
  391.5 120.0 all-reduce.76
  515.4 41.5 reduce-scatter.16
  561.1 42.4 reduce-scatter.14
  607.0 33.8 reduce-scatter.22
  644.0 33.8 reduce-scatter.24
  681.0 34.9 reduce-scatter.20
  717.9 24.0 all-gather.6
  744.3 24.0 all-gather.4
  771.8 40.3 reduce-scatter.18
  815.1 121.1 all-reduce.78
where the time goes:
time: 957 us; the launch traced here: 950 us
  waiting for transfers between devices  554 us (58%)
  matrix products  160 us (17%)
  other arithmetic  116 us (12%)
  local copies, waits for them, and re-layouts  62.9 us (7%)
  blocking collectives  37.6 us (4%)
  between operations  17.7 us (2%)
    psum x1, waiting for transfers between devices, body(): lax.psum(attn_part.astype(jnp.bfloat16), 'mp').astype(jnp.float32)  122 us
    psum x1, waiting for transfers between devices, body(): lax.psum(branch_part.astype(jnp.bfloat16), 'mp').astype(jnp.float32)  120 us
    psum x1, waiting for transfers between devices, body(): lax.psum(input_part.astype(jnp.bfloat16), 'mp').astype(jnp.float32)  108 us
    psum x1, waiting for transfers between devices, body(): lax.psum(normed_part.astype(jnp.bfloat16), 'mp').astype(jnp.float32)  101 us
    unnamed x16, waiting for transfers between devices  63.3 us
    unnamed x355, local copies, waits for them, and re-layouts  38.9 us
    dot_general x1, matrix products, attend_forward(): jnp.einsum('wpb,wbi->pwi', first_kernel, mixing_matrix, preferred_element...  36.9 us
    all_gather x1, waiting for transfers between devices, body(): lax.all_gather(shares[3].astype(jnp.bfloat16), 'dp', axis=0, tiled=True)  23.7 us
  transfers between devices with their start and end apart: 12, of which 8 were waited for; matrix products, arithmetic and copies ran while one was open for 19% of the time, Pallas kernels for 0%

commit v1 on v0

v1 whole, which is shorter than its diff:
```python
import functools
import jax
import jax.numpy as jnp
import numpy as np
from jax import lax
from jax.experimental import pallas as pl
from jax.experimental.pallas import tpu as pltpu
from jax.sharding import PartitionSpec as P

HD = 64
LM = 64
KSIZE = 33
HALF = 16
NS_ITERS = 6
EPS = 1e-5
HI = lax.Precision.HIGHEST
BF = jnp.bfloat16
F32 = jnp.float32
SCALE = HD ** -0.5
WIN = 512
BLK = 256


def nn(a, b, precision=None):
    return lax.dot_general(a, b, (((1,), (0,)), ((), ())), precision=precision, preferred_element_type=F32)


def nt(a, b, precision=None):
    return lax.dot_general(a, b, (((1,), (1,)), ((), ())), precision=precision, preferred_element_type=F32)


def tn(a, b, precision=None):
    return lax.dot_general(a, b, (((0,), (0,)), ((), ())), precision=precision, preferred_element_type=F32)


def block_mask(width):
    r = lax.broadcasted_iota(jnp.int32, (width, width), 0) // HD
    c = lax.broadcasted_iota(jnp.int32, (width, width), 1) // HD
    return r == c


def spread(x, heads, mask):
    return jnp.where(mask, jnp.concatenate([x] * heads, axis=0), 0.0)


def members(length, first, count):
    s = lax.broadcasted_iota(jnp.int32, (LM, count), 1) + first
    j = lax.broadcasted_iota(jnp.int32, (LM, count), 0)
    s64 = s * LM
    return (j * length <= s64) & (s64 < (j + 1) * length) & (s < length)


def live_lanes(length, first, count):
    s = lax.broadcasted_iota(jnp.int32, (1, count), 1) + first
    return s < length


def toeplitz(row):
    full = jnp.broadcast_to(row, (BLK, WIN))
    return pltpu.roll(full, 0, 1, stride=1, stride_axis=0)


def windows(x, seq):
    rows = x.shape[0]
    pad = jnp.zeros((rows, 128), x.dtype)
    padded = jnp.concatenate([pad, x, pad], axis=1)
    return [padded[:, b * BLK : b * BLK + WIN] for b in range(seq // BLK)]


def hi_lo(x):
    hi = x.astype(BF)
    return hi, (x - hi.astype(F32)).astype(BF)


def banded(x, row, heads, seq):
    outs = []
    nblk = seq // BLK
    for h in range(heads):
        wins = jnp.concatenate(windows(x[h * HD : (h + 1) * HD], seq), axis=0)
        hi, lo = hi_lo(toeplitz(row[h : h + 1]))
        y = nt(wins, hi) + nt(wins, lo)
        outs.append(jnp.concatenate([y[b * HD : (b + 1) * HD] for b in range(nblk)], axis=1))
    return jnp.concatenate(outs, axis=0)


def attn_fwd_kernel(docs, heads, seq, dest, len_ref, x_ref, wt_ref, taps_ref, qkv_ref, ctx_ref, lq_ref, lk_ref, sum_ref, mix_ref, k2_ref, z_ref, p_ref, l1_ref, l3_ref):
    width = heads * HD
    mask = block_mask(width)
    eye = jnp.where(
        lax.broadcasted_iota(jnp.int32, (width, width), 0) == lax.broadcasted_iota(jnp.int32, (width, width), 1), 1.0, 0.0
    ).astype(F32)
    for d in range(docs):
        for c in range(seq // BLK):
            xc = x_ref[d, c * BLK : (c + 1) * BLK, :]
            qkv_ref[d, :, c * BLK : (c + 1) * BLK] = nt(wt_ref[...], xc).astype(BF)
    k2s = []
    for d in range(docs):
        length = len_ref[d]
        memb = jnp.where(members(length, 0, seq), 1.0, 0.0).astype(F32)
        counts = jnp.maximum(jnp.sum(memb, axis=1, keepdims=True), 1.0)
        memb_b = memb.astype(BF)
        q = qkv_ref[d, 0:width, :]
        k = qkv_ref[d, width : 2 * width, :]
        v = qkv_ref[d, 2 * width : 3 * width, :]
        lq = spread(nt(memb_b, q) / counts, heads, mask).astype(BF)
        lk = spread(nt(memb_b, k) / counts, heads, mask).astype(BF)
        lq_ref[d] = lq
        lk_ref[d] = lk
        s2 = jnp.where(mask, nt(lq, lk) * SCALE, -1e30)
        e2 = jnp.where(mask, jnp.exp(s2 - jnp.max(s2, axis=1, keepdims=True)), 0.0)
        k2 = e2 / jnp.sum(e2, axis=1, keepdims=True)
        k2_ref[d] = k2
        k2s.append(k2)
        s3 = jnp.where(live_lanes(length, 0, seq), nn(lq, k) * SCALE, -1e30)
        m3 = jnp.max(s3, axis=1, keepdims=True)
        e3 = jnp.exp(s3 - m3)
        t3 = jnp.sum(e3, axis=1, keepdims=True)
        l3_ref[d] = jnp.broadcast_to(m3 + jnp.log(t3), (width, 128))
        k3 = (e3 / t3).astype(BF)
        sum_ref[d] = jnp.where(mask, nt(k3, v), 0.0)
    zs = []
    for d in range(docs):
        rows = jnp.sum(k2s[d] * k2s[d], axis=1, keepdims=True)
        tot = jnp.sum(rows.reshape(heads, HD, 1), axis=1, keepdims=True)
        tot = jnp.broadcast_to(tot, (heads, HD, 1)).reshape(width, 1)
        z = k2s[d].T / tot
        z_ref[d, 0] = z
        zs.append(z)
    for i in range(NS_ITERS):
        ps = [nn(k2s[d], zs[d], HI) for d in range(docs)]
        bs = [15.0 * eye - nn(ps[d], 7.0 * eye - ps[d], HI) for d in range(docs)]
        cs = [13.0 * eye - nn(ps[d], bs[d], HI) for d in range(docs)]
        zs = [0.25 * nn(zs[d], cs[d], HI) for d in range(docs)]
        for d in range(docs):
            p_ref[d, i, 0] = ps[d]
            p_ref[d, i, 1] = bs[d]
            p_ref[d, i, 2] = cs[d]
            z_ref[d, i + 1] = zs[d]
    for d in range(docs):
        length = len_ref[d]
        q = qkv_ref[d, 0:width, :]
        v = qkv_ref[d, 2 * width : 3 * width, :]
        live = live_lanes(length, 0, seq)
        mix = jnp.where(mask, nn(zs[d], sum_ref[d], HI), 0.0)
        mix_ref[d] = mix.astype(BF)
        mix_t = mix.T.astype(BF)
        s1 = (nn(lk_ref[d], q) * SCALE).reshape(heads, LM, seq)
        m1 = jnp.max(s1, axis=1, keepdims=True)
        e1 = jnp.exp(s1 - m1)
        t1 = jnp.sum(e1, axis=1, keepdims=True)
        l1_ref[d] = (m1 + jnp.log(t1)).reshape(heads, seq)
        k1 = (e1 / t1).reshape(width, seq).astype(BF)
        vl = jnp.where(live, v, 0).astype(BF)
        ctx = nn(mix_t, k1) + banded(vl, taps_ref[...], heads, seq)
        ctx = jnp.where(live, ctx, 0.0).astype(BF)
        part = seq // dest
        for i in range(dest):
            ctx_ref[i, d] = ctx[:, i * part : (i + 1) * part]


def attn_fwd(lengths, x, wt, taps, dest):
    docs, seq, dim = x.shape
    width = wt.shape[0] // 3
    heads = width // HD
    vm = pl.BlockSpec(memory_space=pltpu.VMEM)
    out = [
        jax.ShapeDtypeStruct((docs, 3 * width, seq), BF),
        jax.ShapeDtypeStruct((dest, docs, width, seq // dest), BF),
        jax.ShapeDtypeStruct((docs, width, width), BF),
        jax.ShapeDtypeStruct((docs, width, width), BF),
        jax.ShapeDtypeStruct((docs, width, width), F32),
        jax.ShapeDtypeStruct((docs, width, width), BF),
        jax.ShapeDtypeStruct((docs, width, width), F32),
        jax.ShapeDtypeStruct((docs, NS_ITERS + 1, width, width), F32),
        jax.ShapeDtypeStruct((docs, NS_ITERS, 3, width, width), F32),
        jax.ShapeDtypeStruct((docs, heads, seq), F32),
        jax.ShapeDtypeStruct((docs, width, 128), F32),
    ]
    return pl.pallas_call(
        functools.partial(attn_fwd_kernel, docs, heads, seq, dest),
        out_shape=out,
        in_specs=[pl.BlockSpec(memory_space=pltpu.SMEM), vm, vm, vm],
        out_specs=[vm] * len(out),
        compiler_params=pltpu.CompilerParams(vmem_limit_bytes=60 * 2**20),
        cost_estimate=pl.CostEstimate(flops=int(8e9), bytes_accessed=int(3e7), transcendentals=0),
        name="attn_fwd",
    )(lengths, x, wt, taps)


def ln_stats(v):
    mu = jnp.mean(v, axis=-1, keepdims=True)
    cen = v - mu
    var = jnp.mean(cen * cen, axis=-1, keepdims=True)
    r = lax.rsqrt(var + EPS)
    return cen * r, r


def ln_back(g, xhat, r):
    m1 = jnp.mean(g, axis=-1, keepdims=True)
    m2 = jnp.mean(g * xhat, axis=-1, keepdims=True)
    return r * (g - m1 - xhat * m2)


ROOT_HALF = 0.7071067811865476
INV_ROOT_2PI = 0.3989422804014327


def ffn_kernel(groups, docs, rows, len_ref, pos_ref, x_ref, cot_ref, ctx_ref, ow_ref, up_ref, dn_ref, g1_ref, b1_ref, g2_ref, b2_ref,
               out_ref, gmix_ref, gctx_ref, gow_ref, gup_ref, gdn_ref, small_ref, nb_s, fac_s, act_s, br_s, x1_s, gn_s):
    n = docs * rows
    dim = x_ref.shape[-1]
    attn = None
    for g in range(groups):
        for d in range(docs):
            pass
    first = pos_ref[0]
    live = jnp.concatenate(
        [
            (lax.broadcasted_iota(jnp.int32, (rows, 1), 0) + first < len_ref[d]).astype(F32)
            for d in range(docs)
        ],
        axis=0,
    )
    parts = []
    for d in range(docs):
        acc = None
        for g in range(groups):
            t = tn(ctx_ref[g, d], ow_ref[g]).astype(BF).astype(F32)
            acc = t if acc is None else acc + t
        parts.append(acc)
    mixed = x_ref[...].reshape(n, dim).astype(F32) + jnp.concatenate(parts, axis=0)
    xh1, r1 = ln_stats(mixed)
    x1_s[...] = xh1
    normed = xh1 * g1_ref[...] + b1_ref[...]
    nb_s[...] = normed.astype(BF)
    br_s[...] = normed

    def fwd_group(g, _):
        h = nt(nb_s[...], up_ref[g])
        phi_big = 0.5 * (1.0 + lax.erf(h * ROOT_HALF))
        act = (h * phi_big).astype(BF)
        act_s[g] = act
        fac_s[g] = phi_big + h * (jnp.exp(-0.5 * h * h) * INV_ROOT_2PI)
        br_s[...] += nn(act, dn_ref[g]).astype(BF).astype(F32)
        return 0

    lax.fori_loop(0, groups, fwd_group, 0)
    xh2, r2 = ln_stats(br_s[...])
    out_ref[...] = (live * (xh2 * g2_ref[...] + b2_ref[...])).astype(BF).reshape(docs, rows, dim)
    g_out = live * cot_ref[...].reshape(n, dim).astype(F32)
    gg2 = jnp.sum(g_out * xh2, axis=0, keepdims=True)
    gb2 = jnp.sum(g_out, axis=0, keepdims=True)
    g_res = ln_back(g_out * g2_ref[...], xh2, r2)
    gn_s[...] = g_res
    gbr = g_res.astype(BF)

    def bwd_group(g, _):
        act = act_s[g]
        gdn_ref[g] = tn(act, gbr).astype(BF)
        g_pre = (nt(gbr, dn_ref[g]) * fac_s[g]).astype(BF)
        gup_ref[g] = tn(g_pre, nb_s[...]).astype(BF)
        gn_s[...] += nn(g_pre, up_ref[g])
        return 0

    lax.fori_loop(0, groups, bwd_group, 0)
    g_n = gn_s[...]
    xh1 = x1_s[...]
    gg1 = jnp.sum(g_n * xh1, axis=0, keepdims=True)
    gb1 = jnp.sum(g_n, axis=0, keepdims=True)
    small_ref[...] = jnp.concatenate([gg1, gb1, gg2, gb2, jnp.zeros((4, dim), F32)], axis=0)
    g_mix = ln_back(g_n * g1_ref[...], xh1, r1)
    gmix_ref[...] = g_mix.reshape(docs, rows, dim)
    g_att = g_mix.astype(BF)
    for g in range(groups):
        acc = None
        for d in range(docs):
            ga = g_att[d * rows : (d + 1) * rows]
            t = nn(ctx_ref[g, d], ga)
            acc = t if acc is None else acc + t
            gctx_ref[g, d] = nt(ow_ref[g], ga).astype(BF)
        gow_ref[g] = acc.astype(BF)


def ffn(lengths, pos, x, cot, ctx, ow, up, dn, g1, b1, g2, b2):
    docs, rows, dim = x.shape
    groups, _, width, _ = ctx.shape
    ff = up.shape[1]
    n = docs * rows
    vm = pl.BlockSpec(memory_space=pltpu.VMEM)
    sm = pl.BlockSpec(memory_space=pltpu.SMEM)
    out = [
        jax.ShapeDtypeStruct((docs, rows, dim), BF),
        jax.ShapeDtypeStruct((docs, rows, dim), F32),
        jax.ShapeDtypeStruct((groups, docs, width, rows), BF),
        jax.ShapeDtypeStruct((groups, width, dim), BF),
        jax.ShapeDtypeStruct((groups, ff, dim), BF),
        jax.ShapeDtypeStruct((groups, ff, dim), BF),
        jax.ShapeDtypeStruct((8, dim), F32),
    ]
    return pl.pallas_call(
        functools.partial(ffn_kernel, groups, docs, rows),
        out_shape=out,
        in_specs=[sm, sm] + [vm] * 10,
        out_specs=[vm] * len(out),
        scratch_shapes=[
            pltpu.VMEM((n, dim), BF),
            pltpu.VMEM((groups, n, ff), F32),
            pltpu.VMEM((groups, n, ff), BF),
            pltpu.VMEM((n, dim), F32),
            pltpu.VMEM((n, dim), F32),
            pltpu.VMEM((n, dim), F32),
        ],
        compiler_params=pltpu.CompilerParams(vmem_limit_bytes=60 * 2**20),
        cost_estimate=pl.CostEstimate(flops=int(1.8e10), bytes_accessed=int(4e7), transcendentals=0),
        name="ffn",
    )(lengths, pos, x, cot, ctx, ow, up, dn, g1, b1, g2, b2)


def attn_bwd_kernel(docs, heads, seq, parts, len_ref, x_ref, wt_ref, taps_ref, rtaps_ref, qkv_ref, gctx_ref, lq_ref, lk_ref, sum_ref, mix_ref, k2_ref,
                    z_ref, p_ref, l1_ref, l3_ref, gqkv_ref, ipart_ref, gtaps_ref, g_s, ginv_s, glq_s, glk_s):
    width = heads * HD
    nblk = seq // BLK
    mask = block_mask(width)
    anti = jnp.where(
        lax.broadcasted_iota(jnp.int32, (BLK, BLK), 0) + lax.broadcasted_iota(jnp.int32, (BLK, BLK), 1) == BLK - 1, 1.0, 0.0
    ).astype(BF)
    gaccs = [None] * heads
    for d in range(docs):
        length = len_ref[d]
        live = live_lanes(length, 0, seq)
        q = qkv_ref[d, 0:width, :]
        k = qkv_ref[d, width : 2 * width, :]
        v = qkv_ref[d, 2 * width : 3 * width, :]
        gc = jnp.concatenate([gctx_ref[i, d] for i in range(parts)], axis=1)
        gc = jnp.where(live, gc, 0).astype(BF)
        lq, lk = lq_ref[d], lk_ref[d]
        s1 = (nn(lk, q) * SCALE).reshape(heads, LM, seq)
        k1 = jnp.exp(s1 - l1_ref[d].reshape(heads, 1, seq))
        gmixing = jnp.where(mask, nt(k1.reshape(width, seq).astype(BF), gc), 0.0)
        gk1 = nn(mix_ref[d], gc).reshape(heads, LM, seq)
        gs1 = (k1 * (gk1 - jnp.sum(gk1 * k1, axis=1, keepdims=True))).reshape(width, seq).astype(BF)
        ginv_s[d] = nt(gmixing, sum_ref[d], HI)
        gsum = tn(z_ref[d, NS_ITERS], gmixing, HI)
        gsum = jnp.where(mask, gsum, 0.0)
        gsum_b = gsum.astype(BF)
        s3 = jnp.where(live, nn(lq, k) * SCALE, -1e30)
        k3 = jnp.exp(s3 - l3_ref[d][:, 0:1])
        gk3 = nn(gsum_b, v)
        gs3 = (k3 * (gk3 - jnp.sum(gk3 * k3, axis=1, keepdims=True))).astype(BF)
        glq_s[d] = jnp.where(mask, nt(gs3, k), 0.0) * SCALE
        glk_s[d] = jnp.where(mask, nt(gs1, q), 0.0) * SCALE
        lq_t = lq.astype(F32).T.astype(BF)
        lk_t = lk.astype(F32).T.astype(BF)
        g_s[d, 0:width, :] = nn(lk_t, gs1) * SCALE
        g_s[d, width : 2 * width, :] = nn(lq_t, gs3) * SCALE
        gv = nn(gsum.T.astype(BF), k3.astype(BF))
        gvl = banded(gc, rtaps_ref[...], heads, seq)
        g_s[d, 2 * width : 3 * width, :] = gv + jnp.where(live, gvl, 0.0)
        vl = jnp.where(live, v, 0).astype(BF)
        for h in range(heads):
            wins = jnp.concatenate(windows(vl[h * HD : (h + 1) * HD], seq), axis=0)
            gch = gc[h * HD : (h + 1) * HD]
            stack = jnp.concatenate([gch[:, b * BLK : (b + 1) * BLK] for b in range(nblk)], axis=0)
            rev = nt(anti, stack).astype(BF)
            t = nn(rev, wins)
            gaccs[h] = t if gaccs[h] is None else gaccs[h] + t
    for h in range(heads):
        rolled = pltpu.roll(gaccs[h], 0, 1, stride=1, stride_axis=0)
        gtaps_ref[h : h + 1, :] = jnp.sum(rolled, axis=0, keepdims=True)
    gz = [ginv_s[d] for d in range(docs)]
    gk = [jnp.zeros((width, width), F32) for _ in range(docs)]
    eye = jnp.where(
        lax.broadcasted_iota(jnp.int32, (width, width), 0) == lax.broadcasted_iota(jnp.int32, (width, width), 1), 1.0, 0.0
    ).astype(F32)
    for i in reversed(range(NS_ITERS)):
        for d in range(docs):
            z, p, b, c = z_ref[d, i], p_ref[d, i, 0], p_ref[d, i, 1], p_ref[d, i, 2]
            a = 7.0 * eye - p
            g = 0.25 * gz[d]
            gc_ = tn(z, g, HI)
            gzn = nt(g, c, HI)
            gp = -nt(gc_, b, HI)
            gb = -tn(p, gc_, HI)
            gp = gp - nt(gb, a, HI)
            ga = -tn(p, gb, HI)
            gp = gp - ga
            gk[d] = gk[d] + nt(gp, z, HI)
            gz[d] = gzn + tn(k2_ref[d], gp, HI)
    for d in range(docs):
        length = len_ref[d]
        k2 = k2_ref[d]
        rows = jnp.sum(k2 * k2, axis=1, keepdims=True)
        tot = jnp.sum(rows.reshape(heads, HD, 1), axis=1, keepdims=True)
        tot = jnp.broadcast_to(tot, (heads, HD, 1)).reshape(width, 1)
        g = gz[d]
        dot = jnp.sum(g * k2.T, axis=1, keepdims=True)
        dot = jnp.sum(dot.reshape(heads, HD, 1), axis=1, keepdims=True)
        dot = jnp.broadcast_to(dot, (heads, HD, 1)).reshape(width, 1)
        gk2 = gk[d] + (g / tot).T - k2 * (2.0 * dot / (tot * tot))
        gs2 = k2 * (gk2 - jnp.sum(gk2 * k2, axis=1, keepdims=True)) * SCALE
        memb = jnp.where(members(length, 0, seq), 1.0, 0.0).astype(F32)
        counts = jnp.maximum(jnp.sum(memb, axis=1, keepdims=True), 1.0)
        counts = jnp.concatenate([counts] * heads, axis=0)
        memb3 = jnp.concatenate([memb.astype(BF)] * heads, axis=0)
        glq = (glq_s[d] + nn(gs2, lk_ref[d].astype(F32), HI)) / counts
        glk = (glk_s[d] + tn(gs2, lq_ref[d].astype(F32), HI)) / counts
        hi, lo = hi_lo(glq.T)
        gq = g_s[d, 0:width, :] + nn(hi, memb3) + nn(lo, memb3)
        hi, lo = hi_lo(glk.T)
        gkk = g_s[d, width : 2 * width, :] + nn(hi, memb3) + nn(lo, memb3)
        g_all = jnp.concatenate([gq, gkk, g_s[d, 2 * width : 3 * width, :]], axis=0).astype(BF)
        gw = nn(g_all, x_ref[d])
        if d == 0:
            gqkv_ref[...] = gw
        else:
            gqkv_ref[...] += gw
        for c in range(nblk):
            ipart_ref[d, c * BLK : (c + 1) * BLK, :] = tn(g_all[:, c * BLK : (c + 1) * BLK], wt_ref[...]).astype(BF)


def attn_bwd(lengths, x, wt, taps, rtaps, qkv, gctx, lq, lk, sm, mix, k2, z, p, l1, l3):
    docs, seq, dim = x.shape
    width = wt.shape[0] // 3
    heads = width // HD
    parts = gctx.shape[0]
    vm = pl.BlockSpec(memory_space=pltpu.VMEM)
    out = [
        jax.ShapeDtypeStruct((3 * width, dim), F32),
        jax.ShapeDtypeStruct((docs, seq, dim), BF),
        jax.ShapeDtypeStruct((heads, WIN), F32),
    ]
    return pl.pallas_call(
        functools.partial(attn_bwd_kernel, docs, heads, seq, parts),
        out_shape=out,
        in_specs=[pl.BlockSpec(memory_space=pltpu.SMEM)] + [vm] * 15,
        out_specs=[vm] * len(out),
        scratch_shapes=[
            pltpu.VMEM((docs, 3 * width, seq), F32),
            pltpu.VMEM((docs, width, width), F32),
            pltpu.VMEM((docs, width, width), F32),
            pltpu.VMEM((docs, width, width), F32),
        ],
        compiler_params=pltpu.CompilerParams(vmem_limit_bytes=60 * 2**20),
        cost_estimate=pl.CostEstimate(flops=int(1.2e10), bytes_accessed=int(3e7), transcendentals=0),
        name="attn_bwd",
    )(lengths, x, wt, taps, rtaps, qkv, gctx, lq, lk, sm, mix, k2, z, p, l1, l3)


def body_factory(dp, mp):
    def body(tokens, lengths, qkv_weight, out_weight, conv_taps, norm1_gain, norm1_bias, norm2_gain, norm2_bias, up_weight, down_weight, cotangent):
        docs, seq, dim = tokens.shape
        width = qkv_weight.shape[2]
        ff = up_weight.shape[1]
        me = lax.axis_index("mp")
        rows = seq // mp
        wt = jnp.transpose(qkv_weight, (0, 2, 1)).reshape(3 * width, dim)
        taps = jnp.pad(conv_taps, ((0, 0), (112, WIN - 112 - KSIZE)))
        rtaps = jnp.pad(conv_taps[:, ::-1], ((0, 0), (112, WIN - 112 - KSIZE)))
        qkv, ctx, lq, lk, sm, mix, k2, z, p, l1, l3 = attn_fwd(lengths, tokens, wt, taps, mp)
        ctx_rows = lax.all_to_all(ctx, "mp", 0, 0, tiled=True)
        w_all = jnp.concatenate([out_weight, up_weight.T, down_weight], axis=0)
        w_all = lax.all_gather(w_all, "mp", axis=0, tiled=False)
        ow, up, dn = w_all[:, :width], w_all[:, width : width + ff], w_all[:, width + ff :]
        first = me * rows
        x_rows = lax.dynamic_slice_in_dim(tokens, first, rows, 1)
        cot_rows = lax.dynamic_slice_in_dim(cotangent, first, rows, 1)
        pos = jnp.reshape(first, (1,)).astype(jnp.int32)
        out_rows, gmix, gctx, gow, gup, gdn, small = ffn(
            lengths, pos, x_rows, cot_rows, ctx_rows, ow, up, dn,
            norm1_gain[None], norm1_bias[None], norm2_gain[None], norm2_bias[None],
        )
        output = lax.all_gather(out_rows, "mp", axis=1, tiled=True)
        gctx_heads = lax.all_to_all(gctx, "mp", 0, 0, tiled=True)
        gw = jnp.concatenate([gow, gup, gdn], axis=1)
        gw = lax.psum_scatter(gw, "mp", scatter_dimension=0, tiled=False)
        gw = lax.psum(gw, "dp").astype(F32)
        gqkv, ipart, gtaps = attn_bwd(lengths, tokens, wt, taps, rtaps, qkv, gctx_heads, lq, lk, sm, mix, k2, z, p, l1, l3)
        ipart = lax.psum_scatter(ipart, "mp", scatter_dimension=1, tiled=True).astype(F32)
        input_grad = lax.all_gather((gmix + ipart).astype(BF), "mp", axis=1, tiled=True)
        gqkv = lax.psum(gqkv.astype(BF), "dp").astype(F32)
        gqkv = jnp.transpose(gqkv.reshape(3, width, dim), (0, 2, 1))
        small = lax.psum(small, ("dp", "mp"))
        gtaps = lax.psum(gtaps, "dp")
        gtaps = lax.slice_in_dim(gtaps, 367, 367 + KSIZE, axis=1)
        return (
            output, input_grad, gqkv, gw[:width], gtaps, small[0], small[1], small[2], small[3],
            gw[width : width + ff].T, gw[width + ff :],
        )
    return body


def solution(mesh):
    return jax.shard_map(
        body_factory(mesh.shape["dp"], mesh.shape["mp"]),
        mesh=mesh,
        in_specs=(
            P("dp", None, None), P("dp"), P(None, None, "mp"), P("mp", None), P("mp", None),
            P(), P(), P(), P(), P(None, "mp"), P("mp", None), P("dp", None, None),
        ),
        out_specs=(
            P("dp", None, None), P("dp", None, None), P(None, None, "mp"), P("mp", None), P("mp", None),
            P(), P(), P(), P(), P(None, "mp"), P("mp", None),
        ),
        check_vma=False,
    )
```

time: 957 us -> 805 us (0.84)
  matrix products: 160 us -> 0 us
  other arithmetic: 116 us -> 18.6 us
  Pallas kernels: 0 us -> 94.4 us
  local copies, waits for them, and re-layouts: 62.9 us -> 33 us
  blocking collectives: 37.6 us -> 59.8 us
  waiting for transfers between devices: 554 us -> 564 us
    psum x4 -> x1, waiting for transfers between devices: 451 us -> 76.7 us  [body(): gqkv = lax.psum(gqkv.astype(BF), 'dp').astype(F32)]
    reduce_scatter x2, waiting for transfers between devices: 0.04 us -> 228 us  [the longest x1 179 us: body(): gw = lax.psum_scatter(gw, 'mp', scatter_dimension=0, tiled=False)]
    all_gather x2 -> x3, waiting for transfers between devices: 38.9 us -> 240 us  [the longest x1 170 us: body(): w_all = lax.all_gather(w_all, 'mp', axis=0, tiled=False)]
    dot_general x103 -> x0, matrix products: 155 us -> none  [the longest x1 36.9 us: attend_forward(): jnp.einsum('wpb,wbi->pwi', first_kernel, mixing_matrix, preferred_element...]
    pallas_call x0 -> x3, Pallas kernels: none -> 94.4 us  [the longest x1 39.6 us: attn_bwd(): pl.pallas_call(functools.partial(attn_bwd_kernel, docs, heads, seq, parts...]
    unnamed x16 -> x6, waiting for transfers between devices: 63.3 us -> 0.6 us
    psum x0 -> x2, blocking collectives: none -> 59.8 us  [the longest x1 46.9 us: body(): small = lax.psum(small, ('dp', 'mp'))]
    reduce_sum x16 -> x0, other arithmetic: 52.4 us -> none  [the longest x2 15.9 us: depthwise(): padded[offset:offset + seq_len] * tap_weights[:, offset][None, :, None]]
  transfers between devices with their start and end apart: 12 -> 8, of which waited for: 8 -> 7; matrix products, arithmetic and copies ran while one was open for 19% -> 4% of each run, Pallas kernels for 0% -> 3%
where the time goes in v1:
time: 805 us; the launch traced here: 794 us
  waiting for transfers between devices  564 us (70%)
  Pallas kernels  94.4 us (12%)
  blocking collectives  59.8 us (7%)
  local copies, waits for them, and re-layouts  33 us (4%)
  other arithmetic  18.6 us (2%)
  between operations  14.7 us (2%)
  starting transfers between devices  8.78 us (1%)
    reduce_scatter x1, waiting for transfers between devices, body(): gw = lax.psum_scatter(gw, 'mp', scatter_dimension=0, tiled=False)  179 us
    all_gather x1, waiting for transfers between devices, body(): w_all = lax.all_gather(w_all, 'mp', axis=0, tiled=False)  170 us
    psum x1, waiting for transfers between devices, body(): gqkv = lax.psum(gqkv.astype(BF), 'dp').astype(F32)  76.7 us
    all_gather x1, waiting for transfers between devices, body(): lax.all_gather((gmix + ipart).astype(BF), 'mp', axis=1, tiled=True)  64.4 us
    reduce_scatter x1, waiting for transfers between devices, body(): lax.psum_scatter(ipart, 'mp', scatter_dimension=1, tiled=True).astype(F32)  48.4 us
    psum x1, blocking collectives, body(): small = lax.psum(small, ('dp', 'mp'))  46.9 us
    pallas_call x1, Pallas kernels, attn_bwd(): pl.pallas_call(functools.partial(attn_bwd_kernel, docs, heads, seq, parts...  39.6 us
    pallas_call x1, Pallas kernels, ffn(): pl.pallas_call(functools.partial(ffn_kernel, groups, docs, rows), out_sha...  30.8 us
  transfers between devices with their start and end apart: 8, of which 7 were waited for; matrix products, arithmetic and copies ran while one was open for 4% of the time, Pallas kernels for 3%

profile of v1, /device:TPU:4, one launch (start us, length us, event | category | flops | bytes accessed | tf_op | source)
XLA Modules:
  0.0 793.7 jit_solution(13627078492699553103)
XLA Ops:
  7.2 0.0 copy-start.4
  7.2 0.0 all-gather.9.cloned.1.call-start
  7.2 1.7 copy.23
  8.9 0.0 copy-done.4
  8.9 0.0 copy-start.11
  8.9 2.6 pad_maximum_fusion.1
  11.6 0.0 all-gather.9.cloned.1.call-update
  11.6 0.0 copy-done.11
  11.6 0.7 pad.7.taps_ref
  12.3 24.0 %attn_fwd.1 = (bf16[2,576,1024]{2,1,0:T(8,128)(2,1)}, bf16[4,2,192,256]{3,2,1,0:T(8,128)(2,1)}, bf16[2,192,192]{2,1,0:T(8,128)(2,1)}, bf16[2,192,192]{2,1,0:T(8,...) custom-call(s32[2]{0:T(128)} %len_ref.5, ...), custom_call_target="tpu_custom_call" | custom-call | flops 8000000000 | bytes 30000000 | tf_op jit(solution)/shard_map/attn_fwd/pallas_call | solution.py:179
  36.3 4.9 all-to-all-start
  41.1 0.6 broadcast_in_dim.12.g1_ref
  41.7 0.6 broadcast_in_dim.13.b1_ref
  42.3 0.6 broadcast_in_dim.14.g2_ref
  42.9 0.0 copy-done.15
  42.9 0.6 broadcast_in_dim.15.b2_ref
  43.5 2.7 constant_dynamic-slice_fusion
  46.1 169.7 %all-gather.9.cloned.1.call-done = bf16[6912,768]{1,0:T(8,128)(2,1)} async-done(((bf16[1728,768]{1,0:T(8,128)(2,1)}), bf16[6912,768]{1,0:T(8,128)(2,1)}) %all-gather.9.cloned.1.call-update) | async-done | bytes 10616848 | tf_op jit(solution)/shard_map/all_gather | solution.py:462
  215.8 2.4 slice.44.ow_ref
  218.2 7.9 %fusion = (bf16[4,768,768]{2,1,0:T(8,128)(2,1)}, bf16[4,768,768]{2,1,0:T(8,128)(2,1)}) fusion(bf16[4,1728,768]{2,1,0:T(8,128)(2,1)} %bitcast.13), kind=kLoop, calls=%fused_computation.10 | loop fusion | bytes 18874368 | tf_op jit(solution)/shard_map/slice | solution.py:463
  226.1 0.0 all-to-all-done.ctx_ref
  226.1 0.9 copy-done.7
  227.0 30.8 %ffn.1 = (bf16[2,256,768]{2,1,0:T(8,128)(2,1)}, f32[2,256,768]{2,1,0:T(8,128)}, bf16[4,2,192,256]{3,2,1,0:T(8,128)(2,1)}, bf16[4,192,768]{2,1,0:T(8,128)(2,1)}, ...) custom-call(s32[2]{0:T(128)} %len_ref.5, s32[1]{0:T(128)} %bitcast.pos_ref, ...), custom_call_target="tpu_custom_call" | custom-call | flops 17999998976 | bytes 40000000 | tf_op jit(solution)/shard_map/ffn/pallas_call | solution.py:300
  257.8 3.5 all-to-all-start.1
  261.3 0.2 reduce-scatter.3.cloned.1.call-start
  261.5 0.1 rev.3
  261.6 0.7 pad.8.rtaps_ref
  262.3 19.6 %all-to-all-done.1.gctx_ref = bf16[4,2,192,256]{3,2,1,0:T(8,128)(2,1)S(1)} async-done(((bf16[4,2,192,256]{3,2,1,0:T(8,128)(2,1)}), bf16[4,2,192,256]{3,2,1,0:T(8,128)(2,1)S(1)}, u32[]{:S(2)}, u32[]{:S(2)}) %all-to-all-start.1) | async-done | bytes 786464 | tf_op jit(solution)/shard_map/all_to_all | solution.py:473
  281.9 0.9 copy-done.8
  282.8 39.6 %attn_bwd.1 = (f32[576,768]{1,0:T(8,128)}, bf16[2,1024,768]{2,1,0:T(8,128)(2,1)}, f32[3,512]{1,0:T(4,128)}) custom-call(s32[2]{0:T(128)} %len_ref.5, bf16[2,1024,768]{2,1,0:T(8,128)(2,1)} %x_ref.3, bf16[576,768]{1,0:T(8,128)(2,1)} %bitcast.18, f32[3,512]{1,0:T(4,128)} %pad.7.taps_ref, f32[3,512]{1,0:T(4,128)} %pad.8.rtaps_ref, ...), custom_call_target="tpu_custom_call" | custom-call | flops 12000000000 | bytes 30000000 | tf_op jit(solution)/shard_map/attn_bwd/pallas_call | solution.py:432
  322.4 0.0 reduce-scatter.3.cloned.1.call-update
  322.4 0.0 reduce-scatter.5.cloned.1.call-start
  322.4 1.2 copy-done.5
  323.6 9.2 %pad_maximum_fusion = bf16[4,1728,768]{2,1,0:T(8,128)(2,1)} fusion(bf16[4,768,768]{2,1,0:T(8,128)(2,1)} %get-tuple-element.50, bf16[4,768,768]{2,1,0:T(8,128)(2,1)} %get-tuple-element.49, bf16[4,192,768]{2,1,0:T(8,128)(2,1)S(1)} %copy-done.5), kind=kLoop, calls=%fused_computation | loop fusion | flops 31850496 | bytes 21233664 | tf_op jit(solution)/shard_map/concatenate | solution.py:474
  332.8 0.0 reduce-scatter.5.cloned.1.call-update
  332.9 0.0 copy-start.2
  332.9 0.0 all-gather.5.cloned.1.call-start
  332.9 0.5 all-gather.5.cloned.1.call-update
  333.4 0.0 all-gather.7.cloned.1.call-start
  333.5 48.4 %reduce-scatter.3.cloned.1.call-done = bf16[2,256,768]{2,1,0:T(8,128)(2,1)} async-done(((bf16[2,1024,768]{2,1,0:T(8,128)(2,1)}), bf16[2,256,768]{2,1,0:T(8,128)(2,1)}) %reduce-scatter.3.cloned.1.call-update) | async-done | bytes 786448 | tf_op jit(solution)/shard_map/reduce_scatter | solution.py:478
  381.9 2.2 add_convert_fusion
  384.0 0.0 all-gather.7.cloned.1.call-update
  384.1 0.0 all-reduce.5.cloned.1.call-start
  384.1 1.0 convert_element_type.18
  385.1 179.3 %reduce-scatter.5.cloned.1.call-done = bf16[1,1728,768]{2,1,0:T(8,128)(2,1)} async-done(((bf16[4,1728,768]{2,1,0:T(8,128)(2,1)}), bf16[1,1728,768]{2,1,0:T(8,128)(2,1)}) %reduce-scatter.5.cloned.1.call-update) | async-done | bytes 2654224 | tf_op jit(solution)/shard_map/reduce_scatter | solution.py:475
  564.4 0.0 all-reduce.5.cloned.1.call-update
  564.4 0.0 copy-done.9
  564.4 46.9 %psum.31 = f32[8,768]{1,0:T(8,128)S(1)} all-reduce(f32[8,768]{1,0:T(8,128)S(1)} %copy-done.9), channel_id=1, replica_groups=mesh['dp'=8,'mp'=4] {'dp','mp'}, use_global_device_ids=true, to_apply=%region_5.6 | all-reduce | flops 6144 | bytes 49152 | tf_op jit(solution)/shard_map/psum | solution.py:482
  611.4 0.6 slice_reduce_fusion
  612.0 12.8 %psum.30 = f32[3,512]{1,0:T(4,128)S(1)} all-reduce(f32[3,512]{1,0:T(4,128)S(1)} %copy-done.10), channel_id=1, replica_groups=mesh['dp'=8,'mp'=4] {'dp'}, use_global_device_ids=true, to_apply=%region_4.5 | all-reduce | flops 1536 | bytes 12288 | tf_op jit(solution)/shard_map/psum | solution.py:483
  624.9 0.6 slice.48
  625.5 5.8 all-gather.5.cloned.1.call-done
  631.3 64.4 %all-gather.7.cloned.1.call-done = bf16[2,1024,768]{2,1,0:T(8,128)(2,1)} async-done(((bf16[2,256,768]{2,1,0:T(8,128)(2,1)}), bf16[2,1024,768]{2,1,0:T(8,128)(2,1)}) %all-gather.7.cloned.1.call-update) | async-done | bytes 3145744 | tf_op jit(solution)/shard_map/all_gather | solution.py:479
  695.7 76.7 %all-reduce.5.cloned.1.call-done = (bf16[3,768,192]{1,2,0:T(8,128)(2,1)}, bf16[1728,768]{1,0:T(8,128)(2,1)}) async-done(((bf16[3,768,192]{1,2,0:T(8,128)(2,1)}, bf16[1728,768]{1,0:T(8,128)(2,1)}), (bf16[3,768,192]{1,2,0:T(8,128)(2,1)}, bf16[1728,768]{1,0:T(8,128)(2,1)})) %all-reduce.5.cloned.1.call-update) | async-done | bytes 3538960 | tf_op jit(solution)/shard_map/psum | solution.py:480
  772.4 2.3 convert_element_type.19
  774.7 0.2 copy-done
  775.0 1.6 slice.54
  776.5 0.9 slice.47
  777.4 0.2 slice_bitcast_fusion
  777.6 2.0 copy.24
  779.5 1.4 transpose.18
  780.9 3.9 copy.29
  784.8 0.0 copy-done.1
  784.8 1.7 copy.30
  (20 shorter events, 0.0 us)
Async XLA Ops:
  7.2 1.7 copy-start.4
  7.2 208.6 %all-gather.9.cloned.1.call-start = ((), (), s32[]{:S(2)}) async-start(), calls=%async_computation.8 | async-start | bytes 13271040 | tf_op jit(solution)/shard_map/all_gather | solution.py:462
  8.9 2.7 copy-start.11
  12.3 28.9 %copy-start.12 = (f32[768]{0:T(1024)S(1)}, f32[768]{0:T(1024)}, u32[]{:S(2)}) copy-start(f32[768]{0:T(1024)} %param.17) | copy-start | bytes 9220
  12.3 29.5 %copy-start.13 = (f32[768]{0:T(1024)S(1)}, f32[768]{0:T(1024)}, u32[]{:S(2)}) copy-start(f32[768]{0:T(1024)} %param.18) | copy-start | bytes 9220
  12.3 30.0 %copy-start.14 = (f32[768]{0:T(1024)S(1)}, f32[768]{0:T(1024)}, u32[]{:S(2)}) copy-start(f32[768]{0:T(1024)} %param.19) | copy-start | bytes 9220
  12.3 30.6 %copy-start.15 = (f32[768]{0:T(1024)S(1)}, f32[768]{0:T(1024)}, u32[]{:S(2)}) copy-start(f32[768]{0:T(1024)} %param.20) | copy-start | bytes 9220
  36.3 189.9 %all-to-all-start = ((bf16[4,2,192,256]{3,2,1,0:T(8,128)(2,1)}), bf16[4,2,192,256]{3,2,1,0:T(8,128)(2,1)S(1)}, u32[]{:S(2)}, u32[]{:S(2)}) async-start(bf16[4,2,192,256]{3,2,1,0:T(8,128)(2,1)} %get-tuple-element.32), calls=%async_computation | async-start | bytes 1572864 | tf_op jit(solution)/shard_map/all_to_all | solution.py:460
  226.1 0.9 copy-start.7
  257.8 24.1 %all-to-all-start.1 = ((bf16[4,2,192,256]{3,2,1,0:T(8,128)(2,1)}), bf16[4,2,192,256]{3,2,1,0:T(8,128)(2,1)S(1)}, u32[]{:S(2)}, u32[]{:S(2)}) async-start(bf16[4,2,192,256]{3,2,1,0:T(8,128)(2,1)} %get-tuple-element.36), calls=%async_computation.1 | async-start | bytes 1572864 | tf_op jit(solution)/shard_map/all_to_all | solution.py:473
  261.3 120.6 %reduce-scatter.3.cloned.1.call-start = ((), (), s32[]{:S(2)}) async-start(), calls=%async_computation.5 | async-start | bytes 3932160 | tf_op jit(solution)/shard_map/reduce_scatter | solution.py:478
  281.9 0.9 copy-start.8
  322.4 1.3 copy-start.5
  322.4 242.0 %reduce-scatter.5.cloned.1.call-start = ((), (), s32[]{:S(2)}) async-start(), calls=%async_computation.7 | async-start | bytes 13271040 | tf_op jit(solution)/shard_map/reduce_scatter | solution.py:475
  332.8 49.0 %copy-start.3 = (f32[2,256,768]{2,1,0:T(8,128)S(1)}, f32[2,256,768]{2,1,0:T(8,128)}, u32[]{:S(2)}) copy-start(f32[2,256,768]{2,1,0:T(8,128)} %get-tuple-element.34) | copy-start | bytes 4718596
  332.9 51.3 %copy-start.2 = (f32[576,768]{1,0:T(8,128)S(1)}, f32[576,768]{1,0:T(8,128)}, u32[]{:S(2)}) copy-start(f32[576,768]{1,0:T(8,128)} %get-tuple-element.47) | copy-start | bytes 5308420
  332.9 298.4 %all-gather.5.cloned.1.call-start = ((), (), s32[]{:S(2)}) async-start(), calls=%async_computation.4 | async-start | bytes 3932160 | tf_op jit(solution)/shard_map/all_gather | solution.py:472
  333.4 362.3 %all-gather.7.cloned.1.call-start = ((), (), s32[]{:S(2)}) async-start(), calls=%async_computation.6 | async-start | bytes 3932160 | tf_op jit(solution)/shard_map/all_gather | solution.py:479
  384.1 180.4 %copy-start.9 = (f32[8,768]{1,0:T(8,128)S(1)}, f32[8,768]{1,0:T(8,128)}, u32[]{:S(2)}) copy-start(f32[8,768]{1,0:T(8,128)} %get-tuple-element.52) | copy-start | bytes 73732
  384.1 228.0 %copy-start.10 = (f32[3,512]{1,0:T(4,128)S(1)}, f32[3,512]{1,0:T(4,128)}, u32[]{:S(2)}) copy-start(f32[3,512]{1,0:T(4,128)} %get-tuple-element.51) | copy-start | bytes 18436
  384.1 388.3 %all-reduce.5.cloned.1.call-start = ((), (), s32[]{:S(2)}) async-start(), calls=%async_computation.9 | async-start | bytes 7077888 | tf_op jit(solution)/shard_map/psum | solution.py:480
  772.4 2.5 copy-start
  777.6 2.0 copy-start.6
  780.9 3.9 copy-start.1
Sparse Core Ops, SparseCore 0:
  11.7 204.0 all-gather.8
  322.5 59.2 reduce-scatter.2
  384.2 180.1 reduce-scatter.4
  565.9 65.3 all-gather.4
  633.4 62.2 all-gather.6
  699.9 72.4 all-reduce.4

commit v2 on v1

--- a/solution.py
+++ b/solution.py
@@ -83,8 +83,136 @@
     return jnp.concatenate(outs, axis=0)
 
 
-def attn_fwd_kernel(docs, heads, seq, dest, len_ref, x_ref, wt_ref, taps_ref, qkv_ref, ctx_ref, lq_ref, lk_ref, sum_ref, mix_ref, k2_ref, z_ref, p_ref, l1_ref, l3_ref):
+MESH = pl.DeviceIdType.MESH
+
+
+def flip(i, bit):
+    return i + bit * (1 - 2 * ((i // bit) % 2))
+
+
+def partner(i, m):
+    for bit in (1, 2, 4):
+        if m & bit:
+            i = flip(i, bit)
+    return i
+
+
+def greet(peers):
+    bar = pltpu.get_barrier_semaphore()
+    for p in peers:
+        pl.semaphore_signal(bar, inc=1, device_id=p, device_id_type=MESH)
+    pl.semaphore_wait(bar, len(peers))
+
+
+def rcopy(src, dst, ss, rs, dev):
+    return pltpu.make_async_remote_copy(src_ref=src, dst_ref=dst, send_sem=ss, recv_sem=rs, device_id=dev, device_id_type=MESH)
+
+
+SLOTS = 8
+OW_ROWS, UP_ROWS, DN_ROWS = 24, 96, 96
+SLICE = OW_ROWS + UP_ROWS + DN_ROWS
+CUT = OW_ROWS + UP_ROWS
+
+
+class Gather:
+    def __init__(self, mp, srcs, wall, zsem, xsem, csem, lsem):
+        self.wall, self.zsem, self.xsem, self.csem, self.lsem = wall, zsem, xsem, csem, lsem
+        self.srcs = srcs
+        self.mp = mp
+        self.z = lax.axis_index("mp")
+        self.d = lax.axis_index("dp")
+        self.r = lax.rem(self.d, SLOTS)
+
+    def rows(self, i):
+        size = (OW_ROWS, UP_ROWS, DN_ROWS)[i]
+        lo = (0, OW_ROWS, CUT)[i]
+        return self.srcs[i].at[pl.ds(pl.multiple_of(self.r * size, 8), size)], lo, size
+
+    def z_copies(self, m):
+        out = []
+        for i in range(3):
+            src, lo, size = self.rows(i)
+            out.append(rcopy(src, self.wall.at[self.z, self.r, pl.ds(lo, size)], self.zsem.at[0, m - 1, i], self.zsem.at[1, m - 1, i], {"mp": partner(self.z, m)}))
+        return out
+
+    def y(self, m):
+        s = self.wall.at[partner(self.z, m), self.r]
+        return rcopy(s, s, self.xsem.at[0, m - 1, 0], self.xsem.at[1, m - 1, 0], {"dp": flip(self.d, 4)})
+
+    def x(self, m):
+        s = self.wall.at[partner(self.z, m), self.r]
+        return rcopy(s, s, self.xsem.at[0, m - 1, 1], self.xsem.at[1, m - 1, 1], {"dp": flip(self.d, 2)})
+
+    def yx(self, m):
+        s = self.wall.at[partner(self.z, m), flip(self.r, 4), pl.ds(0, CUT)]
+        return rcopy(s, s, self.xsem.at[0, m - 1, 2], self.xsem.at[1, m - 1, 2], {"dp": flip(self.d, 2)})
+
+    def xy(self, m):
+        s = self.wall.at[partner(self.z, m), flip(self.r, 2), pl.ds(CUT, DN_ROWS)]
+        return rcopy(s, s, self.xsem.at[0, m - 1, 3], self.xsem.at[1, m - 1, 3], {"dp": flip(self.d, 4)})
+
+    def core(self, m, q):
+        r = (self.r, flip(self.r, 4), flip(self.r, 2), partner(self.r, 6))[q]
+        s = self.wall.at[partner(self.z, m), r]
+        return rcopy(s, s, self.csem.at[0, m - 1, q], self.csem.at[1, m - 1, q], {"dp": flip(self.d, 1)})
+
+    def start(self):
+        for m in range(1, self.mp):
+            for c in self.z_copies(m):
+                c.start()
+        for i in range(3):
+            size = (OW_ROWS, UP_ROWS, DN_ROWS)[i]
+            lo = (0, OW_ROWS, CUT)[i]
+            for r in range(SLOTS):
+                pltpu.make_async_copy(self.srcs[i].at[pl.ds(r * size, size)], self.wall.at[self.z, r, pl.ds(lo, size)], self.lsem.at[i, r]).start()
+
+    def step1(self, m):
+        for c in self.z_copies(m):
+            c.wait_recv()
+        self.y(m).start()
+        self.x(m).start()
+        self.core(m, 0).start()
+
+    def step2(self, m):
+        self.y(m).wait_recv()
+        self.yx(m).start()
+        self.core(m, 1).start()
+        self.x(m).wait_recv()
+        self.xy(m).start()
+        self.core(m, 2).start()
+
+    def step3(self, m):
+        self.yx(m).wait_recv()
+        self.xy(m).wait_recv()
+        self.core(m, 3).start()
+
+    def finish(self):
+        for i in range(3):
+            size = (OW_ROWS, UP_ROWS, DN_ROWS)[i]
+            lo = (0, OW_ROWS, CUT)[i]
+            for r in range(SLOTS):
+                pltpu.make_async_copy(self.srcs[i].at[pl.ds(r * size, size)], self.wall.at[self.z, r, pl.ds(lo, size)], self.lsem.at[i, r]).wait()
+        for m in range(1, self.mp):
+            for c in self.z_copies(m):
+                c.wait_send()
+            for c in (self.y(m), self.x(m), self.yx(m), self.xy(m)):
+                c.wait_send()
+            for q in range(4):
+                self.core(m, q).wait()
+
+
+def attn_fwd_kernel(docs, heads, seq, dest, len_ref, x_ref, wt_ref, taps_ref, ow_ref, up_ref, dn_ref, qkv_ref, ctx_ref, lq_ref, lk_ref, sum_ref, mix_ref, k2_ref, z_ref, p_ref, l1_ref, l3_ref, wall_ref,
+                    ctx_s, zsem, xsem, csem, lsem, asem):
     width = heads * HD
+    me = lax.axis_index("mp")
+    dd = lax.axis_index("dp")
+    greet([{"mp": partner(me, m)} for m in range(1, dest)] + [{"dp": flip(dd, b)} for b in (1, 2, 4)])
+    gather = Gather(dest, (ow_ref, up_ref, dn_ref), wall_ref, zsem, xsem, csem, lsem)
+    gather.start()
+
+    def a_copy(m, d):
+        return rcopy(ctx_s.at[partner(me, m), d], ctx_ref.at[me, d], asem.at[0, m - 1, d], asem.at[1, m - 1, d], {"mp": partner(me, m)})
+
     mask = block_mask(width)
     eye = jnp.where(
         lax.broadcasted_iota(jnp.int32, (width, width), 0) == lax.broadcasted_iota(jnp.int32, (width, width), 1), 1.0, 0.0
@@ -93,8 +221,11 @@
         for c in range(seq // BLK):
             xc = x_ref[d, c * BLK : (c + 1) * BLK, :]
             qkv_ref[d, :, c * BLK : (c + 1) * BLK] = nt(wt_ref[...], xc).astype(BF)
+    gather.step1(1)
     k2s = []
     for d in range(docs):
+        if d == 1:
+            gather.step1(2)
         length = len_ref[d]
         memb = jnp.where(members(length, 0, seq), 1.0, 0.0).astype(F32)
         counts = jnp.maximum(jnp.sum(memb, axis=1, keepdims=True), 1.0)
@@ -136,6 +267,10 @@
             p_ref[d, i, 1] = bs[d]
             p_ref[d, i, 2] = cs[d]
             z_ref[d, i + 1] = zs[d]
+        if i == 2:
+            gather.step1(3)
+        if i == 4:
+            gather.step2(1)
     for d in range(docs):
         length = len_ref[d]
         q = qkv_ref[d, 0:width, :]
@@ -155,10 +290,23 @@
         ctx = jnp.where(live, ctx, 0.0).astype(BF)
         part = seq // dest
         for i in range(dest):
-            ctx_ref[i, d] = ctx[:, i * part : (i + 1) * part]
-
-
-def attn_fwd(lengths, x, wt, taps, dest):
+            ctx_s[i, d] = ctx[:, i * part : (i + 1) * part]
+        for m in range(1, dest):
+            a_copy(m, d).start()
+        ctx_ref[me, d] = ctx_s[me, d]
+        if d == 0:
+            gather.step2(2)
+    gather.step3(1)
+    gather.step2(3)
+    gather.step3(2)
+    gather.step3(3)
+    gather.finish()
+    for d in range(docs):
+        for m in range(1, dest):
+            a_copy(m, d).wait()
+
+
+def attn_fwd(lengths, x, wt, taps, ow, up, dn, dest):
     docs, seq, dim = x.shape
     width = wt.shape[0] // 3
     heads = width // HD
@@ -175,16 +323,27 @@
         jax.ShapeDtypeStruct((docs, NS_ITERS, 3, width, width), F32),
         jax.ShapeDtypeStruct((docs, heads, seq), F32),
         jax.ShapeDtypeStruct((docs, width, 128), F32),
+        jax.ShapeDtypeStruct((dest, SLOTS, SLICE, dim), BF),
     ]
+    any_ = pl.BlockSpec(memory_space=pl.ANY)
+    dma = pltpu.SemaphoreType.DMA
     return pl.pallas_call(
         functools.partial(attn_fwd_kernel, docs, heads, seq, dest),
         out_shape=out,
-        in_specs=[pl.BlockSpec(memory_space=pltpu.SMEM), vm, vm, vm],
-        out_specs=[vm] * len(out),
-        compiler_params=pltpu.CompilerParams(vmem_limit_bytes=60 * 2**20),
+        in_specs=[pl.BlockSpec(memory_space=pltpu.SMEM), vm, vm, vm, any_, any_, any_],
+        out_specs=[vm] * (len(out) - 1) + [any_],
+        scratch_shapes=[
+            pltpu.VMEM((dest, docs, width, seq // dest), BF),
+            dma((2, dest - 1, 3)),
+            dma((2, dest - 1, 4)),
+            dma((2, dest - 1, 4)),
+            dma((3, SLOTS)),
+            dma((2, dest - 1, docs)),
+        ],
+        compiler_params=pltpu.CompilerParams(vmem_limit_bytes=60 * 2**20, collective_id=0, has_side_effects=True),
         cost_estimate=pl.CostEstimate(flops=int(8e9), bytes_accessed=int(3e7), transcendentals=0),
         name="attn_fwd",
-    )(lengths, x, wt, taps)
+    )(lengths, x, wt, taps, ow, up, dn)
 
 
 def ln_stats(v):
@@ -205,14 +364,21 @@
 INV_ROOT_2PI = 0.3989422804014327
 
 
-def ffn_kernel(groups, docs, rows, len_ref, pos_ref, x_ref, cot_ref, ctx_ref, ow_ref, up_ref, dn_ref, g1_ref, b1_ref, g2_ref, b2_ref,
-               out_ref, gmix_ref, gctx_ref, gow_ref, gup_ref, gdn_ref, small_ref, nb_s, fac_s, act_s, br_s, x1_s, gn_s):
+def ffn_kernel(groups, docs, rows, len_ref, pos_ref, x_ref, cot_ref, ctx_ref, wall_ref, g1_ref, b1_ref, g2_ref, b2_ref,
+               out_ref, gmix_ref, gctx_ref, gw_ref, small_ref, nb_s, fac_s, act_s, br_s, x1_s, gn_s):
     n = docs * rows
     dim = x_ref.shape[-1]
-    attn = None
-    for g in range(groups):
-        for d in range(docs):
-            pass
+    ff = SLOTS * UP_ROWS
+
+    def ow(g):
+        return wall_ref[g, :, 0:OW_ROWS, :].reshape(SLOTS * OW_ROWS, dim)
+
+    def up(g):
+        return wall_ref[g, :, OW_ROWS:CUT, :].reshape(SLOTS * UP_ROWS, dim)
+
+    def dn(g):
+        return wall_ref[g, :, CUT:SLICE, :].reshape(SLOTS * DN_ROWS, dim)
+
     first = pos_ref[0]
     live = jnp.concatenate(
         [
@@ -225,7 +391,7 @@
     for d in range(docs):
         acc = None
         for g in range(groups):
-            t = tn(ctx_ref[g, d], ow_ref[g]).astype(BF).astype(F32)
+            t = tn(ctx_ref[g, d], ow(g)).astype(BF).astype(F32)
             acc = t if acc is None else acc + t
         parts.append(acc)
     mixed = x_ref[...].reshape(n, dim).astype(F32) + jnp.concatenate(parts, axis=0)
@@ -236,12 +402,12 @@
     br_s[...] = normed
 
     def fwd_group(g, _):
-        h = nt(nb_s[...], up_ref[g])
+        h = nn(nb_s[...], up(g))
         phi_big = 0.5 * (1.0 + lax.erf(h * ROOT_HALF))
         act = (h * phi_big).astype(BF)
         act_s[g] = act
         fac_s[g] = phi_big + h * (jnp.exp(-0.5 * h * h) * INV_ROOT_2PI)
-        br_s[...] += nn(act, dn_ref[g]).astype(BF).astype(F32)
+        br_s[...] += nn(act, dn(g)).astype(BF).astype(F32)
         return 0
 
     lax.fori_loop(0, groups, fwd_group, 0)
@@ -256,10 +422,10 @@
 
     def bwd_group(g, _):
         act = act_s[g]
-        gdn_ref[g] = tn(act, gbr).astype(BF)
-        g_pre = (nt(gbr, dn_ref[g]) * fac_s[g]).astype(BF)
-        gup_ref[g] = tn(g_pre, nb_s[...]).astype(BF)
-        gn_s[...] += nn(g_pre, up_ref[g])
+        gw_ref[g, :, CUT:SLICE, :] = tn(act, gbr).astype(BF).reshape(SLOTS, DN_ROWS, dim)
+        g_pre = (nt(gbr, dn(g)) * fac_s[g]).astype(BF)
+        gw_ref[g, :, OW_ROWS:CUT, :] = tn(nb_s[...], g_pre).astype(BF).reshape(SLOTS, UP_ROWS, ff)
+        gn_s[...] += nt(g_pre, up(g))
         return 0
 
     lax.fori_loop(0, groups, bwd_group, 0)
@@ -277,14 +443,14 @@
             ga = g_att[d * rows : (d + 1) * rows]
             t = nn(ctx_ref[g, d], ga)
             acc = t if acc is None else acc + t
-            gctx_ref[g, d] = nt(ow_ref[g], ga).astype(BF)
-        gow_ref[g] = acc.astype(BF)
-
-
-def ffn(lengths, pos, x, cot, ctx, ow, up, dn, g1, b1, g2, b2):
+            gctx_ref[g, d] = nt(ow(g), ga).astype(BF)
+        gw_ref[g, :, 0:OW_ROWS, :] = acc.astype(BF).reshape(SLOTS, OW_ROWS, dim)
+
+
+def ffn(lengths, pos, x, cot, ctx, wall, g1, b1, g2, b2):
     docs, rows, dim = x.shape
     groups, _, width, _ = ctx.shape
-    ff = up.shape[1]
+    ff = SLOTS * UP_ROWS
     n = docs * rows
     vm = pl.BlockSpec(memory_space=pltpu.VMEM)
     sm = pl.BlockSpec(memory_space=pltpu.SMEM)
@@ -292,15 +458,13 @@
         jax.ShapeDtypeStruct((docs, rows, dim), BF),
         jax.ShapeDtypeStruct((docs, rows, dim), F32),
         jax.ShapeDtypeStruct((groups, docs, width, rows), BF),
-        jax.ShapeDtypeStruct((groups, width, dim), BF),
-        jax.ShapeDtypeStruct((groups, ff, dim), BF),
-        jax.ShapeDtypeStruct((groups, ff, dim), BF),
+        jax.ShapeDtypeStruct(wall.shape, BF),
         jax.ShapeDtypeStruct((8, dim), F32),
     ]
     return pl.pallas_call(
         functools.partial(ffn_kernel, groups, docs, rows),
         out_shape=out,
-        in_specs=[sm, sm] + [vm] * 10,
+        in_specs=[sm, sm] + [vm] * 8,
         out_specs=[vm] * len(out),
         scratch_shapes=[
             pltpu.VMEM((n, dim), BF),
@@ -313,7 +477,7 @@
         compiler_params=pltpu.CompilerParams(vmem_limit_bytes=60 * 2**20),
         cost_estimate=pl.CostEstimate(flops=int(1.8e10), bytes_accessed=int(4e7), transcendentals=0),
         name="ffn",
-    )(lengths, pos, x, cot, ctx, ow, up, dn, g1, b1, g2, b2)
+    )(lengths, pos, x, cot, ctx, wall, g1, b1, g2, b2)
 
 
 def attn_bwd_kernel(docs, heads, seq, parts, len_ref, x_ref, wt_ref, taps_ref, rtaps_ref, qkv_ref, gctx_ref, lq_ref, lk_ref, sum_ref, mix_ref, k2_ref,
@@ -456,22 +620,17 @@
         wt = jnp.transpose(qkv_weight, (0, 2, 1)).reshape(3 * width, dim)
         taps = jnp.pad(conv_taps, ((0, 0), (112, WIN - 112 - KSIZE)))
         rtaps = jnp.pad(conv_taps[:, ::-1], ((0, 0), (112, WIN - 112 - KSIZE)))
-        qkv, ctx, lq, lk, sm, mix, k2, z, p, l1, l3 = attn_fwd(lengths, tokens, wt, taps, mp)
-        ctx_rows = lax.all_to_all(ctx, "mp", 0, 0, tiled=True)
-        w_all = jnp.concatenate([out_weight, up_weight.T, down_weight], axis=0)
-        w_all = lax.all_gather(w_all, "mp", axis=0, tiled=False)
-        ow, up, dn = w_all[:, :width], w_all[:, width : width + ff], w_all[:, width + ff :]
+        qkv, ctx_rows, lq, lk, sm, mix, k2, z, p, l1, l3, wall = attn_fwd(lengths, tokens, wt, taps, out_weight, up_weight, down_weight, mp)
         first = me * rows
         x_rows = lax.dynamic_slice_in_dim(tokens, first, rows, 1)
         cot_rows = lax.dynamic_slice_in_dim(cotangent, first, rows, 1)
         pos = jnp.reshape(first, (1,)).astype(jnp.int32)
-        out_rows, gmix, gctx, gow, gup, gdn, small = ffn(
-            lengths, pos, x_rows, cot_rows, ctx_rows, ow, up, dn,
+        out_rows, gmix, gctx, gw, small = ffn(
+            lengths, pos, x_rows, cot_rows, ctx_rows, wall,
             norm1_gain[None], norm1_bias[None], norm2_gain[None], norm2_bias[None],
         )
         output = lax.all_gather(out_rows, "mp", axis=1, tiled=True)
         gctx_heads = lax.all_to_all(gctx, "mp", 0, 0, tiled=True)
-        gw = jnp.concatenate([gow, gup, gdn], axis=1)
         gw = lax.psum_scatter(gw, "mp", scatter_dimension=0, tiled=False)
         gw = lax.psum(gw, "dp").astype(F32)
         gqkv, ipart, gtaps = attn_bwd(lengths, tokens, wt, taps, rtaps, qkv, gctx_heads, lq, lk, sm, mix, k2, z, p, l1, l3)
@@ -483,8 +642,8 @@
         gtaps = lax.psum(gtaps, "dp")
         gtaps = lax.slice_in_dim(gtaps, 367, 367 + KSIZE, axis=1)
         return (
-            output, input_grad, gqkv, gw[:width], gtaps, small[0], small[1], small[2], small[3],
-            gw[width : width + ff].T, gw[width + ff :],
+            output, input_grad, gqkv, gw[:, :OW_ROWS].reshape(width, dim), gtaps, small[0], small[1], small[2], small[3],
+            gw[:, OW_ROWS:CUT].reshape(dim, ff), gw[:, CUT:].reshape(ff, dim),
         )
     return body
 

time: 805 us -> 686 us (0.85)
  waiting for transfers between devices: 564 us -> 407 us
  Pallas kernels: 94.4 us -> 165 us
  other arithmetic: 18.6 us -> 4.52 us
  local copies, waits for them, and re-layouts: 33 us -> 23 us
    all_gather x1 -> x0, waiting for transfers between devices: 170 us -> none  [body(): w_all = lax.all_gather(w_all, 'mp', axis=0, tiled=False)]
    pallas_call x1, Pallas kernels: 24 us -> 93.6 us  [attn_fwd(): pl.pallas_call(functools.partial(attn_fwd_kernel, docs, heads, seq, dest)...]
    concatenate x2 -> x0, other arithmetic: 11.8 us -> none  [the longest x1 9.19 us: body(): gw = jnp.concatenate([gow, gup, gdn], axis=1)]
    reduce_scatter x1, waiting for transfers between devices: 48.4 us -> 57.9 us  [body(): lax.psum_scatter(ipart, 'mp', scatter_dimension=1, tiled=True).astype(F32)]
  transfers between devices with their start and end apart: 8 -> 6, of which waited for: 7 -> 6; matrix products, arithmetic and copies ran while one was open for 4% -> 1% of each run, Pallas kernels for 3% -> 0%
where the time goes in v2:
time: 686 us; the launch traced here: 676 us
  waiting for transfers between devices  407 us (59%)
  Pallas kernels  165 us (24%)
  blocking collectives  57.8 us (8%)
  local copies, waits for them, and re-layouts  23 us (3%)
  between operations  14.3 us (2%)
    reduce_scatter x1, waiting for transfers between devices, body(): gw = lax.psum_scatter(gw, 'mp', scatter_dimension=0, tiled=False)  179 us
    pallas_call x1, Pallas kernels, attn_fwd(): pl.pallas_call(functools.partial(attn_fwd_kernel, docs, heads, seq, dest)...  93.6 us
    psum x1, waiting for transfers between devices, body(): gqkv = lax.psum(gqkv.astype(BF), 'dp').astype(F32)  76.7 us
    all_gather x1, waiting for transfers between devices, body(): lax.all_gather((gmix + ipart).astype(BF), 'mp', axis=1, tiled=True)  64.3 us
    reduce_scatter x1, waiting for transfers between devices, body(): lax.psum_scatter(ipart, 'mp', scatter_dimension=1, tiled=True).astype(F32)  57.9 us
    psum x1, blocking collectives, body(): small = lax.psum(small, ('dp', 'mp'))  44.8 us
    pallas_call x1, Pallas kernels, attn_bwd(): pl.pallas_call(functools.partial(attn_bwd_kernel, docs, heads, seq, parts...  39.6 us
    pallas_call x1, Pallas kernels, ffn(): pl.pallas_call(functools.partial(ffn_kernel, groups, docs, rows), out_sha...  31.7 us
  transfers between devices with their start and end apart: 6, of which 6 were waited for; matrix products, arithmetic and copies ran while one was open for 1% of the time, Pallas kernels for 0%

profile of v2, /device:TPU:4, one launch (start us, length us, event | category | flops | bytes accessed | tf_op | source)
XLA Modules:
  0.0 675.7 jit_solution(7555048059917653361)
XLA Ops:
  7.2 1.3 broadcast_in_dim.12.g1_ref
  8.4 1.3 broadcast_in_dim.13.b1_ref
  9.7 1.3 broadcast_in_dim.14.g2_ref
  11.0 1.3 broadcast_in_dim.15.b2_ref
  12.2 1.3 pad.7.taps_ref
  13.6 2.6 constant_dynamic-slice_fusion
  16.2 93.6 %attn_fwd.1 = (bf16[2,576,1024]{2,1,0:T(8,128)(2,1)}, bf16[4,2,192,256]{3,2,1,0:T(8,128)(2,1)}, bf16[2,192,192]{2,1,0:T(8,128)(2,1)}, bf16[2,192,192]{2,1,0:T(8,...) custom-call(s32[2]{0:T(128)} %len_ref.5, ...), custom_call_target="tpu_custom_call" | custom-call | flops 8000000000 | bytes 30000000 | tf_op jit(solution)/shard_map/attn_fwd/pallas_call | solution.py:330
  109.8 0.0 copy-start.8
  109.9 31.7 %ffn.1 = (bf16[2,256,768]{2,1,0:T(8,128)(2,1)}, f32[2,256,768]{2,1,0:T(8,128)}, bf16[4,2,192,256]{3,2,1,0:T(8,128)(2,1)}, bf16[4,8,216,768]{3,2,1,0:T(8,128)(2,1)}, f32[8,768]{1,0:T(8,128)}) custom-call(s32[2]{0:T(128)} %len_ref.5, s32[1]{0:T(128)} %bitcast.pos_ref, bf16[2,256,768]{2,1,0:T(8,128)(2,1)} %get-tuple-element.60.x_ref, ...), custom_call_target="tpu_custom_call" | custom-call | flops 17999998976 | bytes 40000000 | tf_op jit(solution)/shard_map/ffn/pallas_call | solution.py:464
  141.6 3.5 all-to-all-start
  145.1 0.2 reduce-scatter.3.cloned.1.call-start
  145.3 0.0 copy-done.8
  145.3 0.1 rev.3
  145.4 0.7 pad.8.rtaps_ref
  146.1 19.1 %all-to-all-done.gctx_ref = bf16[4,2,192,256]{3,2,1,0:T(8,128)(2,1)S(1)} async-done(((bf16[4,2,192,256]{3,2,1,0:T(8,128)(2,1)}), bf16[4,2,192,256]{3,2,1,0:T(8,128)(2,1)S(1)}, u32[]{:S(2)}, u32[]{:S(2)}) %all-to-all-start) | async-done | bytes 786464 | tf_op jit(solution)/shard_map/all_to_all | solution.py:633
  165.1 0.0 copy-start.5
  165.1 0.9 copy-done.5
  166.0 39.6 %attn_bwd.1 = (f32[576,768]{1,0:T(8,128)}, bf16[2,1024,768]{2,1,0:T(8,128)(2,1)}, f32[3,512]{1,0:T(4,128)}) custom-call(s32[2]{0:T(128)} %len_ref.5, bf16[2,1024,768]{2,1,0:T(8,128)(2,1)} %x_ref.3, bf16[576,768]{1,0:T(8,128)(2,1)} %bitcast.17, f32[3,512]{1,0:T(4,128)} %pad.7.taps_ref, f32[3,512]{1,0:T(4,128)} %pad.8.rtaps_ref, ...), custom_call_target="tpu_custom_call" | custom-call | flops 12000000000 | bytes 30000000 | tf_op jit(solution)/shard_map/attn_bwd/pallas_call | solution.py:596
  205.6 0.0 reduce-scatter.3.cloned.1.call-update
  205.6 0.0 reduce-scatter.5.cloned.1.call-start
  205.6 0.0 copy-start.3
  205.7 0.7 reduce-scatter.5.cloned.1.call-update
  206.3 0.0 copy-start.2
  206.4 0.0 all-gather.3.cloned.1.call-start
  206.4 0.7 all-gather.3.cloned.1.call-update
  207.1 0.0 all-gather.5.cloned.1.call-start
  207.1 57.9 %reduce-scatter.3.cloned.1.call-done = bf16[2,256,768]{2,1,0:T(8,128)(2,1)} async-done(((bf16[2,1024,768]{2,1,0:T(8,128)(2,1)}), bf16[2,256,768]{2,1,0:T(8,128)(2,1)}) %reduce-scatter.3.cloned.1.call-update) | async-done | bytes 786448 | tf_op jit(solution)/shard_map/reduce_scatter | solution.py:637
  265.1 0.0 copy-done.3
  265.1 2.2 add_convert_fusion
  267.3 0.0 all-gather.5.cloned.1.call-update
  267.3 0.0 all-reduce.5.cloned.1.call-start
  267.3 0.0 copy-done.2
  267.3 0.0 copy-start.6
  267.4 0.0 copy-start.7
  267.4 1.0 convert_element_type.18
  268.4 179.3 %reduce-scatter.5.cloned.1.call-done = bf16[1,8,216,768]{3,2,1,0:T(8,128)(2,1)} async-done(((bf16[4,8,216,768]{3,2,1,0:T(8,128)(2,1)}), bf16[1,8,216,768]{3,2,1,0:T(8,128)(2,1)}) %reduce-scatter.5.cloned.1.call-update) | async-done | bytes 2654224 | tf_op jit(solution)/shard_map/reduce_scatter | solution.py:634
  447.6 0.0 all-reduce.5.cloned.1.call-update
  447.6 0.0 copy-done.6
  447.7 44.8 %psum.31 = f32[8,768]{1,0:T(8,128)S(1)} all-reduce(f32[8,768]{1,0:T(8,128)S(1)} %copy-done.6), channel_id=1, replica_groups=mesh['dp'=8,'mp'=4] {'dp','mp'}, use_global_device_ids=true, to_apply=%region_5.6 | all-reduce | flops 6144 | bytes 49152 | tf_op jit(solution)/shard_map/psum | solution.py:641
  492.5 0.6 slice_reduce_fusion
  493.1 0.0 copy-done.7
  493.1 12.9 %psum.30 = f32[3,512]{1,0:T(4,128)S(1)} all-reduce(f32[3,512]{1,0:T(4,128)S(1)} %copy-done.7), channel_id=1, replica_groups=mesh['dp'=8,'mp'=4] {'dp'}, use_global_device_ids=true, to_apply=%region_4.5 | all-reduce | flops 1536 | bytes 12288 | tf_op jit(solution)/shard_map/psum | solution.py:642
  506.1 0.6 slice.33
  506.7 8.7 %all-gather.3.cloned.1.call-done = bf16[2,1024,768]{2,1,0:T(8,128)(2,1)} async-done(((bf16[2,256,768]{2,1,0:T(8,128)(2,1)}), bf16[2,1024,768]{2,1,0:T(8,128)(2,1)}) %all-gather.3.cloned.1.call-update) | async-done | bytes 3145744 | tf_op jit(solution)/shard_map/all_gather | solution.py:632
  515.4 64.3 %all-gather.5.cloned.1.call-done = bf16[2,1024,768]{2,1,0:T(8,128)(2,1)} async-done(((bf16[2,256,768]{2,1,0:T(8,128)(2,1)}), bf16[2,1024,768]{2,1,0:T(8,128)(2,1)}) %all-gather.5.cloned.1.call-update) | async-done | bytes 3145744 | tf_op jit(solution)/shard_map/all_gather | solution.py:638
  579.7 76.7 %all-reduce.5.cloned.1.call-done = (bf16[3,768,192]{1,2,0:T(8,128)(2,1)}, bf16[8,216,768]{2,1,0:T(8,128)(2,1)}) async-done(((bf16[3,768,192]{1,2,0:T(8,128)(2,1)}, bf16[8,216,768]{2,1,0:T(8,128)(2,1)}), (bf16[3,768,192]{1,2,0:T(8,128)(2,1)}, bf16[8,216,768]{2,1,0:T(8,128)(2,1)})) %all-reduce.5.cloned.1.call-update) | async-done | bytes 3538960 | tf_op jit(solution)/shard_map/psum | solution.py:639
  656.4 0.0 copy-start.4
  656.4 4.4 fusion
  660.8 0.0 copy-start
  660.8 2.0 slice.32
  662.7 0.0 copy-done.4
  662.7 1.4 transpose.11
  664.1 0.0 copy-done
  664.1 0.0 copy-start.1
  664.1 1.7 copy.27
  665.7 1.4 copy-done.1
  667.1 1.7 copy.28
Async XLA Ops:
  109.8 35.5 %copy-start.8 = (f32[3,33]{1,0:T(4,128)S(1)}, f32[3,33]{1,0:T(4,128)}, u32[]{:S(2)}) copy-start(f32[3,33]{1,0:T(4,128)} %param.16) | copy-start | bytes 1192
  141.6 23.6 %all-to-all-start = ((bf16[4,2,192,256]{3,2,1,0:T(8,128)(2,1)}), bf16[4,2,192,256]{3,2,1,0:T(8,128)(2,1)S(1)}, u32[]{:S(2)}, u32[]{:S(2)}) async-start(bf16[4,2,192,256]{3,2,1,0:T(8,128)(2,1)} %get-tuple-element.36), calls=%async_computation | async-start | bytes 1572864 | tf_op jit(solution)/shard_map/all_to_all | solution.py:633
  145.1 120.0 %reduce-scatter.3.cloned.1.call-start = ((), (), s32[]{:S(2)}) async-start(), calls=%async_computation.4 | async-start | bytes 3932160 | tf_op jit(solution)/shard_map/reduce_scatter | solution.py:637
  165.1 0.9 copy-start.5
  205.6 242.0 %reduce-scatter.5.cloned.1.call-start = ((), (), s32[]{:S(2)}) async-start(), calls=%async_computation.6 | async-start | bytes 13271040 | tf_op jit(solution)/shard_map/reduce_scatter | solution.py:634
  205.6 59.4 %copy-start.3 = (f32[2,256,768]{2,1,0:T(8,128)S(1)}, f32[2,256,768]{2,1,0:T(8,128)}, u32[]{:S(2)}) copy-start(f32[2,256,768]{2,1,0:T(8,128)} %get-tuple-element.34) | copy-start | bytes 4718596
  206.3 61.0 %copy-start.2 = (f32[576,768]{1,0:T(8,128)S(1)}, f32[576,768]{1,0:T(8,128)}, u32[]{:S(2)}) copy-start(f32[576,768]{1,0:T(8,128)} %get-tuple-element.47) | copy-start | bytes 5308420
  206.4 309.0 %all-gather.3.cloned.1.call-start = ((), (), s32[]{:S(2)}) async-start(), calls=%async_computation.3 | async-start | bytes 3932160 | tf_op jit(solution)/shard_map/all_gather | solution.py:632
  207.1 372.6 %all-gather.5.cloned.1.call-start = ((), (), s32[]{:S(2)}) async-start(), calls=%async_computation.5 | async-start | bytes 3932160 | tf_op jit(solution)/shard_map/all_gather | solution.py:638
  267.3 389.1 %all-reduce.5.cloned.1.call-start = ((), (), s32[]{:S(2)}) async-start(), calls=%async_computation.7 | async-start | bytes 7077888 | tf_op jit(solution)/shard_map/psum | solution.py:639
  267.3 180.3 %copy-start.6 = (f32[8,768]{1,0:T(8,128)S(1)}, f32[8,768]{1,0:T(8,128)}, u32[]{:S(2)}) copy-start(f32[8,768]{1,0:T(8,128)} %get-tuple-element.50) | copy-start | bytes 73732
  267.4 225.8 %copy-start.7 = (f32[3,512]{1,0:T(4,128)S(1)}, f32[3,512]{1,0:T(4,128)}, u32[]{:S(2)}) copy-start(f32[3,512]{1,0:T(4,128)} %get-tuple-element.49) | copy-start | bytes 18436
  656.4 6.4 copy-start.4
  660.8 3.3 copy-start
  664.1 3.0 copy-start.1
Sparse Core Ops, SparseCore 0:
  205.7 59.3 reduce-scatter.2
  267.4 180.1 reduce-scatter.4
  449.9 65.4 all-gather.2
  517.5 62.1 all-gather.4
  583.8 72.4 all-reduce.4

commit v3 on v1

--- a/solution.py
+++ b/solution.py
@@ -83,8 +83,127 @@
     return jnp.concatenate(outs, axis=0)
 
 
-def attn_fwd_kernel(docs, heads, seq, dest, len_ref, x_ref, wt_ref, taps_ref, qkv_ref, ctx_ref, lq_ref, lk_ref, sum_ref, mix_ref, k2_ref, z_ref, p_ref, l1_ref, l3_ref):
+MESH = pl.DeviceIdType.MESH
+
+
+def flip(i, bit):
+    return i + bit * (1 - 2 * ((i // bit) % 2))
+
+
+def partner(i, m):
+    for bit in (1, 2, 4):
+        if m & bit:
+            i = flip(i, bit)
+    return i
+
+
+def greet(peers):
+    bar = pltpu.get_barrier_semaphore()
+    for p in peers:
+        pl.semaphore_signal(bar, inc=1, device_id=p, device_id_type=MESH)
+    pl.semaphore_wait(bar, len(peers))
+
+
+def rcopy(src, dst, ss, rs, dev):
+    return pltpu.make_async_remote_copy(src_ref=src, dst_ref=dst, send_sem=ss, recv_sem=rs, device_id=dev, device_id_type=MESH)
+
+
+SLOTS = 8
+OW_ROWS, UP_ROWS, DN_ROWS = 24, 96, 96
+SLICE = OW_ROWS + UP_ROWS + DN_ROWS
+CUT = OW_ROWS + UP_ROWS
+PARTS = ((0, OW_ROWS), (OW_ROWS, UP_ROWS), (CUT, DN_ROWS))
+TAP0 = 112
+
+
+class Net:
+    def __init__(self, ssem, rsem):
+        self.ssem, self.rsem, self.n = ssem, rsem, 0
+        self.sent = []
+
+    def copy(self, src, dst, dev, late=True):
+        i = self.n
+        self.n += 1
+        c = rcopy(src, dst, self.ssem.at[i], self.rsem.at[i], dev)
+        if late:
+            self.sent.append(c)
+        return c
+
+    def drain(self):
+        for c in self.sent:
+            c.wait_send()
+        self.sent = []
+
+
+def place_taps(ref, scratch, reverse=False):
+    scratch[...] = jnp.zeros_like(scratch)
+    scratch[:, TAP0 : TAP0 + KSIZE] = ref[...]
+    return scratch[...]
+
+
+class Gather:
+    def __init__(self, mp, srcs, wall, net):
+        z, d = lax.axis_index("mp"), lax.axis_index("dp")
+        r = lax.rem(d, SLOTS)
+        self.ms = range(1, mp)
+        self.zc, self.yc, self.xc, self.yxc, self.xyc, self.cc = {}, {}, {}, {}, {}, {}
+        for m in self.ms:
+            w = wall.at[m - 1]
+            dev = {"mp": partner(z, m)}
+            self.zc[m] = [net.copy(srcs[i].at[r], w.at[r, pl.ds(*PARTS[i])], dev) for i in range(3)]
+            r4, r2, r6 = flip(r, 4), flip(r, 2), partner(r, 6)
+            dy, dx, dc = {"dp": flip(d, 4)}, {"dp": flip(d, 2)}, {"dp": flip(d, 1)}
+            self.yc[m] = net.copy(w.at[r], w.at[r], dy)
+            self.xc[m] = net.copy(w.at[r], w.at[r], dx)
+            s = w.at[r4, pl.ds(0, CUT)]
+            self.yxc[m] = net.copy(s, s, dx)
+            s = w.at[r2, pl.ds(CUT, DN_ROWS)]
+            self.xyc[m] = net.copy(s, s, dy)
+            self.cc[m] = [net.copy(w.at[q], w.at[q], dc) for q in (r, r4, r2, r6)]
+
+    def start(self):
+        for m in self.ms:
+            for c in self.zc[m]:
+                c.start()
+
+    def step1(self, m):
+        for c in self.zc[m]:
+            c.wait_recv()
+        self.yc[m].start()
+        self.xc[m].start()
+        self.cc[m][0].start()
+
+    def step2(self, m):
+        self.yc[m].wait_recv()
+        self.yxc[m].start()
+        self.cc[m][1].start()
+        self.xc[m].wait_recv()
+        self.xyc[m].start()
+        self.cc[m][2].start()
+
+    def step3(self, m):
+        self.yxc[m].wait_recv()
+        self.xyc[m].wait_recv()
+        self.cc[m][3].start()
+
+    def finish(self):
+        for m in self.ms:
+            for c in self.cc[m]:
+                c.wait_recv()
+
+
+def attn_fwd_kernel(docs, heads, seq, dest, len_ref, x_ref, wt_ref, taps_ref, ow_ref, up_ref, dn_ref, qkv_ref, ctx_ref, lq_ref, lk_ref, sum_ref, mix_ref, k2_ref, z_ref, p_ref, l1_ref, l3_ref, wall_ref,
+                    ctx_s, taps_s, ssem, rsem):
     width = heads * HD
+    me = lax.axis_index("mp")
+    dd = lax.axis_index("dp")
+    greet([{"mp": partner(me, m)} for m in range(1, dest)] + [{"dp": flip(dd, b)} for b in (1, 2, 4)])
+    net = Net(ssem, rsem)
+    gather = Gather(dest, (ow_ref, up_ref, dn_ref), wall_ref, net)
+    gather.start()
+
+    acs = {(m, d): net.copy(ctx_s.at[partner(me, m), d], ctx_ref.at[m, d], {"mp": partner(me, m)}) for d in range(docs) for m in range(1, dest)}
+    taps = place_taps(taps_ref, taps_s)
     mask = block_mask(width)
     eye = jnp.where(
         lax.broadcasted_iota(jnp.int32, (width, width), 0) == lax.broadcasted_iota(jnp.int32, (width, width), 1), 1.0, 0.0
@@ -93,8 +212,11 @@
         for c in range(seq // BLK):
             xc = x_ref[d, c * BLK : (c + 1) * BLK, :]
             qkv_ref[d, :, c * BLK : (c + 1) * BLK] = nt(wt_ref[...], xc).astype(BF)
+    gather.step1(1)
     k2s = []
     for d in range(docs):
+        if d == 1:
+            gather.step1(2)
         length = len_ref[d]
         memb = jnp.where(members(length, 0, seq), 1.0, 0.0).astype(F32)
         counts = jnp.maximum(jnp.sum(memb, axis=1, keepdims=True), 1.0)
@@ -136,6 +258,10 @@
             p_ref[d, i, 1] = bs[d]
             p_ref[d, i, 2] = cs[d]
             z_ref[d, i + 1] = zs[d]
+        if i == 2:
+            gather.step1(3)
+        if i == 4:
+            gather.step2(1)
     for d in range(docs):
         length = len_ref[d]
         q = qkv_ref[d, 0:width, :]
@@ -151,14 +277,28 @@
         l1_ref[d] = (m1 + jnp.log(t1)).reshape(heads, seq)
         k1 = (e1 / t1).reshape(width, seq).astype(BF)
         vl = jnp.where(live, v, 0).astype(BF)
-        ctx = nn(mix_t, k1) + banded(vl, taps_ref[...], heads, seq)
+        ctx = nn(mix_t, k1) + banded(vl, taps, heads, seq)
         ctx = jnp.where(live, ctx, 0.0).astype(BF)
         part = seq // dest
         for i in range(dest):
-            ctx_ref[i, d] = ctx[:, i * part : (i + 1) * part]
-
-
-def attn_fwd(lengths, x, wt, taps, dest):
+            ctx_s[i, d] = ctx[:, i * part : (i + 1) * part]
+        for m in range(1, dest):
+            acs[m, d].start()
+        ctx_ref[0, d] = ctx_s[me, d]
+        if d == 0:
+            gather.step2(2)
+    gather.step3(1)
+    gather.step2(3)
+    gather.step3(2)
+    gather.step3(3)
+    gather.finish()
+    for d in range(docs):
+        for m in range(1, dest):
+            acs[m, d].wait_recv()
+    net.drain()
+
+
+def attn_fwd(lengths, x, wt, taps, ow, up, dn, dest):
     docs, seq, dim = x.shape
     width = wt.shape[0] // 3
     heads = width // HD
@@ -175,16 +315,25 @@
         jax.ShapeDtypeStruct((docs, NS_ITERS, 3, width, width), F32),
         jax.ShapeDtypeStruct((docs, heads, seq), F32),
         jax.ShapeDtypeStruct((docs, width, 128), F32),
+        jax.ShapeDtypeStruct((dest - 1, SLOTS, SLICE, dim), BF),
     ]
+    any_ = pl.BlockSpec(memory_space=pl.ANY)
+    dma = pltpu.SemaphoreType.DMA
     return pl.pallas_call(
         functools.partial(attn_fwd_kernel, docs, heads, seq, dest),
         out_shape=out,
-        in_specs=[pl.BlockSpec(memory_space=pltpu.SMEM), vm, vm, vm],
-        out_specs=[vm] * len(out),
-        compiler_params=pltpu.CompilerParams(vmem_limit_bytes=60 * 2**20),
+        in_specs=[pl.BlockSpec(memory_space=pltpu.SMEM), vm, vm, vm, any_, any_, any_],
+        out_specs=[vm] * (len(out) - 1) + [any_],
+        scratch_shapes=[
+            pltpu.VMEM((dest, docs, width, seq // dest), BF),
+            pltpu.VMEM((heads, WIN), F32),
+            dma((64,)),
+            dma((64,)),
+        ],
+        compiler_params=pltpu.CompilerParams(vmem_limit_bytes=60 * 2**20, collective_id=0, has_side_effects=True),
         cost_estimate=pl.CostEstimate(flops=int(8e9), bytes_accessed=int(3e7), transcendentals=0),
         name="attn_fwd",
-    )(lengths, x, wt, taps)
+    )(lengths, x, wt, taps, ow, up, dn)
 
 
 def ln_stats(v):
@@ -205,120 +354,176 @@
 INV_ROOT_2PI = 0.3989422804014327
 
 
-def ffn_kernel(groups, docs, rows, len_ref, pos_ref, x_ref, cot_ref, ctx_ref, ow_ref, up_ref, dn_ref, g1_ref, b1_ref, g2_ref, b2_ref,
-               out_ref, gmix_ref, gctx_ref, gow_ref, gup_ref, gdn_ref, small_ref, nb_s, fac_s, act_s, br_s, x1_s, gn_s):
+def ffn_kernel(groups, docs, rows, len_ref, x_hbm, cot_hbm, ctx_ref, ow_hbm, up_hbm, dn_hbm, wall_hbm, g1_ref, b1_ref, g2_ref, b2_ref,
+               out_ref, gmix_ref, gctx_ref, s1_ref, small_ref, x_s, cot_s, w_s, rc_s, gc_s, nb_s, fac_s, act_s, br_s, x1_s, gn_s, lsem, ssem, rsem):
     n = docs * rows
-    dim = x_ref.shape[-1]
-    attn = None
+    dim = x_s.shape[-1]
+    z, dd = lax.axis_index("mp"), lax.axis_index("dp")
+    kk = lax.rem(dd, 2)
+    loads = []
+    for d in range(docs):
+        loads.append(pltpu.make_async_copy(x_hbm.at[d, pl.ds(pl.multiple_of(z * rows, rows), rows)], x_s.at[pl.ds(d * rows, rows)], lsem.at[d]))
+        loads.append(pltpu.make_async_copy(cot_hbm.at[d, pl.ds(pl.multiple_of(z * rows, rows), rows)], cot_s.at[pl.ds(d * rows, rows)], lsem.at[docs + d]))
+    own = [pltpu.make_async_copy(src, w_s.at[0, :, :, pl.ds(*PARTS[i])], lsem.at[2 * docs + i]) for i, src in enumerate((ow_hbm, up_hbm, dn_hbm))]
+    walls = [pltpu.make_async_copy(wall_hbm.at[m - 1], w_s.at[m], lsem.at[2 * docs + 2 + m]) for m in range(1, groups)]
+    for c in own + walls + loads:
+        c.start()
+    greet([{"mp": partner(z, m)} for m in range(1, groups)] + [{"dp": flip(dd, 1)}])
+    net = Net(ssem, rsem)
+    dc = {"dp": flip(dd, 1)}
+    ccs = {}
     for g in range(groups):
-        for d in range(docs):
-            pass
-    first = pos_ref[0]
-    live = jnp.concatenate(
-        [
-            (lax.broadcasted_iota(jnp.int32, (rows, 1), 0) + first < len_ref[d]).astype(F32)
-            for d in range(docs)
-        ],
-        axis=0,
-    )
+        for part, (lo, size) in enumerate(((OW_ROWS, SLICE - OW_ROWS), (0, OW_ROWS))):
+            ccs[g, part] = net.copy(w_s.at[g, :, 1 - kk, pl.ds(lo, size)], rc_s.at[g, :, pl.ds(lo, size)], dc)
+    gcs = {m: net.copy(gc_s.at[m - 1], gctx_ref.at[z], {"mp": partner(z, m)}) for m in range(1, groups)}
+
+    def take(g, part):
+        lo, size = PARTS[part]
+        return w_s[g, :, :, lo : lo + size, :].reshape(SLOTS * size, dim)
+
+    def put(g, part, val):
+        lo, size = PARTS[part]
+        w_s[g, :, :, lo : lo + size, :] = val.astype(BF).reshape(SLOTS // 2, 2, size, dim)
+
+    first = z * rows
+    live = jnp.concatenate([(lax.broadcasted_iota(jnp.int32, (rows, 1), 0) + first < len_ref[d]).astype(F32) for d in range(docs)], axis=0)
+    gain1, bias1 = g1_ref[...].reshape(1, dim), b1_ref[...].reshape(1, dim)
+    gain2, bias2 = g2_ref[...].reshape(1, dim), b2_ref[...].reshape(1, dim)
+    for c in own + walls + loads:
+        c.wait()
     parts = []
     for d in range(docs):
         acc = None
         for g in range(groups):
-            t = tn(ctx_ref[g, d], ow_ref[g]).astype(BF).astype(F32)
+            t = tn(ctx_ref[g, d], take(g, 0)).astype(BF).astype(F32)
             acc = t if acc is None else acc + t
         parts.append(acc)
-    mixed = x_ref[...].reshape(n, dim).astype(F32) + jnp.concatenate(parts, axis=0)
+    mixed = x_s[...].astype(F32) + jnp.concatenate(parts, axis=0)
     xh1, r1 = ln_stats(mixed)
     x1_s[...] = xh1
-    normed = xh1 * g1_ref[...] + b1_ref[...]
+    normed = xh1 * gain1 + bias1
     nb_s[...] = normed.astype(BF)
     br_s[...] = normed
 
     def fwd_group(g, _):
-        h = nt(nb_s[...], up_ref[g])
+        h = nn(nb_s[...], take(g, 1))
         phi_big = 0.5 * (1.0 + lax.erf(h * ROOT_HALF))
         act = (h * phi_big).astype(BF)
         act_s[g] = act
         fac_s[g] = phi_big + h * (jnp.exp(-0.5 * h * h) * INV_ROOT_2PI)
-        br_s[...] += nn(act, dn_ref[g]).astype(BF).astype(F32)
+        br_s[...] += nn(act, take(g, 2)).astype(BF).astype(F32)
         return 0
 
     lax.fori_loop(0, groups, fwd_group, 0)
     xh2, r2 = ln_stats(br_s[...])
-    out_ref[...] = (live * (xh2 * g2_ref[...] + b2_ref[...])).astype(BF).reshape(docs, rows, dim)
-    g_out = live * cot_ref[...].reshape(n, dim).astype(F32)
+    out_ref[...] = (live * (xh2 * gain2 + bias2)).astype(BF).reshape(docs, rows, dim)
+    g_out = live * cot_s[...].astype(F32)
     gg2 = jnp.sum(g_out * xh2, axis=0, keepdims=True)
     gb2 = jnp.sum(g_out, axis=0, keepdims=True)
-    g_res = ln_back(g_out * g2_ref[...], xh2, r2)
+    g_res = ln_back(g_out * gain2, xh2, r2)
     gn_s[...] = g_res
-    gbr = g_res.astype(BF)
-
-    def bwd_group(g, _):
-        act = act_s[g]
-        gdn_ref[g] = tn(act, gbr).astype(BF)
-        g_pre = (nt(gbr, dn_ref[g]) * fac_s[g]).astype(BF)
-        gup_ref[g] = tn(g_pre, nb_s[...]).astype(BF)
-        gn_s[...] += nn(g_pre, up_ref[g])
-        return 0
-
-    lax.fori_loop(0, groups, bwd_group, 0)
+    br_s[...] = g_res
+    gbr_s = x_s
+    gbr_s[...] = g_res.astype(BF)
+
+    def bwd_group(g):
+        gbr = gbr_s[...]
+        g_pre = (nt(gbr, take(g, 2)) * fac_s[g]).astype(BF)
+        put(g, 2, tn(act_s[g], gbr))
+        gn_s[...] += nt(g_pre, take(g, 1))
+        put(g, 1, tn(nb_s[...], g_pre))
+
+    for g in range(groups):
+        bwd_group(g)
+        ccs[g, 0].start()
     g_n = gn_s[...]
     xh1 = x1_s[...]
     gg1 = jnp.sum(g_n * xh1, axis=0, keepdims=True)
     gb1 = jnp.sum(g_n, axis=0, keepdims=True)
     small_ref[...] = jnp.concatenate([gg1, gb1, gg2, gb2, jnp.zeros((4, dim), F32)], axis=0)
-    g_mix = ln_back(g_n * g1_ref[...], xh1, r1)
+    g_mix = ln_back(g_n * gain1, xh1, r1)
     gmix_ref[...] = g_mix.reshape(docs, rows, dim)
     g_att = g_mix.astype(BF)
+    for m in (3, 2, 1, 0) if groups == 4 else reversed(range(groups)):
+        t = nt(take(m, 0), g_att).astype(BF)
+        for d in range(docs):
+            if m:
+                gc_s[m - 1, d] = t[:, d * rows : (d + 1) * rows]
+            else:
+                gctx_ref[z, d] = t[:, d * rows : (d + 1) * rows]
+        if m:
+            gcs[m].start()
     for g in range(groups):
         acc = None
         for d in range(docs):
-            ga = g_att[d * rows : (d + 1) * rows]
-            t = nn(ctx_ref[g, d], ga)
+            t = nn(ctx_ref[g, d], g_att[d * rows : (d + 1) * rows])
             acc = t if acc is None else acc + t
-            gctx_ref[g, d] = nt(ow_ref[g], ga).astype(BF)
-        gow_ref[g] = acc.astype(BF)
-
-
-def ffn(lengths, pos, x, cot, ctx, ow, up, dn, g1, b1, g2, b2):
-    docs, rows, dim = x.shape
-    groups, _, width, _ = ctx.shape
-    ff = up.shape[1]
+        put(g, 0, acc)
+        ccs[g, 1].start()
+    for g in range(groups):
+        ccs[g, 0].wait_recv()
+        ccs[g, 1].wait_recv()
+        for j in range(SLOTS // 2):
+            s1_ref[g, j // 2, j % 2] = (w_s[g, j, kk].astype(F32) + rc_s[g, j].astype(F32)).astype(BF)
+    for m in range(1, groups):
+        gcs[m].wait_recv()
+    net.drain()
+
+
+def ffn(lengths, x, cot, ctx, ow, up, dn, wall, g1, b1, g2, b2):
+    docs, seq, dim = x.shape
+    groups, _, width, rows = ctx.shape
+    ff = SLOTS * UP_ROWS
     n = docs * rows
     vm = pl.BlockSpec(memory_space=pltpu.VMEM)
+    any_ = pl.BlockSpec(memory_space=pl.ANY)
     sm = pl.BlockSpec(memory_space=pltpu.SMEM)
+    dma = pltpu.SemaphoreType.DMA
     out = [
         jax.ShapeDtypeStruct((docs, rows, dim), BF),
         jax.ShapeDtypeStruct((docs, rows, dim), F32),
         jax.ShapeDtypeStruct((groups, docs, width, rows), BF),
-        jax.ShapeDtypeStruct((groups, width, dim), BF),
-        jax.ShapeDtypeStruct((groups, ff, dim), BF),
-        jax.ShapeDtypeStruct((groups, ff, dim), BF),
+        jax.ShapeDtypeStruct((groups, 2, 2, SLICE, dim), BF),
         jax.ShapeDtypeStruct((8, dim), F32),
     ]
+    wall = wall.reshape(groups - 1, SLOTS // 2, 2, SLICE, dim)
+    ow, up, dn = (t.reshape(SLOTS // 2, 2, -1, dim) for t in (ow, up, dn))
     return pl.pallas_call(
         functools.partial(ffn_kernel, groups, docs, rows),
         out_shape=out,
-        in_specs=[sm, sm] + [vm] * 10,
+        in_specs=[sm, any_, any_, vm, any_, any_, any_, any_, vm, vm, vm, vm],
         out_specs=[vm] * len(out),
         scratch_shapes=[
+            pltpu.VMEM((n, dim), BF),
+            pltpu.VMEM((n, dim), BF),
+            pltpu.VMEM((groups, SLOTS // 2, 2, SLICE, dim), BF),
+            pltpu.VMEM((groups, SLOTS // 2, SLICE, dim), BF),
+            pltpu.VMEM((groups - 1, docs, width, rows), BF),
             pltpu.VMEM((n, dim), BF),
             pltpu.VMEM((groups, n, ff), F32),
             pltpu.VMEM((groups, n, ff), BF),
             pltpu.VMEM((n, dim), F32),
             pltpu.VMEM((n, dim), F32),
             pltpu.VMEM((n, dim), F32),
+            dma((2 * docs + 2 + groups,)),
+            dma((16,)),
+            dma((16,)),
         ],
-        compiler_params=pltpu.CompilerParams(vmem_limit_bytes=60 * 2**20),
+        compiler_params=pltpu.CompilerParams(vmem_limit_bytes=62 * 2**20, collective_id=1, has_side_effects=True),
         cost_estimate=pl.CostEstimate(flops=int(1.8e10), bytes_accessed=int(4e7), transcendentals=0),
         name="ffn",
-    )(lengths, pos, x, cot, ctx, ow, up, dn, g1, b1, g2, b2)
-
-
-def attn_bwd_kernel(docs, heads, seq, parts, len_ref, x_ref, wt_ref, taps_ref, rtaps_ref, qkv_ref, gctx_ref, lq_ref, lk_ref, sum_ref, mix_ref, k2_ref,
-                    z_ref, p_ref, l1_ref, l3_ref, gqkv_ref, ipart_ref, gtaps_ref, g_s, ginv_s, glq_s, glk_s):
+    )(lengths, x, cot, ctx, ow, up, dn, wall, g1, b1, g2, b2)
+
+
+def attn_bwd_kernel(docs, heads, seq, parts, dp, len_ref, x_ref, wt_ref, taps_ref, qkv_ref, gctx_ref, lq_ref, lk_ref, sum_ref, mix_ref, k2_ref,
+                    z_ref, p_ref, l1_ref, l3_ref, s1_ref, small_in, gmix_ref, gq_ref, ig_ref, taps_out, gw_ref, small_ref,
+                    g_s, ginv_s, glq_s, glk_s, taps_s, ipart_ref, gqkv_ref, ri_s, ra1, rb1, ra2, rb2, rz, fin_s, rfin, rq0, rq1, rq2, gqb, q_s, rsm, gt_s, rtp, ssem, rsem):
     width = heads * HD
+    dim = x_ref.shape[-1]
+    nd = net_setup(docs, seq, parts, dp, s1_ref, small_in, gq_ref, ig_ref, taps_out, gw_ref, small_ref, ipart_ref, gqkv_ref, ri_s, ra1, rb1, ra2, rb2, rz, fin_s, rfin, rq0, rq1, rq2, gqb, q_s, rsm, gt_s, rtp, ssem, rsem)
+    zi = lax.axis_index("mp")
+    nd.begin()
+    rtaps = place_taps(taps_ref, taps_s)
     nblk = seq // BLK
     mask = block_mask(width)
     anti = jnp.where(
@@ -354,7 +559,7 @@
         g_s[d, 0:width, :] = nn(lk_t, gs1) * SCALE
         g_s[d, width : 2 * width, :] = nn(lq_t, gs3) * SCALE
         gv = nn(gsum.T.astype(BF), k3.astype(BF))
-        gvl = banded(gc, rtaps_ref[...], heads, seq)
+        gvl = banded(gc, rtaps, heads, seq)
         g_s[d, 2 * width : 3 * width, :] = gv + jnp.where(live, gvl, 0.0)
         vl = jnp.where(live, v, 0).astype(BF)
         for h in range(heads):
@@ -366,13 +571,15 @@
             gaccs[h] = t if gaccs[h] is None else gaccs[h] + t
     for h in range(heads):
         rolled = pltpu.roll(gaccs[h], 0, 1, stride=1, stride_axis=0)
-        gtaps_ref[h : h + 1, :] = jnp.sum(rolled, axis=0, keepdims=True)
+        gt_s[h : h + 1, :] = jnp.sum(rolled, axis=0, keepdims=True)
     gz = [ginv_s[d] for d in range(docs)]
     gk = [jnp.zeros((width, width), F32) for _ in range(docs)]
     eye = jnp.where(
         lax.broadcasted_iota(jnp.int32, (width, width), 0) == lax.broadcasted_iota(jnp.int32, (width, width), 1), 1.0, 0.0
     ).astype(F32)
     for i in reversed(range(NS_ITERS)):
+        if i < NS_ITERS - 1:
+            nd.small_step()
         for d in range(docs):
             z, p, b, c = z_ref[d, i], p_ref[d, i, 0], p_ref[d, i, 1], p_ref[d, i, 2]
             a = 7.0 * eye - p
@@ -386,6 +593,7 @@
             gp = gp - ga
             gk[d] = gk[d] + nt(gp, z, HI)
             gz[d] = gzn + tn(k2_ref[d], gp, HI)
+    nd.g_step1()
     for d in range(docs):
         length = len_ref[d]
         k2 = k2_ref[d]
@@ -415,35 +623,322 @@
         else:
             gqkv_ref[...] += gw
         for c in range(nblk):
-            ipart_ref[d, c * BLK : (c + 1) * BLK, :] = tn(g_all[:, c * BLK : (c + 1) * BLK], wt_ref[...]).astype(BF)
-
-
-def attn_bwd(lengths, x, wt, taps, rtaps, qkv, gctx, lq, lk, sm, mix, k2, z, p, l1, l3):
+            t = tn(g_all[:, c * BLK : (c + 1) * BLK], wt_ref[...])
+            ipart_ref[d, c] = (t + jnp.where(zi == c, 1.0, 0.0) * gmix_ref[d]).astype(BF)
+    nd.tail()
+
+
+class net_setup:
+    def __init__(self, docs, seq, parts, dp, s1, small_in, gq, ig, taps_out, gw, small, ipart, gqkv, ri, ra1, rb1, ra2, rb2, rz, fin, rfin, rq0, rq1, rq2, gqb, q, rsm, gt, rtp, ssem, rsem):
+        self.__dict__.update({k: v for k, v in locals().items() if k != "self"})
+        self.z, self.d = lax.axis_index("mp"), lax.axis_index("dp")
+        self.r = lax.rem(self.d, SLOTS)
+        self.y, self.x, self.k = self.r // 4, lax.rem(self.r // 2, 2), lax.rem(self.r, 2)
+        self.net = Net(ssem, rsem)
+        self.extra = [b for b in (8, 16, 32, 64, 128) if b < dp]
+        self.low = (1, 2, 4)
+        self.bits = list(self.low) + self.extra
+
+    def dev(self, bit):
+        return {"dp": flip(self.d, bit)}
+
+    def zdev(self, m):
+        return {"mp": partner(self.z, m)}
+
+    def begin(self):
+        greet([self.zdev(m) for m in range(1, self.parts)] + [self.dev(b) for b in self.bits])
+        c = self.net.copy
+        self.a1 = c(self.s1.at[:, 1 - self.y, :, pl.ds(0, CUT)], self.ra1, self.dev(4))
+        self.b1 = c(self.s1.at[:, :, 1 - self.x, pl.ds(CUT, DN_ROWS)], self.rb1, self.dev(2))
+        self.a1.start()
+        self.b1.start()
+        self.small[...] = self.small_in[...]
+        self.smalls = self.chain(self.small, self.rsm, [self.dev(b) for b in self.bits] + [self.zdev(1 << j) for j in range(self.parts.bit_length() - 1)])
+        self.small_step()
+
+    def double(self, buf, recv, bit_dev):
+        c = self.net.copy(buf, recv, bit_dev, late=False)
+        c.start()
+        c.wait()
+        buf[...] = (buf[...].astype(F32) + recv[...].astype(F32)).astype(buf.dtype)
+
+    def chain(self, buf, recv, devs):
+        for i, dev in enumerate(devs):
+            c = self.net.copy(buf, recv.at[i], dev, late=False)
+            c.start()
+            yield
+            c.wait()
+            buf[...] = buf[...] + recv[i]
+        while True:
+            yield
+
+    def small_step(self):
+        next(self.smalls)
+
+    def g_step1(self):
+        c = self.net.copy
+        self.a1.wait_recv()
+        self.b1.wait_recv()
+        for g in range(self.parts):
+            for j in range(2):
+                self.ra1[g, j] = (self.ra1[g, j].astype(F32) + self.s1[g, self.y, j, 0:CUT].astype(F32)).astype(BF)
+                self.rb1[g, j] = (self.rb1[g, j].astype(F32) + self.s1[g, j, self.x, CUT:SLICE].astype(F32)).astype(BF)
+        self.a2 = c(self.ra1.at[:, 1 - self.x], self.ra2, self.dev(2))
+        self.b2 = c(self.rb1.at[:, 1 - self.y], self.rb2, self.dev(4))
+        self.a2.start()
+        self.b2.start()
+
+    def g_step2(self):
+        c = self.net.copy
+        self.a2.wait_recv()
+        self.b2.wait_recv()
+        for g in range(self.parts):
+            self.ra2[g] = (self.ra2[g].astype(F32) + self.ra1[g, self.x].astype(F32)).astype(BF)
+            self.rb2[g] = (self.rb2[g].astype(F32) + self.rb1[g, self.y].astype(F32)).astype(BF)
+        self.zs = []
+        for m in range(1, self.parts):
+            self.zs.append(c(self.ra2.at[m], self.rz.at[m - 1, pl.ds(0, CUT)], self.zdev(m)))
+            self.zs.append(c(self.rb2.at[m], self.rz.at[m - 1, pl.ds(CUT, DN_ROWS)], self.zdev(m)))
+        for s in self.zs:
+            s.start()
+
+    def g_step3(self):
+        c = self.net.copy
+        for s in self.zs:
+            s.wait_recv()
+        top, bot = self.ra2[0].astype(F32), self.rb2[0].astype(F32)
+        for m in range(1, self.parts):
+            top = top + self.rz[m - 1, 0:CUT].astype(F32)
+            bot = bot + self.rz[m - 1, CUT:SLICE].astype(F32)
+        self.fin[0:CUT] = top.astype(BF)
+        self.fin[CUT:SLICE] = bot.astype(BF)
+        for i, b in enumerate(self.extra):
+            self.double(self.fin, self.rfin.at[i], self.dev(b))
+        r, gw = self.r, self.gw
+        gw[r] = self.fin[...]
+        r4, r2, r6 = flip(r, 4), flip(r, 2), partner(r, 6)
+        self.gy = c(gw.at[r], gw.at[r], self.dev(4))
+        self.gx = c(gw.at[r], gw.at[r], self.dev(2))
+        self.gyx = c(gw.at[r4, pl.ds(0, CUT)], gw.at[r4, pl.ds(0, CUT)], self.dev(2))
+        self.gxy = c(gw.at[r2, pl.ds(CUT, DN_ROWS)], gw.at[r2, pl.ds(CUT, DN_ROWS)], self.dev(4))
+        self.gc = [c(gw.at[q], gw.at[q], self.dev(1)) for q in (r, r4, r2, r6)]
+        self.gy.start()
+        self.gx.start()
+        self.gc[0].start()
+
+    def g_step4(self):
+        self.gy.wait_recv()
+        self.gyx.start()
+        self.gc[1].start()
+        self.gx.wait_recv()
+        self.gxy.start()
+        self.gc[2].start()
+
+    def g_step5(self):
+        self.gyx.wait_recv()
+        self.gxy.wait_recv()
+        self.gc[3].start()
+        for s in self.gc:
+            s.wait_recv()
+
+    def q_step0(self):
+        self.half = self.gqkv.shape[0] // 2
+        self.gqb[...] = self.gqkv[...].astype(BF)
+        h = self.half
+        self.q0 = self.net.copy(self.gqb.at[pl.ds(pl.multiple_of((1 - self.k) * h, 8), h)], self.rq0, self.dev(1))
+        self.q0.start()
+
+    def q_step1(self):
+        h = self.half
+        self.q0.wait_recv()
+        self.q[...] = (self.gqb[pl.ds(pl.multiple_of(self.k * h, 8), h)].astype(F32) + self.rq0[...].astype(F32)).astype(BF)
+        self.qa = [self.net.copy(self.q.at[pl.ds(0, h // 2)], self.rq1.at[pl.ds(0, h // 2)], self.dev(4), late=False),
+                   self.net.copy(self.q.at[pl.ds(h // 2, h // 2)], self.rq1.at[pl.ds(h // 2, h // 2)], self.dev(2), late=False)]
+        for s in self.qa:
+            s.start()
+
+    def q_step2(self):
+        h = self.half
+        for s in self.qa:
+            s.wait()
+        self.q[...] = (self.q[...].astype(F32) + self.rq1[...].astype(F32)).astype(BF)
+        self.qb = [self.net.copy(self.q.at[pl.ds(0, h // 2)], self.rq2.at[0, pl.ds(0, h // 2)], self.dev(2), late=False),
+                   self.net.copy(self.q.at[pl.ds(h // 2, h // 2)], self.rq2.at[0, pl.ds(h // 2, h // 2)], self.dev(4), late=False)]
+        for s in self.qb:
+            s.start()
+
+    def q_step3(self):
+        h = self.half
+        for s in self.qb:
+            s.wait()
+        self.q[...] = (self.q[...].astype(F32) + self.rq2[0].astype(F32)).astype(BF)
+        for i, b in enumerate(self.extra):
+            self.double(self.q, self.rq2.at[1 + i], self.dev(b))
+        mine = pl.ds(pl.multiple_of(self.k * h, 8), h)
+        self.gq[mine] = self.q[...]
+        self.qc = self.net.copy(self.gq.at[mine], self.gq.at[mine], self.dev(1))
+        self.qc.start()
+
+    def taps_step(self):
+        next(self.taps)
+
+    def i_setup(self):
+        last = self.parts - 1
+        self.chunks = self.ipart.shape[1]
+        rows = self.ipart.shape[2]
+        self.pos, self.red, self.bc = [], {}, {}
+        for d in range(self.docs):
+            p = self.z if d % 2 == 0 else last - self.z
+            step = 1 if d % 2 == 0 else -1
+            self.pos.append(p)
+            lower = {"mp": lax.rem(self.z - step + self.parts, self.parts)}
+            upper = {"mp": lax.rem(self.z + step + self.parts, self.parts)}
+            for c in range(self.chunks):
+                self.red[d, c] = self.net.copy(self.ipart.at[d, c], self.ri.at[d, c], lower, late=False)
+                out = self.ig.at[d, pl.ds(c * rows, rows)]
+                self.bc[d, c] = self.net.copy(out, out, upper, late=False)
+
+    def i_reduce(self, d, c):
+        last = self.parts - 1
+        p = self.pos[d]
+        rows = self.ipart.shape[2]
+
+        @pl.when(p < last)
+        def _():
+            self.red[d, c].wait_recv()
+            self.ipart[d, c] = (self.ipart[d, c].astype(F32) + self.ri[d, c].astype(F32)).astype(BF)
+
+        @pl.when(p > 0)
+        def _():
+            self.red[d, c].start()
+
+        @pl.when(p == 0)
+        def _():
+            self.ig[d, c * rows : (c + 1) * rows] = self.ipart[d, c]
+            self.bc[d, c].start()
+
+    def i_back(self, d, c):
+        last = self.parts - 1
+        p = self.pos[d]
+
+        @pl.when(p > 0)
+        def _():
+            self.bc[d, c].wait_recv()
+
+        @pl.when((p > 0) & (p < last))
+        def _():
+            self.bc[d, c].start()
+
+    def i_end(self):
+        last = self.parts - 1
+        for d in range(self.docs):
+            p = self.pos[d]
+            for c in range(self.chunks):
+
+                @pl.when(p > 0)
+                def _():
+                    self.red[d, c].wait_send()
+
+                @pl.when(p < last)
+                def _():
+                    self.bc[d, c].wait_send()
+
+    def tail(self):
+        self.i_setup()
+        self.taps_out[...] = self.gt[...]
+        self.taps = self.chain(self.taps_out, self.rtp, [self.dev(b) for b in self.bits])
+        two = range(self.docs)
+
+        def red(c):
+            for d in two:
+                self.i_reduce(d, c)
+
+        def back(c):
+            for d in two:
+                self.i_back(d, c)
+
+        self.q_step0()
+        self.taps_step()
+        red(0)
+        self.q_step1()
+        self.g_step2()
+        self.taps_step()
+        red(1)
+        self.q_step2()
+        self.taps_step()
+        red(2)
+        self.q_step3()
+        self.taps_step()
+        back(0)
+        for _ in self.extra:
+            self.taps_step()
+            self.small_step()
+        red(3)
+        self.g_step3()
+        back(1)
+        self.g_step4()
+        back(2)
+        self.g_step5()
+        back(3)
+        self.qc.wait_recv()
+        self.i_end()
+        self.net.drain()
+
+
+def attn_bwd(dp, lengths, x, wt, taps, qkv, gctx, lq, lk, sm, mix, k2, z, p, l1, l3, s1, small, gmix):
     docs, seq, dim = x.shape
     width = wt.shape[0] // 3
     heads = width // HD
     parts = gctx.shape[0]
+    nblk = seq // BLK
+    more = max(1, dp.bit_length() - 4)
+    steps = dp.bit_length() + parts.bit_length()
     vm = pl.BlockSpec(memory_space=pltpu.VMEM)
+    dma = pltpu.SemaphoreType.DMA
     out = [
-        jax.ShapeDtypeStruct((3 * width, dim), F32),
+        jax.ShapeDtypeStruct((3 * width, dim), BF),
         jax.ShapeDtypeStruct((docs, seq, dim), BF),
         jax.ShapeDtypeStruct((heads, WIN), F32),
+        jax.ShapeDtypeStruct((SLOTS, SLICE, dim), BF),
+        jax.ShapeDtypeStruct((8, dim), F32),
     ]
+    h = 3 * width // 2
     return pl.pallas_call(
-        functools.partial(attn_bwd_kernel, docs, heads, seq, parts),
+        functools.partial(attn_bwd_kernel, docs, heads, seq, parts, dp),
         out_shape=out,
-        in_specs=[pl.BlockSpec(memory_space=pltpu.SMEM)] + [vm] * 15,
+        in_specs=[pl.BlockSpec(memory_space=pltpu.SMEM)] + [vm] * 17,
         out_specs=[vm] * len(out),
         scratch_shapes=[
             pltpu.VMEM((docs, 3 * width, seq), F32),
             pltpu.VMEM((docs, width, width), F32),
             pltpu.VMEM((docs, width, width), F32),
             pltpu.VMEM((docs, width, width), F32),
+            pltpu.VMEM((heads, WIN), F32),
+            pltpu.VMEM((docs, nblk, BLK, dim), BF),
+            pltpu.VMEM((3 * width, dim), F32),
+            pltpu.VMEM((docs, nblk, BLK, dim), BF),
+            pltpu.VMEM((parts, 2, CUT, dim), BF),
+            pltpu.VMEM((parts, 2, DN_ROWS, dim), BF),
+            pltpu.VMEM((parts, CUT, dim), BF),
+            pltpu.VMEM((parts, DN_ROWS, dim), BF),
+            pltpu.VMEM((parts - 1, SLICE, dim), BF),
+            pltpu.VMEM((SLICE, dim), BF),
+            pltpu.VMEM((more, SLICE, dim), BF),
+            pltpu.VMEM((h, dim), BF),
+            pltpu.VMEM((h, dim), BF),
+            pltpu.VMEM((1 + more, h, dim), BF),
+            pltpu.VMEM((3 * width, dim), BF),
+            pltpu.VMEM((h, dim), BF),
+            pltpu.VMEM((steps, 8, dim), F32),
+            pltpu.VMEM((heads, WIN), F32),
+            pltpu.VMEM((steps, heads, WIN), F32),
+            dma((96,)),
+            dma((96,)),
         ],
-        compiler_params=pltpu.CompilerParams(vmem_limit_bytes=60 * 2**20),
+        compiler_params=pltpu.CompilerParams(vmem_limit_bytes=62 * 2**20, collective_id=2, has_side_effects=True),
         cost_estimate=pl.CostEstimate(flops=int(1.2e10), bytes_accessed=int(3e7), transcendentals=0),
         name="attn_bwd",
-    )(lengths, x, wt, taps, rtaps, qkv, gctx, lq, lk, sm, mix, k2, z, p, l1, l3)
+    )(lengths, x, wt, taps, qkv, gctx, lq, lk, sm, mix, k2, z, p, l1, l3, s1, small, gmix)
 
 
 def body_factory(dp, mp):
@@ -451,40 +946,19 @@
         docs, seq, dim = tokens.shape
         width = qkv_weight.shape[2]
         ff = up_weight.shape[1]
-        me = lax.axis_index("mp")
-        rows = seq // mp
         wt = jnp.transpose(qkv_weight, (0, 2, 1)).reshape(3 * width, dim)
-        taps = jnp.pad(conv_taps, ((0, 0), (112, WIN - 112 - KSIZE)))
-        rtaps = jnp.pad(conv_taps[:, ::-1], ((0, 0), (112, WIN - 112 - KSIZE)))
-        qkv, ctx, lq, lk, sm, mix, k2, z, p, l1, l3 = attn_fwd(lengths, tokens, wt, taps, mp)
-        ctx_rows = lax.all_to_all(ctx, "mp", 0, 0, tiled=True)
-        w_all = jnp.concatenate([out_weight, up_weight.T, down_weight], axis=0)
-        w_all = lax.all_gather(w_all, "mp", axis=0, tiled=False)
-        ow, up, dn = w_all[:, :width], w_all[:, width : width + ff], w_all[:, width + ff :]
-        first = me * rows
-        x_rows = lax.dynamic_slice_in_dim(tokens, first, rows, 1)
-        cot_rows = lax.dynamic_slice_in_dim(cotangent, first, rows, 1)
-        pos = jnp.reshape(first, (1,)).astype(jnp.int32)
-        out_rows, gmix, gctx, gow, gup, gdn, small = ffn(
-            lengths, pos, x_rows, cot_rows, ctx_rows, ow, up, dn,
-            norm1_gain[None], norm1_bias[None], norm2_gain[None], norm2_bias[None],
-        )
+        ow, up, dn = (t.reshape(SLOTS, -1, dim) for t in (out_weight, up_weight, down_weight))
+        qkv, ctx, lq, lk, sm, mix, k2, z, p, l1, l3, wall = attn_fwd(lengths, tokens, wt, conv_taps, ow, up, dn, mp)
+        out_rows, gmix, gctx, s1, small = ffn(lengths, tokens, cotangent, ctx, ow, up, dn, wall, norm1_gain, norm1_bias, norm2_gain, norm2_bias)
         output = lax.all_gather(out_rows, "mp", axis=1, tiled=True)
-        gctx_heads = lax.all_to_all(gctx, "mp", 0, 0, tiled=True)
-        gw = jnp.concatenate([gow, gup, gdn], axis=1)
-        gw = lax.psum_scatter(gw, "mp", scatter_dimension=0, tiled=False)
-        gw = lax.psum(gw, "dp").astype(F32)
-        gqkv, ipart, gtaps = attn_bwd(lengths, tokens, wt, taps, rtaps, qkv, gctx_heads, lq, lk, sm, mix, k2, z, p, l1, l3)
-        ipart = lax.psum_scatter(ipart, "mp", scatter_dimension=1, tiled=True).astype(F32)
-        input_grad = lax.all_gather((gmix + ipart).astype(BF), "mp", axis=1, tiled=True)
-        gqkv = lax.psum(gqkv.astype(BF), "dp").astype(F32)
-        gqkv = jnp.transpose(gqkv.reshape(3, width, dim), (0, 2, 1))
-        small = lax.psum(small, ("dp", "mp"))
-        gtaps = lax.psum(gtaps, "dp")
+        rtaps = conv_taps[:, ::-1]
+        gqkv, input_grad, gtaps, gw, small = attn_bwd(dp, lengths, tokens, wt, rtaps, qkv, gctx, lq, lk, sm, mix, k2, z, p, l1, l3, s1, small, gmix)
+        gqkv = jnp.transpose(gqkv.astype(F32).reshape(3, width, dim), (0, 2, 1))
         gtaps = lax.slice_in_dim(gtaps, 367, 367 + KSIZE, axis=1)
+        gw = gw.astype(F32)
         return (
-            output, input_grad, gqkv, gw[:width], gtaps, small[0], small[1], small[2], small[3],
-            gw[width : width + ff].T, gw[width + ff :],
+            output, input_grad, gqkv, gw[:, :OW_ROWS].reshape(width, dim), gtaps, small[0], small[1], small[2], small[3],
+            gw[:, OW_ROWS:CUT].reshape(dim, ff), gw[:, CUT:].reshape(ff, dim),
         )
     return body
 

time: 805 us -> 520 us (0.65)
  waiting for transfers between devices: 564 us -> 0.02 us
  Pallas kernels: 94.4 us -> 481 us
  blocking collectives: 59.8 us -> 0 us
  local copies, waits for them, and re-layouts: 33 us -> 13.7 us
  other arithmetic: 18.6 us -> 2.52 us
  starting transfers between devices: 8.78 us -> 0.04 us
    pallas_call x1, Pallas kernels: 39.6 us -> 366 us  [attn_bwd(): pl.pallas_call(functools.partial(attn_bwd_kernel, docs, heads, seq, parts...]
    all_gather x2 -> x0, waiting for transfers between devices: 234 us -> none  [the longest x1 170 us: body(): w_all = lax.all_gather(w_all, 'mp', axis=0, tiled=False)]
    reduce_scatter x2 -> x0, waiting for transfers between devices: 228 us -> none  [the longest x1 179 us: body(): gw = lax.psum_scatter(gw, 'mp', scatter_dimension=0, tiled=False)]
    psum x1 -> x0, waiting for transfers between devices: 76.7 us -> none  [body(): gqkv = lax.psum(gqkv.astype(BF), 'dp').astype(F32)]
    psum x2 -> x0, blocking collectives: 59.8 us -> none  [the longest x1 46.9 us: body(): small = lax.psum(small, ('dp', 'mp'))]
    pallas_call x1, Pallas kernels: 24 us -> 64.8 us  [attn_fwd(): pl.pallas_call(functools.partial(attn_fwd_kernel, docs, heads, seq, dest)...]
    all_to_all x2 -> x0, waiting for transfers between devices: 19.6 us -> none  [the longest x1 19.6 us: body(): gctx_heads = lax.all_to_all(gctx, 'mp', 0, 0, tiled=True)]
    pallas_call x1, Pallas kernels: 30.8 us -> 49.8 us  [ffn(): pl.pallas_call(functools.partial(ffn_kernel, groups, docs, rows), out_sha...]
  transfers between devices with their start and end apart: 8 -> 1, of which waited for: 7 -> 0; matrix products, arithmetic and copies ran while one was open for 4% -> 2% of each run, Pallas kernels for 3% -> 72%
where the time goes in v3:
time: 520 us; the launch traced here: 511 us
  Pallas kernels  481 us (92%)
  between operations  14.3 us (3%)
  local copies, waits for them, and re-layouts  13.7 us (3%)
    pallas_call x1, Pallas kernels, attn_bwd(): pl.pallas_call(functools.partial(attn_bwd_kernel, docs, heads, seq, parts...  366 us
    pallas_call x1, Pallas kernels, attn_fwd(): pl.pallas_call(functools.partial(attn_fwd_kernel, docs, heads, seq, dest)...  64.8 us
    pallas_call x1, Pallas kernels, ffn(): pl.pallas_call(functools.partial(ffn_kernel, groups, docs, rows), out_sha...  49.8 us
  transfers between devices with their start and end apart: 1, of which 0 were waited for; matrix products, arithmetic and copies ran while one was open for 2% of the time, Pallas kernels for 72%

profile of v3, /device:TPU:4, one launch (start us, length us, event | category | flops | bytes accessed | tf_op | source)
XLA Modules:
  0.0 511.2 jit_solution(10856050725799406674)
XLA Ops:
  7.2 0.0 all-gather.2.cloned.1.call-start
  7.2 64.8 %attn_fwd.1 = (bf16[2,576,1024]{2,1,0:T(8,128)(2,1)}, bf16[4,2,192,256]{3,2,1,0:T(8,128)(2,1)}, bf16[2,192,192]{2,1,0:T(8,128)(2,1)}, bf16[2,192,192]{2,1,0:T(8,...) custom-call(s32[2]{0:T(128)} %len_ref.5, ...), custom_call_target="tpu_custom_call" | custom-call | flops 8000000000 | bytes 30000000 | tf_op jit(solution)/shard_map/attn_fwd/pallas_call | solution.py:322
  72.1 0.0 copy-start.2
  72.1 49.8 %ffn.1 = (bf16[2,256,768]{2,1,0:T(8,128)(2,1)}, f32[2,256,768]{2,1,0:T(8,128)}, bf16[4,2,192,256]{3,2,1,0:T(8,128)(2,1)}, bf16[4,2,2,216,768]{4,3,2,1,0:T(8,128)(2,1)}, f32[8,768]{1,0:T(8,128)}) custom-call(s32[2]{0:T(128)} %len_ref.5, bf16[2,1024,768]{2,1,0:T(8,128)(2,1)} %x_ref.3, bf16[2,1024,768]{2,1,0:T(8,128)(2,1)} %cot_hbm.1, ...), custom_call_target="tpu_custom_call" | custom-call | flops 17999998976 | bytes 40000000 | tf_op jit(solution)/shard_map/ffn/pallas_call | solution.py:491
  121.9 0.0 all-gather.2.cloned.1.call-update
  122.0 0.0 copy-done.2
  122.0 0.7 rev.3.taps_ref
  122.6 366.0 %attn_bwd.1 = (bf16[576,768]{1,0:T(8,128)(2,1)}, bf16[2,1024,768]{2,1,0:T(8,128)(2,1)}, f32[3,512]{1,0:T(4,128)}, bf16[8,216,768]{2,1,0:T(8,128)(2,1)}, f32[8,768]{1,0:T(8,128)}) custom-call(s32[2]{0:T(128)} %len_ref.5, bf16[2,1024,768]{2,1,0:T(8,128)(2,1)} %x_ref.3, bf16[576,768]{1,0:T(8,128)(2,1)} %bitcast.26, f32[3,33]{1,0:T(4,128)} %rev.3.taps_ref, ...), custom_call_target="tpu_custom_call" | custom-call | flops 12000000000 | bytes 30000000 | tf_op jit(solution)/shard_map/attn_bwd/pallas_call | solution.py:906
  488.6 0.0 copy-start
  488.6 2.0 slice.32
  490.6 1.3 slice.25
  491.9 1.5 slice_reduce_fusion
  493.4 2.5 convert_bitcast_fusion
  496.0 0.0 copy-done
  496.0 2.7 fusion
  498.6 0.0 all-gather.2.cloned.1.call-done
  498.6 0.0 copy-start.1
  498.6 3.9 copy.25
  502.5 0.0 copy-done.1
  502.5 1.7 copy.26
Async XLA Ops:
  7.2 491.4 %all-gather.2.cloned.1.call-start = ((), (), s32[]{:S(2)}) async-start(), calls=%async_computation | async-start | bytes 3932160 | tf_op jit(solution)/shard_map/all_gather | solution.py:953
  72.1 49.9 %copy-start.2 = (f32[3,33]{1,0:T(4,128)S(1)}, f32[3,33]{1,0:T(4,128)}, u32[]{:S(2)}) copy-start(f32[3,33]{1,0:T(4,128)} %taps_ref.1) | copy-start | bytes 1192
  488.6 7.3 %copy-start = (bf16[8,216,768]{2,1,0:T(8,128)(2,1)S(1)}, bf16[8,216,768]{2,1,0:T(8,128)(2,1)}, u32[]{:S(2)}) copy-start(bf16[8,216,768]{2,1,0:T(8,128)(2,1)} %get-tuple-element.52) | copy-start | bytes 7962628
  498.6 3.9 copy-start.1
Sparse Core Ops, SparseCore 0:
  122.1 62.6 all-gather.1

commit v4 on v1

v4 whole, which is shorter than its diff:
```python
import functools

import jax
import jax.numpy as jnp
from jax import lax
from jax.experimental import pallas as pl
from jax.experimental.pallas import tpu as pltpu
from jax.sharding import PartitionSpec as P

HD = 64
LM = 64
KSIZE = 33
NS_ITERS = 6
EPS = 1e-5
HI = lax.Precision.HIGHEST
BF = jnp.bfloat16
F32 = jnp.float32
SCALE = HD**-0.5
WIN = 512
BLK = 256
CHUNK = 128
TAP0 = 112
TAP_END = TAP0 + BLK - 1
ROOT_HALF = 0.7071067811865476
INV_ROOT_2PI = 0.3989422804014327
MESH = pl.DeviceIdType.MESH
SLOTS = 8
OW_ROWS, UP_ROWS, DN_ROWS = 24, 96, 96
SLICE = OW_ROWS + UP_ROWS + DN_ROWS
CUT = OW_ROWS + UP_ROWS
GCUT = 112
PARTS = ((0, OW_ROWS), (OW_ROWS, UP_ROWS), (CUT, DN_ROWS))
VM = pl.BlockSpec(memory_space=pltpu.VMEM)
SM = pl.BlockSpec(memory_space=pltpu.SMEM)
ANY = pl.BlockSpec(memory_space=pl.ANY)
DMA = pltpu.SemaphoreType.DMA


def nn(a, b, precision=None):
    return lax.dot_general(a, b, (((1,), (0,)), ((), ())), precision=precision, preferred_element_type=F32)


def nt(a, b, precision=None):
    return lax.dot_general(a, b, (((1,), (1,)), ((), ())), precision=precision, preferred_element_type=F32)


def tn(a, b, precision=None):
    return lax.dot_general(a, b, (((0,), (0,)), ((), ())), precision=precision, preferred_element_type=F32)


def block_mask(width):
    r = lax.broadcasted_iota(jnp.int32, (width, width), 0) // HD
    c = lax.broadcasted_iota(jnp.int32, (width, width), 1) // HD
    return r == c


def identity(width):
    r = lax.broadcasted_iota(jnp.int32, (width, width), 0)
    c = lax.broadcasted_iota(jnp.int32, (width, width), 1)
    return jnp.where(r == c, 1.0, 0.0).astype(F32)


def spread(x, heads, mask):
    return jnp.where(mask, jnp.concatenate([x] * heads, axis=0), 0.0)


def per_head_total(col, heads):
    tot = jnp.sum(col.reshape(heads, HD, 1), axis=1, keepdims=True)
    return jnp.broadcast_to(tot, (heads, HD, 1)).reshape(heads * HD, 1)


def members(length, count):
    s = lax.broadcasted_iota(jnp.int32, (LM, count), 1)
    j = lax.broadcasted_iota(jnp.int32, (LM, count), 0)
    s64 = s * LM
    return (j * length <= s64) & (s64 < (j + 1) * length) & (s < length)


def live_lanes(length, count):
    return lax.broadcasted_iota(jnp.int32, (1, count), 1) < length


def toeplitz(row):
    return pltpu.roll(jnp.broadcast_to(row, (BLK, WIN)), 0, 1, stride=1, stride_axis=0)


def windows(x, seq):
    pad = jnp.zeros((x.shape[0], 128), x.dtype)
    padded = jnp.concatenate([pad, x, pad], axis=1)
    return jnp.concatenate([padded[:, b * BLK : b * BLK + WIN] for b in range(seq // BLK)], axis=0)


def hi_lo(x):
    hi = x.astype(BF)
    return hi, (x - hi.astype(F32)).astype(BF)


def banded(x, row, heads, seq):
    outs = []
    for h in range(heads):
        wins = windows(x[h * HD : (h + 1) * HD], seq)
        hi, lo = hi_lo(toeplitz(row[h : h + 1]))
        y = nt(wins, hi) + nt(wins, lo)
        outs.append(jnp.concatenate([y[b * HD : (b + 1) * HD] for b in range(seq // BLK)], axis=1))
    return jnp.concatenate(outs, axis=0)


def flip(i, bit):
    return i + bit * (1 - 2 * ((i // bit) % 2))


def partner(i, m):
    for bit in (1, 2, 4):
        if m & bit:
            i = flip(i, bit)
    return i


def greet(peers):
    bar = pltpu.get_barrier_semaphore()
    for p in peers:
        pl.semaphore_signal(bar, inc=1, device_id=p, device_id_type=MESH)
    pl.semaphore_wait(bar, len(peers))


def rcopy(src, dst, ss, rs, dev):
    return pltpu.make_async_remote_copy(src_ref=src, dst_ref=dst, send_sem=ss, recv_sem=rs, device_id=dev, device_id_type=MESH)


class Net:
    def __init__(self, ssem, rsem):
        self.ssem, self.rsem, self.n = ssem, rsem, 0
        self.sent = []

    def copy(self, src, dst, dev, late=True):
        i = self.n
        self.n += 1
        c = rcopy(src, dst, self.ssem.at[i], self.rsem.at[i], dev)
        if late:
            self.sent.append(c)
        return c

    def drain(self):
        for c in self.sent:
            c.wait_send()
        self.sent = []


def at(i, steps):
    for k, f in steps.items():

        @pl.when(i == k)
        def _():
            f()


class Local:
    def __init__(self, sem):
        self.sem, self.n, self.open = sem, 0, []

    def start(self, src, dst):
        c = pltpu.make_async_copy(src, dst, self.sem.at[self.n])
        self.n += 1
        c.start()
        self.open.append(c)
        return c

    def finish(self):
        for c in self.open:
            c.wait()
        self.open = []


class Line:
    def __init__(self, parts):
        self.last, self.z = parts - 1, lax.axis_index("mp")

    def sends(self, way, s):
        z = self.z
        return (z < self.last) & (z >= s) if way == 0 else (z > 0) & (z + s <= self.last)

    def gets(self, way, s):
        z = self.z
        return z - 1 >= s if way == 0 else z + 1 + s <= self.last

    def sent_from(self, way, s):
        return self.z - (1 - 2 * way) * s

    def got_from(self, way, s):
        return self.z - (1 - 2 * way) * (s + 1)

    def ahead(self, way):
        size = self.last + 1
        return {"mp": lax.rem(self.z + (1 - 2 * way) + size, size)}


class Gather:
    def __init__(self, mp, srcs, wall, zsem, psem):
        self.line = Line(mp)
        self.srcs, self.wall, self.zsem, self.psem = srcs, wall, zsem, psem
        self.d = lax.axis_index("dp")
        r = lax.rem(self.d, SLOTS)
        self.rs = (r, flip(r, 4), flip(r, 2), partner(r, 6))
        self.steps = mp - 1

    def z(self, way, s, origin):
        dev = self.line.ahead(way)
        r = self.rs[0]
        out = []
        for i, (lo, size) in enumerate(PARTS):
            dst = self.wall.at[origin, r, pl.ds(lo, size)]
            src = self.srcs[i].at[r] if s == 0 else dst
            out.append(rcopy(src, dst, self.zsem.at[0, way, s, i], self.zsem.at[1, way, s, i], dev))
        return out

    def plane(self, way, s, k):
        w = self.wall.at[self.line.got_from(way, s)]
        q, rows, bit = (
            (0, (0, SLICE), 4),
            (0, (0, SLICE), 2),
            (1, (0, CUT), 2),
            (2, (CUT, DN_ROWS), 4),
            (0, (0, SLICE), 1),
            (1, (0, SLICE), 1),
            (2, (0, SLICE), 1),
            (3, (0, SLICE), 1),
        )[k]
        ref = w.at[self.rs[q], pl.ds(*rows)]
        return rcopy(ref, ref, self.psem.at[0, way, s, k], self.psem.at[1, way, s, k], {"dp": flip(self.d, bit)})

    def send(self, s):
        for way in range(2):

            @pl.when(self.line.sends(way, s))
            def _():
                for c in self.z(way, s, self.line.sent_from(way, s)):
                    c.start()

    def got(self, s, f):
        for way in range(2):
            pl.when(self.line.gets(way, s))(functools.partial(f, way, s))

    def step1(self, s):
        def arrive(way, s):
            for c in self.z(way, s, self.line.got_from(way, s)):
                c.wait_recv()

        self.got(s, arrive)
        if s + 1 < self.steps:
            self.send(s + 1)

        def pass_on(way, s):
            for k in (0, 1, 4):
                self.plane(way, s, k).start()

        self.got(s, pass_on)

    def step2(self, s):
        def f(way, s):
            self.plane(way, s, 0).wait_recv()
            self.plane(way, s, 2).start()
            self.plane(way, s, 5).start()
            self.plane(way, s, 1).wait_recv()
            self.plane(way, s, 3).start()
            self.plane(way, s, 6).start()

        self.got(s, f)

    def step3(self, s):
        def f(way, s):
            self.plane(way, s, 2).wait_recv()
            self.plane(way, s, 3).wait_recv()
            self.plane(way, s, 7).start()

        self.got(s, f)

    def finish(self):
        def f(way, s):
            for k in range(8):
                if k >= 4:
                    self.plane(way, s, k).wait_recv()
                self.plane(way, s, k).wait_send()

        for s in range(self.steps):
            self.got(s, f)
            for way in range(2):

                @pl.when(self.line.sends(way, s))
                def _():
                    for c in self.z(way, s, self.line.sent_from(way, s)):
                        c.wait_send()


def attn_fwd_kernel(docs, heads, seq, dest, len_ref, x_hbm, wt_ref, taps_ref, ow_ref, up_ref, dn_ref,
                    qkv_hbm, ctx_ref, lq_hbm, lk_hbm, sum_hbm, mix_hbm, k2_hbm, z_hbm, p_hbm, l1_ref, l3_ref, wall_ref,
                    x_s, qkv_s, lq_s, lk_s, sum_s, mix_s, k2_s, z_s, p_s, ctx_s, taps_s, lsem, asem, zsem, psem):
    width = heads * HD
    me, dd = lax.axis_index("mp"), lax.axis_index("dp")
    local = Local(lsem)
    loads = [local.start(x_hbm.at[d], x_s.at[d]) for d in range(docs)]
    local.open = []
    greet([{"mp": partner(me, m)} for m in range(1, dest)] + [{"dp": flip(dd, b)} for b in (1, 2, 4)])
    gather = Gather(dest, (ow_ref, up_ref, dn_ref), wall_ref, zsem, psem)
    gather.send(0)

    def a_copy(m, d):
        return rcopy(ctx_s.at[partner(me, m), d], ctx_ref.at[me, d], asem.at[0, m - 1, d], asem.at[1, m - 1, d], {"mp": partner(me, m)})

    taps_s[...] = jnp.zeros_like(taps_s)
    taps_s[:, TAP0 : TAP0 + KSIZE] = taps_ref[...]
    mask = block_mask(width)
    eye = identity(width)
    for c in loads:
        c.wait()

    def project(i, _):
        d, c = i // (seq // BLK), lax.rem(i, seq // BLK)
        rows = pl.ds(pl.multiple_of(c * BLK, BLK), BLK)
        qkv_s[d, :, rows] = nt(wt_ref[...], x_s[d, rows, :]).astype(BF)
        return 0

    lax.fori_loop(0, docs * (seq // BLK), project, 0)
    local.start(qkv_s, qkv_hbm)

    def landmarks(d, _):
        length = len_ref[d]
        memb = jnp.where(members(length, seq), 1.0, 0.0).astype(F32)
        counts = jnp.maximum(jnp.sum(memb, axis=1, keepdims=True), 1.0)
        memb_b = memb.astype(BF)
        q = qkv_s[d, 0:width, :]
        k = qkv_s[d, width : 2 * width, :]
        v = qkv_s[d, 2 * width : 3 * width, :]
        lq = spread(nt(memb_b, q) / counts, heads, mask).astype(BF)
        lk = spread(nt(memb_b, k) / counts, heads, mask).astype(BF)
        lq_s[d] = lq
        lk_s[d] = lk
        s2 = jnp.where(mask, nt(lq, lk) * SCALE, -1e30)
        e2 = jnp.where(mask, jnp.exp(s2 - jnp.max(s2, axis=1, keepdims=True)), 0.0)
        k2_s[d] = e2 / jnp.sum(e2, axis=1, keepdims=True)
        s3 = jnp.where(live_lanes(length, seq), nn(lq, k) * SCALE, -1e30)
        m3 = jnp.max(s3, axis=1, keepdims=True)
        e3 = jnp.exp(s3 - m3)
        t3 = jnp.sum(e3, axis=1, keepdims=True)
        l3_ref[d] = jnp.broadcast_to(m3 + jnp.log(t3), (width, 128))
        k3 = (e3 / t3).astype(BF)
        sum_s[d] = jnp.where(mask, nt(k3, v), 0.0)
        at(d, {0: lambda: gather.step1(0)})
        return 0

    lax.fori_loop(0, docs, landmarks, 0)
    for src, dst in ((lq_s, lq_hbm), (lk_s, lk_hbm), (k2_s, k2_hbm), (sum_s, sum_hbm)):
        local.start(src, dst)
    for d in range(docs):
        k2 = k2_s[d]
        z_s[d, 0] = k2.T / per_head_total(jnp.sum(k2 * k2, axis=1, keepdims=True), heads)

    def newton(i, _):
        k2s = [k2_s[d] for d in range(docs)]
        zs = [z_s[d, i] for d in range(docs)]
        ps = [nn(k2s[d], zs[d], HI) for d in range(docs)]
        bs = [15.0 * eye - nn(ps[d], 7.0 * eye - ps[d], HI) for d in range(docs)]
        cs = [13.0 * eye - nn(ps[d], bs[d], HI) for d in range(docs)]
        zs = [0.25 * nn(zs[d], cs[d], HI) for d in range(docs)]
        for d in range(docs):
            p_s[d, i, 0] = ps[d]
            p_s[d, i, 1] = bs[d]
            p_s[d, i, 2] = cs[d]
            z_s[d, i + 1] = zs[d]
        at(i, {1: lambda: gather.step1(1), 2: lambda: gather.step2(0), 3: lambda: (gather.step3(0), gather.step1(2)), 4: lambda: gather.step2(1), 5: lambda: gather.step3(1)})
        return 0

    lax.fori_loop(0, NS_ITERS, newton, 0)
    local.start(z_s, z_hbm)
    local.start(p_s, p_hbm)
    part = seq // dest

    def contexts(d, _):
        length = len_ref[d]
        q = qkv_s[d, 0:width, :]
        v = qkv_s[d, 2 * width : 3 * width, :]
        live = live_lanes(length, seq)
        mix = jnp.where(mask, nn(z_s[d, NS_ITERS], sum_s[d], HI), 0.0)
        mix_s[d] = mix.astype(BF)
        s1 = (nn(lk_s[d], q) * SCALE).reshape(heads, LM, seq)
        m1 = jnp.max(s1, axis=1, keepdims=True)
        e1 = jnp.exp(s1 - m1)
        t1 = jnp.sum(e1, axis=1, keepdims=True)
        l1_ref[d] = (m1 + jnp.log(t1)).reshape(heads, seq)
        k1 = (e1 / t1).reshape(width, seq).astype(BF)
        vl = jnp.where(live, v, 0).astype(BF)
        ctx = nn(mix.T.astype(BF), k1) + banded(vl, taps_s[...], heads, seq)
        ctx = jnp.where(live, ctx, 0.0).astype(BF)
        for i in range(dest):
            ctx_s[i, d] = ctx[:, i * part : (i + 1) * part]
        for m in range(1, dest):
            a_copy(m, d).start()
        ctx_ref[me, d] = ctx_s[me, d]
        at(d, {0: lambda: gather.step2(2)})
        return 0

    lax.fori_loop(0, docs, contexts, 0)
    local.start(mix_s, mix_hbm)
    gather.step3(2)
    gather.finish()
    for d in range(docs):
        for m in range(1, dest):
            a_copy(m, d).wait()
    local.finish()


def attn_fwd(lengths, x, wt, taps, ow, up, dn, dest):
    docs, seq, dim = x.shape
    width = wt.shape[0] // 3
    heads = width // HD
    sds = jax.ShapeDtypeStruct
    kept = [
        sds((docs, 3 * width, seq), BF),
        sds((docs, width, width), BF),
        sds((docs, width, width), BF),
        sds((docs, width, width), F32),
        sds((docs, width, width), BF),
        sds((docs, width, width), F32),
        sds((docs, NS_ITERS + 1, width, width), F32),
        sds((docs, NS_ITERS, 3, width, width), F32),
    ]
    out = [kept[0], sds((dest, docs, width, seq // dest), BF)] + kept[1:] + [
        sds((docs, heads, seq), F32),
        sds((docs, width, 128), F32),
        sds((dest, SLOTS, SLICE, dim), BF),
    ]
    return pl.pallas_call(
        functools.partial(attn_fwd_kernel, docs, heads, seq, dest),
        out_shape=out,
        in_specs=[SM, ANY, VM, VM, ANY, ANY, ANY],
        out_specs=[ANY, VM] + [ANY] * 7 + [VM, VM, ANY],
        scratch_shapes=[pltpu.VMEM((docs, seq, dim), BF)]
        + [pltpu.VMEM(t.shape, t.dtype) for t in kept]
        + [
            pltpu.VMEM((dest, docs, width, seq // dest), BF),
            pltpu.VMEM((heads, WIN), F32),
            DMA((16,)),
            DMA((2, dest - 1, docs)),
            DMA((2, 2, dest - 1, 3)),
            DMA((2, 2, dest - 1, 8)),
        ],
        compiler_params=pltpu.CompilerParams(vmem_limit_bytes=60 * 2**20, collective_id=0, has_side_effects=True),
        cost_estimate=pl.CostEstimate(flops=int(8e9), bytes_accessed=int(3e7), transcendentals=0),
        name="attn_fwd",
    )(lengths, x, wt, taps, ow, up, dn)


def ln_stats(v):
    mu = jnp.mean(v, axis=-1, keepdims=True)
    cen = v - mu
    var = jnp.mean(cen * cen, axis=-1, keepdims=True)
    r = lax.rsqrt(var + EPS)
    return cen * r, r


def ln_back(g, xhat, r):
    m1 = jnp.mean(g, axis=-1, keepdims=True)
    m2 = jnp.mean(g * xhat, axis=-1, keepdims=True)
    return r * (g - m1 - xhat * m2)


class Spread:
    def __init__(self, parts, buf, sem):
        self.line, self.buf, self.sem = Line(parts), buf, sem

    def one(self, way, s, d, origin, src=None):
        dst = self.buf.at[d, origin]
        return rcopy(dst if src is None else src, dst, self.sem.at[way, 0, s, d], self.sem.at[way, 1, s, d], self.line.ahead(way))

    def start(self, s, d, src=None):
        for way in range(2):

            @pl.when(self.line.sends(way, s))
            def _():
                self.one(way, s, d, self.line.sent_from(way, s), src).start()

    def wait(self, s, d):
        for way in range(2):

            @pl.when(self.line.gets(way, s))
            def _():
                self.one(way, s, d, self.line.got_from(way, s)).wait_recv()

    def sent(self, s, d, src=None):
        for way in range(2):

            @pl.when(self.line.sends(way, s))
            def _():
                self.one(way, s, d, self.line.sent_from(way, s), src).wait_send()


def ffn_kernel(groups, docs, rows, len_ref, x_hbm, cot_hbm, ctx_ref, ow_hbm, up_hbm, dn_hbm, wall_hbm, g1_ref, b1_ref, g2_ref, b2_ref,
               out_hbm, gmix_ref, gctx_ref, s1_hbm, small_ref,
               x_s, cot_s, w_s, rc_s, gc_s, nb_s, fac_s, act_s, gp_s, br_s, x1_s, gn_s, ga_s, o_s, s1_s, lsem, csem, osem, asem):
    n = docs * rows
    dim = x_s.shape[-1]
    z, dd = lax.axis_index("mp"), lax.axis_index("dp")
    kk = lax.rem(dd, 2)
    local = Local(lsem)
    mine = pl.ds(pl.multiple_of(z * rows, rows), rows)
    others = [partner(z, m) for m in range(1, groups)]
    heads_first = [local.start(ow_hbm, w_s.at[z, :, :, pl.ds(*PARTS[0])])]
    heads_first += [local.start(wall_hbm.at[g, :, :, pl.ds(*PARTS[0])], w_s.at[g, :, :, pl.ds(*PARTS[0])]) for g in others]
    heads_first += [local.start(x_hbm.at[d, mine], x_s.at[pl.ds(d * rows, rows)]) for d in range(docs)]
    rest = [local.start(up_hbm, w_s.at[z, :, :, pl.ds(*PARTS[1])]), local.start(dn_hbm, w_s.at[z, :, :, pl.ds(*PARTS[2])])]
    body = pl.ds(OW_ROWS, SLICE - OW_ROWS)
    rest += [local.start(wall_hbm.at[g, :, :, body], w_s.at[g, :, :, body]) for g in others]
    rest += [local.start(cot_hbm.at[d, mine], cot_s.at[pl.ds(d * rows, rows)]) for d in range(docs)]
    local.open = []
    greet([{"mp": partner(z, m)} for m in range(1, groups)] + [{"dp": flip(dd, 1)}])

    def back_copy(m, d):
        return rcopy(gc_s.at[m - 1, d], gctx_ref.at[z, d], asem.at[0, m - 1, d], asem.at[1, m - 1, d], {"mp": partner(z, m)})

    spread_out = Spread(groups, out_hbm, osem)

    def core_copy(g, part):
        lo, size = ((OW_ROWS, SLICE - OW_ROWS), (0, OW_ROWS))[part]
        return rcopy(w_s.at[g, :, 1 - kk, pl.ds(lo, size)], rc_s.at[g, :, pl.ds(lo, size)], csem.at[0, g, part], csem.at[1, g, part], {"dp": flip(dd, 1)})

    def take(g, part):
        lo, size = PARTS[part]
        return w_s[g, :, :, lo : lo + size, :].reshape(SLOTS * size, dim)

    def put(g, part, val):
        lo, size = PARTS[part]
        w_s[g, :, :, lo : lo + size, :] = val.astype(BF).reshape(SLOTS // 2, 2, size, dim)

    first = z * rows
    gain1, bias1 = g1_ref[...].reshape(1, dim), b1_ref[...].reshape(1, dim)
    gain2, bias2 = g2_ref[...].reshape(1, dim), b2_ref[...].reshape(1, dim)
    for c in heads_first:
        c.wait()
    small_ref[...] = jnp.zeros_like(small_ref)

    def doc(d, _):
        here = pl.ds(pl.multiple_of(d * rows, rows), rows)
        live = (lax.broadcasted_iota(jnp.int32, (rows, 1), 0) + first < len_ref[d]).astype(F32)
        mixed = x_s[here].astype(F32)
        for g in range(groups):
            mixed = mixed + tn(ctx_ref[g, d], take(g, 0)).astype(BF).astype(F32)
        xh1, r1 = ln_stats(mixed)
        x1_s[...] = xh1
        normed = xh1 * gain1 + bias1
        nb_s[here] = normed.astype(BF)
        br_s[...] = normed

        @pl.when(d == 0)
        def _():
            for c in rest:
                c.wait()

        def fwd_group(g, _):
            h = nn(nb_s[here], take(g, 1))
            phi_big = 0.5 * (1.0 + lax.erf(h * ROOT_HALF))
            act = (h * phi_big).astype(BF)
            act_s[g, here] = act
            fac_s[g] = phi_big + h * (jnp.exp(-0.5 * h * h) * INV_ROOT_2PI)
            br_s[...] += nn(act, take(g, 2)).astype(BF).astype(F32)
            return 0

        lax.fori_loop(0, groups, fwd_group, 0)
        xh2, r2 = ln_stats(br_s[...])
        o_s[d] = (live * (xh2 * gain2 + bias2)).astype(BF)

        @pl.when(d == 0)
        def _():
            spread_out.start(0, 0, o_s.at[0])

        g_out = live * cot_s[here].astype(F32)
        gg2 = jnp.sum(g_out * xh2, axis=0, keepdims=True)
        gb2 = jnp.sum(g_out, axis=0, keepdims=True)
        g_res = ln_back(g_out * gain2, xh2, r2)
        gn_s[...] = g_res
        gbr_s[here] = g_res.astype(BF)

        def back_group(g, _):
            g_pre = (nt(gbr_s[here], take(g, 2)) * fac_s[g]).astype(BF)
            gp_s[g, here] = g_pre
            gn_s[...] += nt(g_pre, take(g, 1))
            return 0

        lax.fori_loop(0, groups, back_group, 0)
        g_n = gn_s[...]
        xh1 = x1_s[...]
        gg1 = jnp.sum(g_n * xh1, axis=0, keepdims=True)
        gb1 = jnp.sum(g_n, axis=0, keepdims=True)
        small_ref[...] += jnp.concatenate([gg1, gb1, gg2, gb2, jnp.zeros((4, dim), F32)], axis=0)
        g_mix = ln_back(g_n * gain1, xh1, r1)
        gmix_ref[d] = g_mix
        g_att = g_mix.astype(BF)
        ga_s[here] = g_att
        for m in reversed(range(groups)):
            t = nt(take(partner(z, m), 0), g_att).astype(BF)
            if m:
                gc_s[m - 1, d] = t
                back_copy(m, d).start()
            else:
                gctx_ref[z, d] = t
        return 0

    gbr_s = cot_s
    lax.fori_loop(0, docs, doc, 0)
    for d in range(docs):
        local.start(o_s.at[d], out_hbm.at[d, z])

    def weight_group(g, _):
        put(g, 2, tn(act_s[g], gbr_s[...]))
        put(g, 1, tn(nb_s[...], gp_s[g]))
        core_copy(g, 0).start()
        return 0

    lax.fori_loop(0, groups, weight_group, 0)
    for g in range(groups):
        acc = None
        for d in range(docs):
            t = nn(ctx_ref[g, d], ga_s[d * rows : (d + 1) * rows])
            acc = t if acc is None else acc + t
        put(g, 0, acc)
        core_copy(g, 1).start()

    def add_group(g, _):
        core_copy(g, 0).wait_recv()
        core_copy(g, 1).wait_recv()

        def add_slot(j, _):
            s1_s[g, j // 2, j % 2] = (w_s[g, j, kk].astype(F32) + rc_s[g, j].astype(F32)).astype(BF)
            return 0

        lax.fori_loop(0, SLOTS // 2, add_slot, 0)
        return 0

    lax.fori_loop(0, groups, add_group, 0)
    local.start(s1_s, s1_hbm)
    for m in range(1, groups):
        for d in range(docs):
            back_copy(m, d).wait()
    spread_out.wait(0, 0)
    spread_out.sent(0, 0, o_s.at[0])
    for g in range(groups):
        for part in range(2):
            core_copy(g, part).wait_send()
    local.finish()


def ffn(lengths, x, cot, ctx, ow, up, dn, wall, g1, b1, g2, b2):
    docs, seq, dim = x.shape
    groups, _, width, rows = ctx.shape
    ff = SLOTS * UP_ROWS
    n = docs * rows
    sds = jax.ShapeDtypeStruct
    out = [
        sds((docs, groups, rows, dim), BF),
        sds((docs, rows, dim), F32),
        sds((groups, docs, width, rows), BF),
        sds((groups, 2, 2, SLICE, dim), BF),
        sds((8, dim), F32),
    ]
    wall = wall.reshape(groups, SLOTS // 2, 2, SLICE, dim)
    ow, up, dn = (t.reshape(SLOTS // 2, 2, -1, dim) for t in (ow, up, dn))
    return pl.pallas_call(
        functools.partial(ffn_kernel, groups, docs, rows),
        out_shape=out,
        in_specs=[SM, ANY, ANY, VM, ANY, ANY, ANY, ANY, VM, VM, VM, VM],
        out_specs=[ANY, VM, VM, ANY, VM],
        scratch_shapes=[
            pltpu.VMEM((n, dim), BF),
            pltpu.VMEM((n, dim), BF),
            pltpu.VMEM((groups, SLOTS // 2, 2, SLICE, dim), BF),
            pltpu.VMEM((groups, SLOTS // 2, SLICE, dim), BF),
            pltpu.VMEM((groups - 1, docs, width, rows), BF),
            pltpu.VMEM((n, dim), BF),
            pltpu.VMEM((groups, rows, ff), F32),
            pltpu.VMEM((groups, n, ff), BF),
            pltpu.VMEM((groups, n, ff), BF),
            pltpu.VMEM((rows, dim), F32),
            pltpu.VMEM((rows, dim), F32),
            pltpu.VMEM((rows, dim), F32),
            pltpu.VMEM((n, dim), BF),
            pltpu.VMEM((docs, rows, dim), BF),
            pltpu.VMEM((groups, 2, 2, SLICE, dim), BF),
            DMA((24,)),
            DMA((2, groups, 2)),
            DMA((2, 2, groups - 1, docs)),
            DMA((2, groups - 1, docs)),
        ],
        compiler_params=pltpu.CompilerParams(vmem_limit_bytes=62 * 2**20, collective_id=1, has_side_effects=True),
        cost_estimate=pl.CostEstimate(flops=int(1.8e10), bytes_accessed=int(4e7), transcendentals=0),
        name="ffn",
    )(lengths, x, cot, ctx, ow, up, dn, wall, g1, b1, g2, b2)


def attn_bwd_kernel(docs, heads, seq, parts, dp, len_ref, x_hbm, wt_ref, taps_ref, qkv_ref, gctx_ref, lq_ref, lk_ref, sum_ref, mix_ref, k2_ref,
                    z_hbm, p_hbm, l1_ref, l3_ref, s1, small_in, gmix_hbm, out_in, gq, ig, taps_out, gw, small, out_hbm,
                    x_s, z_s, p_s, gmix_s, g_s, gs1_s, gs3_s, ginv_s, glq_s, glk_s, gz_s, gk_s, taps_s, gacc_s,
                    ipart, ri, ra1, rb1, rz, fin, rfin, rq0, rq1, rq2, gqb, q, rsm, rtp, lsem, ssem, rsem, isem, osem, pz, acc, gsem):
    width = heads * HD
    nblk = seq // BLK
    dim = x_s.shape[-1]
    zi = lax.axis_index("mp")
    local = Local(lsem)
    loads = [local.start(a, b) for a, b in ((z_hbm, z_s), (p_hbm, p_s), (x_hbm, x_s), (gmix_hbm, gmix_s))]
    local.open = []
    nd = Sums(docs, seq, parts, dp, locals())
    nd.begin()
    out = Spread(parts, out_hbm, osem)
    left = [(s, d) for s in range(parts - 1) for d in range(docs) if (s, d) != (0, 0)]
    waves = [[(0, d) for d in range(1, docs)] + [(1, 0)]]
    waves += [[(s, d) for d in range(1, docs)] + [(s + 1, 0)] for s in range(1, parts - 2)] + [[(parts - 2, d) for d in range(1, docs)]]

    def out_step(i):
        for s, d in waves[i] if i < len(waves) else ():
            if s > 0 and (s - 1, d) != (0, 0):
                out.wait(s - 1, d)
            out.start(s, d)

    out_step(0)
    taps_s[...] = jnp.zeros_like(taps_s)
    taps_s[:, TAP0 : TAP0 + KSIZE] = taps_ref[...]
    mask = block_mask(width)
    eye = identity(width)
    anti = jnp.where(
        lax.broadcasted_iota(jnp.int32, (BLK, BLK), 0) + lax.broadcasted_iota(jnp.int32, (BLK, BLK), 1) == BLK - 1, 1.0, 0.0
    ).astype(BF)
    gacc_s[...] = jnp.zeros_like(gacc_s)

    def doc(d, _):
        length = len_ref[d]
        live = live_lanes(length, seq)
        q_ = qkv_ref[d, 0:width, :]
        k = qkv_ref[d, width : 2 * width, :]
        v = qkv_ref[d, 2 * width : 3 * width, :]
        gc = jnp.concatenate([gctx_ref[i, d] for i in range(parts)], axis=1)
        gc = jnp.where(live, gc, 0).astype(BF)
        lq, lk = lq_ref[d], lk_ref[d]
        s1_ = (nn(lk, q_) * SCALE).reshape(heads, LM, seq)
        k1 = jnp.exp(s1_ - l1_ref[d].reshape(heads, 1, seq))
        gmixing = jnp.where(mask, nt(k1.reshape(width, seq).astype(BF), gc), 0.0)
        gk1 = nn(mix_ref[d], gc).reshape(heads, LM, seq)
        gs1 = (k1 * (gk1 - jnp.sum(gk1 * k1, axis=1, keepdims=True))).reshape(width, seq).astype(BF)
        gz_s[d] = nt(gmixing, sum_ref[d], HI)
        gk_s[d] = jnp.zeros((width, width), F32)
        gsum = jnp.where(mask, tn(ginv_s[d], gmixing, HI), 0.0)
        gsum_b = gsum.astype(BF)
        s3 = jnp.where(live, nn(lq, k) * SCALE, -1e30)
        k3 = jnp.exp(s3 - l3_ref[d][:, 0:1])
        gk3 = nn(gsum_b, v)
        gs3 = (k3 * (gk3 - jnp.sum(gk3 * k3, axis=1, keepdims=True))).astype(BF)
        glq_s[d] = jnp.where(mask, nt(gs3, k), 0.0) * SCALE
        glk_s[d] = jnp.where(mask, nt(gs1, q_), 0.0) * SCALE
        gs1_s[d] = gs1
        gs3_s[d] = gs3
        gv = nn(gsum.T.astype(BF), k3.astype(BF))
        gvl = banded(gc, taps_s[...], heads, seq)
        g_s[d, 2 * width : 3 * width, :] = (gv + jnp.where(live, gvl, 0.0)).astype(BF)
        vl = jnp.where(live, v, 0).astype(BF)
        for h in range(heads):
            wins = windows(vl[h * HD : (h + 1) * HD], seq)
            gch = gc[h * HD : (h + 1) * HD]
            stack = jnp.concatenate([gch[:, b * BLK : (b + 1) * BLK] for b in range(nblk)], axis=0)
            gacc_s[h] += nn(nt(anti, stack).astype(BF), wins)
        at(d, {i: functools.partial(nd.small_step, 1 + i) for i in range(docs)})
        return 0

    loads[0].wait()
    for d in range(docs):
        ginv_s[d] = z_s[d, NS_ITERS]
    lax.fori_loop(0, docs, doc, 0)
    out_step(1)
    for h in range(heads):
        rolled = pltpu.roll(gacc_s[h], 0, 1, stride=1, stride_axis=0)
        taps_out[h : h + 1, :] = jnp.sum(rolled, axis=0, keepdims=True)
    loads[1].wait()

    def newton_back(j, _):
        i = NS_ITERS - 1 - j
        for d in range(docs):
            z, p, b, c = z_s[d, i], p_s[d, i, 0], p_s[d, i, 1], p_s[d, i, 2]
            a = 7.0 * eye - p
            g = 0.25 * gz_s[d]
            gc_ = tn(z, g, HI)
            gp = -nt(gc_, b, HI)
            gb = -tn(p, gc_, HI)
            gp = gp - nt(gb, a, HI)
            ga = -tn(p, gb, HI)
            gp = gp - ga
            gk_s[d] += nt(gp, z, HI)
            gz_s[d] = nt(g, c, HI) + tn(k2_ref[d], gp, HI)
        base = 1 + docs
        at(j, {
            1: lambda: (nd.small_step(base), nd.taps_step(0)),
            3: lambda: (nd.small_step(base + 1), nd.taps_step(1), nd.g_step1()),
            5: lambda: (nd.small_step(base + 2), nd.taps_step(2), out_step(2)),
        })
        return 0

    lax.fori_loop(0, NS_ITERS, newton_back, 0)
    for c in loads[2:]:
        c.wait()

    def finish(d, _):
        length = len_ref[d]
        k2 = k2_ref[d]
        tot = per_head_total(jnp.sum(k2 * k2, axis=1, keepdims=True), heads)
        g = gz_s[d]
        dot = per_head_total(jnp.sum(g * k2.T, axis=1, keepdims=True), heads)
        gk2 = gk_s[d] + (g / tot).T - k2 * (2.0 * dot / (tot * tot))
        gs2 = k2 * (gk2 - jnp.sum(gk2 * k2, axis=1, keepdims=True)) * SCALE
        memb = jnp.where(members(length, seq), 1.0, 0.0).astype(F32)
        counts = jnp.maximum(jnp.sum(memb, axis=1, keepdims=True), 1.0)
        counts = jnp.concatenate([counts] * heads, axis=0)
        memb3 = jnp.concatenate([memb.astype(BF)] * heads, axis=0)
        lq, lk = lq_ref[d].astype(F32), lk_ref[d].astype(F32)
        glq = (glq_s[d] + nn(gs2, lk, HI)) / counts
        glk = (glk_s[d] + tn(gs2, lq, HI)) / counts
        hi, lo = hi_lo(glq.T)
        gq_ = nn(lk.T.astype(BF), gs1_s[d]) * SCALE + nn(hi, memb3) + nn(lo, memb3)
        hi, lo = hi_lo(glk.T)
        gk_ = nn(lq.T.astype(BF), gs3_s[d]) * SCALE + nn(hi, memb3) + nn(lo, memb3)
        g_s[d, 0:width, :] = gq_.astype(BF)
        g_s[d, width : 2 * width, :] = gk_.astype(BF)

        def inputs(c, _):
            rows = pl.ds(pl.multiple_of(c * BLK, BLK), BLK)
            t = tn(g_s[d, :, rows], wt_ref[...])
            t = (t + jnp.where(zi == c, 1.0, 0.0) * gmix_s[d]).astype(BF)
            per = BLK // CHUNK
            ipart[d, pl.ds(c * per, per)] = t.reshape(per, CHUNK, dim)
            return 0

        lax.fori_loop(0, nblk, inputs, 0)
        return 0

    lax.fori_loop(0, docs, finish, 0)
    for i in range(3, len(waves)):
        out_step(i)
    nd.i_time(0)

    def weights(c, _):
        rows = pl.ds(pl.multiple_of(c * width, width), width)
        acc_q = nn(g_s[0, rows], x_s[0])
        for d in range(1, docs):
            acc_q = acc_q + nn(g_s[d, rows], x_s[d])
        gqb[rows] = acc_q.astype(BF)
        return 0

    lax.fori_loop(0, 3, weights, 0)
    nd.tail()
    for s, d in left:
        if s == parts - 2:
            out.wait(s, d)
    for s, d in left:
        out.sent(s, d)


class Sums:
    def __init__(self, docs, seq, parts, dp, refs):
        for name in ("pz", "acc", "gsem", "s1", "small_in", "gq", "ig", "taps_out", "gw", "small", "ipart", "ri", "ra1", "rb1", "rz", "fin", "rfin", "rq0", "rq1", "rq2", "gqb", "q", "rsm", "rtp", "ssem", "rsem", "isem"):
            setattr(self, name, refs[name])
        self.docs, self.parts = docs, parts
        self.z, self.d = lax.axis_index("mp"), lax.axis_index("dp")
        self.r = lax.rem(self.d, SLOTS)
        self.y, self.x, self.k = self.r // 4, lax.rem(self.r // 2, 2), lax.rem(self.r, 2)
        self.net = Net(self.ssem, self.rsem)
        self.extra = [b for b in (8, 16, 32, 64, 128) if b < dp]
        self.bits = [1, 2, 4] + self.extra

    def dev(self, bit):
        return {"dp": flip(self.d, bit)}

    def zdev(self, m):
        return {"mp": partner(self.z, m)}

    def begin(self):
        greet([self.zdev(m) for m in range(1, self.parts)] + [self.dev(b) for b in self.bits])
        self.i_setup()
        self.line = Line(self.parts)
        c = self.net.copy
        low, high = pl.ds(0, GCUT), pl.ds(GCUT, SLICE - GCUT)
        self.a1 = c(self.s1.at[:, 1 - self.y, :, low], self.ra1, self.dev(4))
        self.b1 = c(self.s1.at[:, :, 1 - self.x, high], self.rb1, self.dev(2))
        self.a1.start()
        self.b1.start()
        self.a2 = c(self.ra1.at[:, 1 - self.x], self.pz.at[:, low], self.dev(2))
        self.b2 = c(self.rb1.at[:, 1 - self.y], self.pz.at[:, high], self.dev(4))
        r, gw = self.r, self.gw
        r4, r2, r6 = flip(r, 4), flip(r, 2), partner(r, 6)
        self.gy = c(gw.at[r], gw.at[r], self.dev(4))
        self.gx = c(gw.at[r], gw.at[r], self.dev(2))
        self.gyx = c(gw.at[r4, low], gw.at[r4, low], self.dev(2))
        self.gxy = c(gw.at[r2, high], gw.at[r2, high], self.dev(4))
        self.gc = [c(gw.at[i], gw.at[i], self.dev(1)) for i in (r, r4, r2, r6)]
        h = self.gqb.shape[0] // 2
        self.half = h
        mine, other = (pl.ds(pl.multiple_of(k * h, 8), h) for k in (self.k, 1 - self.k))
        self.mine = mine
        self.q0 = c(self.gqb.at[other], self.rq0, self.dev(1))
        self.qa = self.q_pair(self.rq1, 4, 2)
        self.qb = self.q_pair(self.rq2.at[0], 2, 4)
        self.qc = c(self.gq.at[mine], self.gq.at[mine], self.dev(1))
        self.extras = [(c(self.fin, self.rfin.at[i], self.dev(b), late=False), c(self.q, self.rq2.at[1 + i], self.dev(b), late=False)) for i, b in enumerate(self.extra)]
        self.small[...] = self.small_in[...]
        zs = [self.zdev(1 << j) for j in range(self.parts.bit_length() - 1)]
        self.smalls = [c(self.small, self.rsm.at[i], dev, late=False) for i, dev in enumerate([self.dev(b) for b in self.bits] + zs)]
        self.tapsums = [c(self.taps_out, self.rtp.at[i], self.dev(b), late=False) for i, b in enumerate(self.bits)]
        self.small_step(0)

    def exchange(self, copies, buf, recv, i):
        if 0 < i <= len(copies):
            copies[i - 1].wait()
            buf[...] = buf[...] + recv[i - 1]
        if i < len(copies):
            copies[i].start()

    def small_step(self, i):
        self.exchange(self.smalls, self.small, self.rsm, i)

    def taps_step(self, i):
        self.exchange(self.tapsums, self.taps_out, self.rtp, i)

    def double(self, c, buf, recv):
        c.start()
        c.wait()
        buf[...] = (buf[...].astype(F32) + recv[...].astype(F32)).astype(buf.dtype)

    def g_step1(self):
        self.a1.wait_recv()
        self.b1.wait_recv()

        def add(i, _):
            g, j = i // 2, i % 2
            self.ra1[g, j] = (self.ra1[g, j].astype(F32) + self.s1[g, self.y, j, 0:GCUT].astype(F32)).astype(BF)
            self.rb1[g, j] = (self.rb1[g, j].astype(F32) + self.s1[g, j, self.x, GCUT:SLICE].astype(F32)).astype(BF)
            return 0

        lax.fori_loop(0, 2 * self.parts, add, 0)
        self.a2.start()
        self.b2.start()

    def g_step2(self):
        self.a2.wait_recv()
        self.b2.wait_recv()

        def add(g, _):
            self.pz[g, 0:GCUT] = (self.pz[g, 0:GCUT].astype(F32) + self.ra1[g, self.x].astype(F32)).astype(BF)
            self.pz[g, GCUT:SLICE] = (self.pz[g, GCUT:SLICE].astype(F32) + self.rb1[g, self.y].astype(F32)).astype(BF)
            return 0

        lax.fori_loop(0, self.parts, add, 0)
        self.z_hop(0)

    def z_piece(self, way, s):
        last = self.parts - 1
        g = last - s + self.z if way == 0 else s - last + self.z
        return g, (self.z <= s) & (self.z < last) if way == 0 else (last - self.z <= s) & (self.z > 0)

    def z_copy(self, way, s, g):
        return rcopy(self.pz.at[g], self.rz.at[way, s], self.gsem.at[0, way, s], self.gsem.at[1, way, s], self.line.ahead(way))

    def z_hop(self, s):
        last = self.parts - 1
        for way in range(2):
            g, ok = self.z_piece(way, s)
            inner = self.z > 0 if way == 0 else self.z < last

            if s > 0:

                @pl.when(ok & inner)
                def _():
                    self.z_copy(way, s - 1, 0).wait_recv()
                    self.pz[g] = (self.pz[g].astype(F32) + self.rz[way, s - 1].astype(F32)).astype(BF)

            @pl.when(ok)
            def _():
                self.z_copy(way, s, g).start()

    def z_done(self):
        last = self.parts - 1
        for way in range(2):
            for s in range(last):
                g, ok = self.z_piece(way, s)

                @pl.when(ok)
                def _():
                    self.z_copy(way, s, g).wait_send()

    def g_step3(self):
        last = self.parts - 1
        self.acc[...] = self.pz[self.z].astype(F32)
        for way in range(2):

            @pl.when(self.z > 0 if way == 0 else self.z < last)
            def _():
                self.z_copy(way, last - 1, 0).wait_recv()
                self.acc[...] += self.rz[way, last - 1].astype(F32)

        self.fin[...] = self.acc[...].astype(BF)
        for i, (c, _) in enumerate(self.extras):
            self.double(c, self.fin, self.rfin.at[i])
        self.gw[self.r] = self.fin[...]
        self.gy.start()
        self.gx.start()
        self.gc[0].start()

    def g_step4(self):
        self.gy.wait_recv()
        self.gyx.start()
        self.gc[1].start()
        self.gx.wait_recv()
        self.gxy.start()
        self.gc[2].start()

    def g_step5(self):
        self.gyx.wait_recv()
        self.gxy.wait_recv()
        self.gc[3].start()
        for s in self.gc:
            s.wait_recv()

    def q_pair(self, recv, a, b):
        h = self.half // 2
        return [
            self.net.copy(self.q.at[pl.ds(0, h)], recv.at[pl.ds(0, h)], self.dev(a), late=False),
            self.net.copy(self.q.at[pl.ds(h, h)], recv.at[pl.ds(h, h)], self.dev(b), late=False),
        ]

    def q_step0(self):
        self.q0.start()

    def q_step1(self):
        self.q0.wait_recv()
        self.q[...] = (self.gqb[self.mine].astype(F32) + self.rq0[...].astype(F32)).astype(BF)
        for s in self.qa:
            s.start()

    def q_step2(self):
        for s in self.qa:
            s.wait()
        self.q[...] = (self.q[...].astype(F32) + self.rq1[...].astype(F32)).astype(BF)
        for s in self.qb:
            s.start()

    def q_step3(self):
        for s in self.qb:
            s.wait()
        self.q[...] = (self.q[...].astype(F32) + self.rq2[0].astype(F32)).astype(BF)
        for i, (_, c) in enumerate(self.extras):
            self.double(c, self.q, self.rq2.at[1 + i])
        self.gq[self.mine] = self.q[...]
        self.qc.start()

    def i_setup(self):
        last = self.parts - 1
        self.chunks = self.ipart.shape[1]
        self.pos, self.lower, self.upper = [], [], []
        for d in range(self.docs):
            step = 1 if d % 2 == 0 else -1
            self.pos.append(self.z if d % 2 == 0 else last - self.z)
            self.lower.append({"mp": lax.rem(self.z - step + self.parts, self.parts)})
            self.upper.append({"mp": lax.rem(self.z + step + self.parts, self.parts)})

    def red(self, d, c):
        return rcopy(self.ipart.at[d, c], self.ri.at[d, c], self.isem.at[0, d, c], self.isem.at[1, d, c], self.lower[d])

    def bc(self, d, c):
        return rcopy(self.ig.at[d, c], self.ig.at[d, c], self.isem.at[2, d, c], self.isem.at[3, d, c], self.upper[d])

    def i_time(self, t):
        last = self.parts - 1
        for d in range(self.docs):
            p = self.pos[d]
            c = t - last + p
            ok = (c >= 0) & (c < self.chunks)

            @pl.when(ok & (p < last))
            def _():
                self.red(d, c).wait_recv()
                self.ipart[d, c] = (self.ipart[d, c].astype(F32) + self.ri[d, c].astype(F32)).astype(BF)

            @pl.when(ok & (p > 0))
            def _():
                self.red(d, c).start()

            @pl.when(ok & (p == 0))
            def _():
                self.ig[d, c] = self.ipart[d, c]
                self.bc(d, c).start()

        for d in range(self.docs):
            p = self.pos[d]
            c = t - last - p
            ok = (c >= 0) & (c < self.chunks) & (p > 0)

            @pl.when(ok)
            def _():
                self.bc(d, c).wait_recv()

            @pl.when(ok & (p < last))
            def _():
                self.bc(d, c).start()

    def i_end(self):
        last = self.parts - 1
        for d in range(self.docs):
            p = self.pos[d]

            def sent(c, _, d=d):
                self.red(d, c).wait_send()
                return 0

            def back(c, _, d=d):
                self.bc(d, c).wait_send()
                return 0

            @pl.when(p > 0)
            def _():
                lax.fori_loop(0, self.chunks, sent, 0)

            @pl.when(p < last)
            def _():
                lax.fori_loop(0, self.chunks, back, 0)

    def tail(self):
        done = 3 + self.docs
        rest = [functools.partial(self.small_step, i) for i in range(done + 1, len(self.smalls) + 1)]
        rest += [functools.partial(self.taps_step, i) for i in range(3, len(self.tapsums) + 1)]

        def run(*fs):
            def go():
                for f in fs:
                    f()

            return go

        todo = {
            1: run(self.g_step2),
            2: run(self.q_step1),
            3: run(lambda: self.z_hop(1)),
            4: run(self.q_step2),
            5: run(lambda: self.z_hop(2)),
            6: run(self.q_step3, *rest),
            8: run(self.g_step3),
            10: run(self.g_step4),
            12: run(self.g_step5),
        }
        self.q_step0()

        def step(t, _):
            self.i_time(t)
            at(t, todo)
            return 0

        lax.fori_loop(1, self.chunks + 2 * (self.parts - 1), step, 0)
        self.qc.wait_recv()
        self.i_end()
        self.z_done()
        self.net.drain()


def attn_bwd(dp, lengths, x, wt, taps, qkv, gctx, lq, lk, sm, mix, k2, z, p, l1, l3, s1, small, gmix, out_rows):
    docs, seq, dim = x.shape
    width = wt.shape[0] // 3
    heads = width // HD
    parts = gctx.shape[0]
    nchunk = seq // CHUNK
    more = max(1, dp.bit_length() - 4)
    steps = dp.bit_length() + parts.bit_length()
    sds = jax.ShapeDtypeStruct
    vmem = pltpu.VMEM
    out = [
        sds((3 * width, dim), BF),
        sds((docs, nchunk, CHUNK, dim), BF),
        sds((heads, WIN), F32),
        sds((SLOTS, SLICE, dim), BF),
        sds((8, dim), F32),
        sds(out_rows.shape, BF),
    ]
    h = 3 * width // 2
    sq = (docs, width, width)
    return pl.pallas_call(
        functools.partial(attn_bwd_kernel, docs, heads, seq, parts, dp),
        out_shape=out,
        in_specs=[SM, ANY, VM, VM, VM, VM, VM, VM, VM, VM, VM, ANY, ANY, VM, VM, VM, VM, ANY, ANY],
        out_specs=[VM] * 5 + [ANY],
        input_output_aliases={18: 5},
        scratch_shapes=[
            vmem(x.shape, BF),
            vmem(z.shape, F32),
            vmem(p.shape, F32),
            vmem(gmix.shape, F32),
            vmem((docs, 3 * width, seq), BF),
            vmem((docs, width, seq), BF),
            vmem((docs, width, seq), BF),
            vmem(sq, F32),
            vmem(sq, F32),
            vmem(sq, F32),
            vmem(sq, F32),
            vmem(sq, F32),
            vmem((heads, WIN), F32),
            vmem((heads, BLK, WIN), F32),
            vmem((docs, nchunk, CHUNK, dim), BF),
            vmem((docs, nchunk, CHUNK, dim), BF),
            vmem((parts, 2, GCUT, dim), BF),
            vmem((parts, 2, SLICE - GCUT, dim), BF),
            vmem((2, parts - 1, SLICE, dim), BF),
            vmem((SLICE, dim), BF),
            vmem((more, SLICE, dim), BF),
            vmem((h, dim), BF),
            vmem((h, dim), BF),
            vmem((1 + more, h, dim), BF),
            vmem((3 * width, dim), BF),
            vmem((h, dim), BF),
            vmem((steps, 8, dim), F32),
            vmem((steps, heads, WIN), F32),
            DMA((4,)),
            DMA((64,)),
            DMA((64,)),
            DMA((4, docs, nchunk)),
            DMA((2, 2, parts - 1, docs)),
            vmem((parts, SLICE, dim), BF),
            vmem((SLICE, dim), F32),
            DMA((2, 2, parts - 1)),
        ],
        compiler_params=pltpu.CompilerParams(vmem_limit_bytes=62 * 2**20, collective_id=2, has_side_effects=True),
        cost_estimate=pl.CostEstimate(flops=int(1.2e10), bytes_accessed=int(3e7), transcendentals=0),
        name="attn_bwd",
    )(lengths, x, wt, taps, qkv, gctx, lq, lk, sm, mix, k2, z, p, l1, l3, s1, small, gmix, out_rows)


def finish_kernel(gw_ref, gq_ref, ig_ref, out_ref, small_ref, taps_ref, ow_o, up_o, dn_o, q_o, ig_o, out_o, g1_o, b1_o, g2_o, b2_o, taps_o):
    for i, o in enumerate((ow_o, up_o, dn_o)):
        lo, size = PARTS[i]
        o[...] = gw_ref[0, lo : lo + size].astype(F32)
    q_o[...] = gq_ref[...].astype(F32)
    ig_o[...] = ig_ref[:, 0]
    out_o[...] = out_ref[...]

    @pl.when(pl.program_id(0) == 0)
    def _():
        for i, o in enumerate((g1_o, b1_o, g2_o, b2_o)):
            o[...] = small_ref[i]
        taps_o[...] = taps_ref[:, TAP_END : TAP_END + KSIZE]


def finish_up(gw, gq, ig, out_rows, small, taps):
    docs, nchunk, chunk, dim = ig.shape
    groups, rows = out_rows.shape[1:3]
    seq = nchunk * chunk
    heads = taps.shape[0]
    qrows = gq.shape[0] // SLOTS
    per = seq // SLOTS
    ratio = rows // per
    sds = jax.ShapeDtypeStruct
    whole = lambda shape: pl.BlockSpec(shape, lambda i: (0,) * len(shape))
    return pl.pallas_call(
        finish_kernel,
        grid=(SLOTS,),
        out_shape=[sds((SLOTS * t, dim), F32) for t in (OW_ROWS, UP_ROWS, DN_ROWS)]
        + [sds(gq.shape, F32), sds((docs, seq, dim), BF), sds((docs, seq, dim), BF)]
        + [sds((dim,), F32)] * 4
        + [sds((heads, KSIZE), F32)],
        in_specs=[
            pl.BlockSpec((1, SLICE, dim), lambda i: (i, 0, 0)),
            pl.BlockSpec((qrows, dim), lambda i: (i, 0)),
            pl.BlockSpec((docs, 1, chunk, dim), lambda i: (0, i, 0, 0)),
            pl.BlockSpec((docs, pl.Squeezed(), per, dim), lambda i: (0, i // ratio, i % ratio, 0)),
            whole(small.shape),
            whole(taps.shape),
        ],
        out_specs=[pl.BlockSpec((t, dim), lambda i: (i, 0)) for t in (OW_ROWS, UP_ROWS, DN_ROWS, qrows)]
        + [pl.BlockSpec((docs, per, dim), lambda i: (0, i, 0))] * 2
        + [whole((dim,))] * 4
        + [whole((heads, KSIZE))],
        compiler_params=pltpu.CompilerParams(vmem_limit_bytes=62 * 2**20),
        name="finish",
    )(gw, gq, ig, out_rows, small, taps)


def body_of(dp, mp):
    def body(tokens, lengths, qkv_weight, out_weight, conv_taps, norm1_gain, norm1_bias, norm2_gain, norm2_bias, up_weight, down_weight, cotangent):
        dim = tokens.shape[2]
        width = qkv_weight.shape[2]
        wt = jnp.transpose(qkv_weight, (0, 2, 1)).reshape(3 * width, dim)
        ow, up, dn = (t.reshape(SLOTS, -1, dim) for t in (out_weight, up_weight, down_weight))
        qkv, ctx, lq, lk, sm, mix, k2, z, p, l1, l3, wall = attn_fwd(lengths, tokens, wt, conv_taps, ow, up, dn, mp)
        out_rows, gmix, gctx, s1, small = ffn(lengths, tokens, cotangent, ctx, ow, up, dn, wall, norm1_gain, norm1_bias, norm2_gain, norm2_bias)
        gq, ig, gtaps, gw, small, out_rows = attn_bwd(
            dp, lengths, tokens, wt, conv_taps[:, ::-1], qkv, gctx, lq, lk, sm, mix, k2, z, p, l1, l3, s1, small, gmix, out_rows
        )
        g_ow, g_up, g_dn, gq, input_grad, output, g1, b1, g2, b2, g_taps = finish_up(gw, gq, ig, out_rows, small, gtaps)
        gqkv = jnp.transpose(gq.reshape(3, width, dim), (0, 2, 1))
        return output, input_grad, gqkv, g_ow, g_taps, g1, b1, g2, b2, g_up, g_dn

    return body


def solution(mesh):
    rep, rows = P(), P("mp", None)
    docs, cols, qkv = P("dp", None, None), P(None, "mp"), P(None, None, "mp")
    return jax.shard_map(
        body_of(mesh.shape["dp"], mesh.shape["mp"]),
        mesh=mesh,
        in_specs=(docs, P("dp"), qkv, rows, rows, rep, rep, rep, rep, cols, rows, docs),
        out_specs=(docs, docs, qkv, rows, rows, rep, rep, rep, rep, cols, rows),
        check_vma=False,
    )
```

time: 805 us -> 305 us (0.38); the launches traced: 794 us -> 303 us
  waiting for transfers between devices: 564 us -> 0 us
  Pallas kernels: 94.4 us -> 302 us
  blocking collectives: 59.8 us -> 0 us
  local copies, waits for them, and re-layouts: 33 us -> 0.67 us
  other arithmetic: 18.6 us -> 0 us
  between operations: 14.7 us -> 0.84 us
  starting transfers between devices: 8.78 us -> 0 us
    all_gather x3 -> x0, waiting for transfers between devices: 240 us -> none  [the longest x1 170 us: body(): w_all = lax.all_gather(w_all, 'mp', axis=0, tiled=False)]
    reduce_scatter x2 -> x0, waiting for transfers between devices: 228 us -> none  [the longest x1 179 us: body(): gw = lax.psum_scatter(gw, 'mp', scatter_dimension=0, tiled=False)]
    pallas_call x1, Pallas kernels: 39.6 us -> 183 us  [attn_bwd(): pl.pallas_call(functools.partial(attn_bwd_kernel, docs, heads, seq, parts...]
    psum x1 -> x0, waiting for transfers between devices: 76.7 us -> none  [body(): gqkv = lax.psum(gqkv.astype(BF), 'dp').astype(F32)]
    psum x2 -> x0, blocking collectives: 59.8 us -> none  [the longest x1 46.9 us: body(): small = lax.psum(small, ('dp', 'mp'))]
    pallas_call x1, Pallas kernels: 24 us -> 66.5 us  [attn_fwd(): pl.pallas_call(functools.partial(attn_fwd_kernel, docs, heads, seq, dest)...]
    all_to_all x2 -> x0, waiting for transfers between devices: 19.6 us -> none  [the longest x1 19.6 us: body(): gctx_heads = lax.all_to_all(gctx, 'mp', 0, 0, tiled=True)]
    slice x6 -> x0, local copies, waits for them, and re-layouts: 14 us -> none  [the longest x1 7.95 us: body(): w_all[:, width + ff:]]
  transfers between devices with their start and end apart: 8 -> 0, of which waited for: 7 -> 0; matrix products, arithmetic and copies ran while one was open for 4% -> 0% of each run, Pallas kernels for 3% -> 0%
where the time goes in v4:
time: 305 us; the launch traced here: 303 us
  Pallas kernels  302 us (99%)
    pallas_call x1, Pallas kernels, attn_bwd(): pl.pallas_call(functools.partial(attn_bwd_kernel, docs, heads, seq, parts...  183 us
    pallas_call x1, Pallas kernels, attn_fwd(): pl.pallas_call(functools.partial(attn_fwd_kernel, docs, heads, seq, dest)...  66.5 us
    pallas_call x1, Pallas kernels, ffn(): pl.pallas_call(functools.partial(ffn_kernel, groups, docs, rows), out_sha...  41.7 us
    pallas_call x1, Pallas kernels, finish_up(): pl.pallas_call(finish_kernel, grid=(SLOTS,), out_shape=[sds((SLOTS * t, d...  10.5 us

profile of v4, /device:TPU:4, one launch (start us, length us, event | category | flops | bytes accessed | tf_op | source)
XLA Modules:
  0.0 303.4 jit_solution(2961441074236670300)
XLA Ops:
  0.6 66.5 %attn_fwd.1 = (bf16[2,576,1024]{2,1,0:T(8,128)(2,1)}, bf16[4,2,192,256]{3,2,1,0:T(8,128)(2,1)}, bf16[2,192,192]{2,1,0:T(8,128)(2,1)}, bf16[2,192,192]{2,1,0:T(8,...) custom-call(s32[2]{0:T(128)} %len_ref.5, ...), custom_call_target="tpu_custom_call" | custom-call | flops 8000000000 | bytes 30000000 | tf_op jit(solution)/shard_map/attn_fwd/pallas_call | solution.py:431
  67.2 0.0 copy-start
  67.2 41.7 %ffn.1 = (bf16[2,4,256,768]{3,2,1,0:T(8,128)(2,1)}, f32[2,256,768]{2,1,0:T(8,128)}, bf16[4,2,192,256]{3,2,1,0:T(8,128)(2,1)}, bf16[4,2,2,216,768]{4,3,2,1,0:T(8,128)(2,1)}, f32[8,768]{1,0:T(8,128)}) custom-call(s32[2]{0:T(128)} %len_ref.5, bf16[2,1024,768]{2,1,0:T(8,128)(2,1)} %x_hbm.5, bf16[2,1024,768]{2,1,0:T(8,128)(2,1)} %cot_hbm.1, ...), custom_call_target="tpu_custom_call" | custom-call | flops 17999998976 | bytes 40000000 | tf_op jit(solution)/shard_map/ffn/pallas_call | solution.py:665
  109.0 0.0 copy-done
  109.0 0.7 rev.3.taps_ref
  109.6 183.1 %attn_bwd.1 = (bf16[576,768]{1,0:T(8,128)(2,1)}, bf16[2,8,128,768]{3,2,1,0:T(8,128)(2,1)}, f32[3,512]{1,0:T(4,128)}, bf16[8,216,768]{2,1,0:T(8,128)(2,1)}, f32[8...) custom-call(s32[2]{0:T(128)} %len_ref.5, bf16[2,1024,768]{2,1,0:T(8,128)(2,1)} %x_hbm.5, ...), custom_call_target="tpu_custom_call", output_to_operand_aliasing={{5}: (18, {})} | custom-call | flops 12000000000 | bytes 30000000 | tf_op jit(solution)/shard_map/attn_bwd/pallas_call | solution.py:1184
  292.7 10.5 %finish.1 = (f32[192,768]{1,0:T(8,128)}, f32[768,768]{1,0:T(8,128)}, f32[768,768]{1,0:T(8,128)}, f32[576,768]{1,0:T(8,128)}, bf16[2,1024,768]{2,1,0:T(8,128)(2,1...) custom-call(bf16[8,216,768]{2,1,0:T(8,128)(2,1)} %get-tuple-element., ...), custom_call_target="tpu_custom_call" | custom-call | tf_op jit(solution)/shard_map/finish/pallas_call | solution.py:1259
Async XLA Ops:
  67.2 41.8 %copy-start = (f32[3,33]{1,0:T(4,128)S(1)}, f32[3,33]{1,0:T(4,128)}, u32[]{:S(2)}) copy-start(f32[3,33]{1,0:T(4,128)} %taps_ref.1) | copy-start | bytes 1192

commit v5 on v4

--- a/solution.py
+++ b/solution.py
@@ -344,7 +344,7 @@
         l3_ref[d] = jnp.broadcast_to(m3 + jnp.log(t3), (width, 128))
         k3 = (e3 / t3).astype(BF)
         sum_s[d] = jnp.where(mask, nt(k3, v), 0.0)
-        at(d, {0: lambda: gather.step1(0)})
+        at(d, {0: lambda: (gather.step1(0),), 1: lambda: (gather.step1(1),)})
         return 0
 
     lax.fori_loop(0, docs, landmarks, 0)
@@ -366,7 +366,7 @@
             p_s[d, i, 1] = bs[d]
             p_s[d, i, 2] = cs[d]
             z_s[d, i + 1] = zs[d]
-        at(i, {1: lambda: gather.step1(1), 2: lambda: gather.step2(0), 3: lambda: (gather.step3(0), gather.step1(2)), 4: lambda: gather.step2(1), 5: lambda: gather.step3(1)})
+        at(i, {3: lambda: (gather.step1(2), gather.step2(0),)})
         return 0
 
     lax.fori_loop(0, NS_ITERS, newton, 0)
@@ -395,11 +395,12 @@
         for m in range(1, dest):
             a_copy(m, d).start()
         ctx_ref[me, d] = ctx_s[me, d]
-        at(d, {0: lambda: gather.step2(2)})
+        at(d, {0: lambda: (gather.step3(0), gather.step2(1), gather.step2(2),)})
         return 0
 
     lax.fori_loop(0, docs, contexts, 0)
     local.start(mix_s, mix_hbm)
+    gather.step3(1)
     gather.step3(2)
     gather.finish()
     for d in range(docs):
@@ -563,7 +564,7 @@
             br_s[...] += nn(act, take(g, 2)).astype(BF).astype(F32)
             return 0
 
-        lax.fori_loop(0, groups, fwd_group, 0)
+        lax.fori_loop(0, groups, fwd_group, 0, unroll=True)
         xh2, r2 = ln_stats(br_s[...])
         o_s[d] = (live * (xh2 * gain2 + bias2)).astype(BF)
 
@@ -750,6 +751,7 @@
         k3 = jnp.exp(s3 - l3_ref[d][:, 0:1])
         gk3 = nn(gsum_b, v)
         gs3 = (k3 * (gk3 - jnp.sum(gk3 * k3, axis=1, keepdims=True))).astype(BF)
+        at(d, {1: lambda: out_step(1)})
         glq_s[d] = jnp.where(mask, nt(gs3, k), 0.0) * SCALE
         glk_s[d] = jnp.where(mask, nt(gs1, q_), 0.0) * SCALE
         gs1_s[d] = gs1
@@ -770,7 +772,6 @@
     for d in range(docs):
         ginv_s[d] = z_s[d, NS_ITERS]
     lax.fori_loop(0, docs, doc, 0)
-    out_step(1)
     for h in range(heads):
         rolled = pltpu.roll(gacc_s[h], 0, 1, stride=1, stride_axis=0)
         taps_out[h : h + 1, :] = jnp.sum(rolled, axis=0, keepdims=True)

time: 305 us -> 289 us (0.948)
  Pallas kernels: 302 us -> 285 us
    pallas_call x1, Pallas kernels: 66.5 us -> 54.5 us  [attn_fwd(): pl.pallas_call(functools.partial(attn_fwd_kernel, docs, heads, seq, dest)...]
where the time goes in v5:
time: 289 us; the launch traced here: 287 us
  Pallas kernels  285 us (99%)
    pallas_call x1, Pallas kernels, attn_bwd(): pl.pallas_call(functools.partial(attn_bwd_kernel, docs, heads, seq, parts...  180 us
    pallas_call x1, Pallas kernels, attn_fwd(): pl.pallas_call(functools.partial(attn_fwd_kernel, docs, heads, seq, dest)...  54.5 us
    pallas_call x1, Pallas kernels, ffn(): pl.pallas_call(functools.partial(ffn_kernel, groups, docs, rows), out_sha...  39.9 us
    pallas_call x1, Pallas kernels, finish_up(): pl.pallas_call(finish_kernel, grid=(SLOTS,), out_shape=[sds((SLOTS * t, d...  10.5 us

profile of v5, /device:TPU:4, one launch (start us, length us, event | category | flops | bytes accessed | tf_op | source)
XLA Modules:
  0.0 287.0 jit_solution(13945280186833619085)
XLA Ops:
  0.6 54.5 %attn_fwd.1 = (bf16[2,576,1024]{2,1,0:T(8,128)(2,1)}, bf16[4,2,192,256]{3,2,1,0:T(8,128)(2,1)}, bf16[2,192,192]{2,1,0:T(8,128)(2,1)}, bf16[2,192,192]{2,1,0:T(8,...) custom-call(s32[2]{0:T(128)} %len_ref.5, ...), custom_call_target="tpu_custom_call" | custom-call | flops 8000000000 | bytes 30000000 | tf_op jit(solution)/shard_map/attn_fwd/pallas_call | solution.py:432
  55.2 0.0 copy-start
  55.2 39.9 %ffn.1 = (bf16[2,4,256,768]{3,2,1,0:T(8,128)(2,1)}, f32[2,256,768]{2,1,0:T(8,128)}, bf16[4,2,192,256]{3,2,1,0:T(8,128)(2,1)}, bf16[4,2,2,216,768]{4,3,2,1,0:T(8,128)(2,1)}, f32[8,768]{1,0:T(8,128)}) custom-call(s32[2]{0:T(128)} %len_ref.5, bf16[2,1024,768]{2,1,0:T(8,128)(2,1)} %x_hbm.5, bf16[2,1024,768]{2,1,0:T(8,128)(2,1)} %cot_hbm.1, ...), custom_call_target="tpu_custom_call" | custom-call | flops 17999998976 | bytes 40000000 | tf_op jit(solution)/shard_map/ffn/pallas_call | solution.py:666
  95.1 0.0 copy-done
  95.1 0.7 rev.3.taps_ref
  95.8 180.5 %attn_bwd.1 = (bf16[576,768]{1,0:T(8,128)(2,1)}, bf16[2,8,128,768]{3,2,1,0:T(8,128)(2,1)}, f32[3,512]{1,0:T(4,128)}, bf16[8,216,768]{2,1,0:T(8,128)(2,1)}, f32[8...) custom-call(s32[2]{0:T(128)} %len_ref.5, bf16[2,1024,768]{2,1,0:T(8,128)(2,1)} %x_hbm.5, ...), custom_call_target="tpu_custom_call", output_to_operand_aliasing={{5}: (18, {})} | custom-call | flops 12000000000 | bytes 30000000 | tf_op jit(solution)/shard_map/attn_bwd/pallas_call | solution.py:1185
  276.3 10.5 %finish.1 = (f32[192,768]{1,0:T(8,128)}, f32[768,768]{1,0:T(8,128)}, f32[768,768]{1,0:T(8,128)}, f32[576,768]{1,0:T(8,128)}, bf16[2,1024,768]{2,1,0:T(8,128)(2,1...) custom-call(bf16[8,216,768]{2,1,0:T(8,128)(2,1)} %get-tuple-element., ...), custom_call_target="tpu_custom_call" | custom-call | tf_op jit(solution)/shard_map/finish/pallas_call | solution.py:1260
Async XLA Ops:
  55.2 40.0 %copy-start = (f32[3,33]{1,0:T(4,128)S(1)}, f32[3,33]{1,0:T(4,128)}, u32[]{:S(2)}) copy-start(f32[3,33]{1,0:T(4,128)} %taps_ref.1) | copy-start | bytes 1192

commit v6 on v5

--- a/solution.py
+++ b/solution.py
@@ -1233,11 +1233,13 @@
 
 
 def finish_kernel(gw_ref, gq_ref, ig_ref, out_ref, small_ref, taps_ref, ow_o, up_o, dn_o, q_o, ig_o, out_o, g1_o, b1_o, g2_o, b2_o, taps_o):
+    each = gw_ref.shape[0]
     for i, o in enumerate((ow_o, up_o, dn_o)):
         lo, size = PARTS[i]
-        o[...] = gw_ref[0, lo : lo + size].astype(F32)
+        for j in range(each):
+            o[j * size : (j + 1) * size] = gw_ref[j, lo : lo + size].astype(F32)
     q_o[...] = gq_ref[...].astype(F32)
-    ig_o[...] = ig_ref[:, 0]
+    ig_o[...] = ig_ref[...].reshape(ig_o.shape)
     out_o[...] = out_ref[...]
 
     @pl.when(pl.program_id(0) == 0)
@@ -1252,27 +1254,29 @@
     groups, rows = out_rows.shape[1:3]
     seq = nchunk * chunk
     heads = taps.shape[0]
-    qrows = gq.shape[0] // SLOTS
-    per = seq // SLOTS
+    steps = 4
+    each = SLOTS // steps
+    qrows = gq.shape[0] // steps
+    per = seq // steps
     ratio = rows // per
     sds = jax.ShapeDtypeStruct
     whole = lambda shape: pl.BlockSpec(shape, lambda i: (0,) * len(shape))
     return pl.pallas_call(
         finish_kernel,
-        grid=(SLOTS,),
+        grid=(steps,),
         out_shape=[sds((SLOTS * t, dim), F32) for t in (OW_ROWS, UP_ROWS, DN_ROWS)]
         + [sds(gq.shape, F32), sds((docs, seq, dim), BF), sds((docs, seq, dim), BF)]
         + [sds((dim,), F32)] * 4
         + [sds((heads, KSIZE), F32)],
         in_specs=[
-            pl.BlockSpec((1, SLICE, dim), lambda i: (i, 0, 0)),
+            pl.BlockSpec((each, SLICE, dim), lambda i: (i, 0, 0)),
             pl.BlockSpec((qrows, dim), lambda i: (i, 0)),
-            pl.BlockSpec((docs, 1, chunk, dim), lambda i: (0, i, 0, 0)),
+            pl.BlockSpec((docs, nchunk // steps, chunk, dim), lambda i: (0, i, 0, 0)),
             pl.BlockSpec((docs, pl.Squeezed(), per, dim), lambda i: (0, i // ratio, i % ratio, 0)),
             whole(small.shape),
             whole(taps.shape),
         ],
-        out_specs=[pl.BlockSpec((t, dim), lambda i: (i, 0)) for t in (OW_ROWS, UP_ROWS, DN_ROWS, qrows)]
+        out_specs=[pl.BlockSpec((t, dim), lambda i: (i, 0)) for t in (each * OW_ROWS, each * UP_ROWS, each * DN_ROWS, qrows)]
         + [pl.BlockSpec((docs, per, dim), lambda i: (0, i, 0))] * 2
         + [whole((dim,))] * 4
         + [whole((heads, KSIZE))],

time: 289 us -> 287 us (level)
  no operation moved by 1% of the time
where the time goes in v6:
time: 287 us; the launch traced here: 285 us
  Pallas kernels  284 us (99%)
    pallas_call x1, Pallas kernels, attn_bwd(): pl.pallas_call(functools.partial(attn_bwd_kernel, docs, heads, seq, parts...  180 us
    pallas_call x1, Pallas kernels, attn_fwd(): pl.pallas_call(functools.partial(attn_fwd_kernel, docs, heads, seq, dest)...  54.5 us
    pallas_call x1, Pallas kernels, ffn(): pl.pallas_call(functools.partial(ffn_kernel, groups, docs, rows), out_sha...  39.9 us
    pallas_call x1, Pallas kernels, finish_up(): pl.pallas_call(finish_kernel, grid=(steps,), out_shape=[sds((SLOTS * t, d...  8.71 us

profile of v6, /device:TPU:4, one launch (start us, length us, event | category | flops | bytes accessed | tf_op | source)
XLA Modules:
  0.0 285.2 jit_solution(1623618334781735814)
XLA Ops:
  0.6 54.5 %attn_fwd.1 = (bf16[2,576,1024]{2,1,0:T(8,128)(2,1)}, bf16[4,2,192,256]{3,2,1,0:T(8,128)(2,1)}, bf16[2,192,192]{2,1,0:T(8,128)(2,1)}, bf16[2,192,192]{2,1,0:T(8,...) custom-call(s32[2]{0:T(128)} %len_ref.5, ...), custom_call_target="tpu_custom_call" | custom-call | flops 8000000000 | bytes 30000000 | tf_op jit(solution)/shard_map/attn_fwd/pallas_call | solution.py:432
  55.2 0.0 copy-start
  55.2 39.9 %ffn.1 = (bf16[2,4,256,768]{3,2,1,0:T(8,128)(2,1)}, f32[2,256,768]{2,1,0:T(8,128)}, bf16[4,2,192,256]{3,2,1,0:T(8,128)(2,1)}, bf16[4,2,2,216,768]{4,3,2,1,0:T(8,128)(2,1)}, f32[8,768]{1,0:T(8,128)}) custom-call(s32[2]{0:T(128)} %len_ref.5, bf16[2,1024,768]{2,1,0:T(8,128)(2,1)} %x_hbm.5, bf16[2,1024,768]{2,1,0:T(8,128)(2,1)} %cot_hbm.1, ...), custom_call_target="tpu_custom_call" | custom-call | flops 17999998976 | bytes 40000000 | tf_op jit(solution)/shard_map/ffn/pallas_call | solution.py:666
  95.1 0.0 copy-done
  95.1 0.7 rev.3.taps_ref
  95.8 180.5 %attn_bwd.1 = (bf16[576,768]{1,0:T(8,128)(2,1)}, bf16[2,8,128,768]{3,2,1,0:T(8,128)(2,1)}, f32[3,512]{1,0:T(4,128)}, bf16[8,216,768]{2,1,0:T(8,128)(2,1)}, f32[8...) custom-call(s32[2]{0:T(128)} %len_ref.5, bf16[2,1024,768]{2,1,0:T(8,128)(2,1)} %x_hbm.5, ...), custom_call_target="tpu_custom_call", output_to_operand_aliasing={{5}: (18, {})} | custom-call | flops 12000000000 | bytes 30000000 | tf_op jit(solution)/shard_map/attn_bwd/pallas_call | solution.py:1185
  276.3 8.7 %finish.1 = (f32[192,768]{1,0:T(8,128)}, f32[768,768]{1,0:T(8,128)}, f32[768,768]{1,0:T(8,128)}, f32[576,768]{1,0:T(8,128)}, bf16[2,1024,768]{2,1,0:T(8,128)(2,1...) custom-call(bf16[8,216,768]{2,1,0:T(8,128)(2,1)} %get-tuple-element., ...), custom_call_target="tpu_custom_call" | custom-call | tf_op jit(solution)/shard_map/finish/pallas_call | solution.py:1264
Async XLA Ops:
  55.2 40.0 %copy-start = (f32[3,33]{1,0:T(4,128)S(1)}, f32[3,33]{1,0:T(4,128)}, u32[]{:S(2)}) copy-start(f32[3,33]{1,0:T(4,128)} %taps_ref.1) | copy-start | bytes 1192

commit v7 on v6

--- a/solution.py
+++ b/solution.py
@@ -721,7 +721,8 @@
 
     out_step(0)
     taps_s[...] = jnp.zeros_like(taps_s)
-    taps_s[:, TAP0 : TAP0 + KSIZE] = taps_ref[...]
+    for i in range(KSIZE):
+        taps_s[:, TAP0 + KSIZE - 1 - i : TAP0 + KSIZE - i] = taps_ref[:, i : i + 1]
     mask = block_mask(width)
     eye = identity(width)
     anti = jnp.where(
@@ -1294,7 +1295,7 @@
         qkv, ctx, lq, lk, sm, mix, k2, z, p, l1, l3, wall = attn_fwd(lengths, tokens, wt, conv_taps, ow, up, dn, mp)
         out_rows, gmix, gctx, s1, small = ffn(lengths, tokens, cotangent, ctx, ow, up, dn, wall, norm1_gain, norm1_bias, norm2_gain, norm2_bias)
         gq, ig, gtaps, gw, small, out_rows = attn_bwd(
-            dp, lengths, tokens, wt, conv_taps[:, ::-1], qkv, gctx, lq, lk, sm, mix, k2, z, p, l1, l3, s1, small, gmix, out_rows
+            dp, lengths, tokens, wt, conv_taps, qkv, gctx, lq, lk, sm, mix, k2, z, p, l1, l3, s1, small, gmix, out_rows
         )
         g_ow, g_up, g_dn, gq, input_grad, output, g1, b1, g2, b2, g_taps = finish_up(gw, gq, ig, out_rows, small, gtaps)
         gqkv = jnp.transpose(gq.reshape(3, width, dim), (0, 2, 1))

time: 287 us -> 286 us (level)
  no operation moved by 1% of the time
where the time goes in v7:
time: 286 us; the launch traced here: 284 us
  Pallas kernels  283 us (99%)
    pallas_call x1, Pallas kernels, attn_bwd(): pl.pallas_call(functools.partial(attn_bwd_kernel, docs, heads, seq, parts...  180 us
    pallas_call x1, Pallas kernels, attn_fwd(): pl.pallas_call(functools.partial(attn_fwd_kernel, docs, heads, seq, dest)...  54.5 us
    pallas_call x1, Pallas kernels, ffn(): pl.pallas_call(functools.partial(ffn_kernel, groups, docs, rows), out_sha...  39.9 us
    pallas_call x1, Pallas kernels, finish_up(): pl.pallas_call(finish_kernel, grid=(steps,), out_shape=[sds((SLOTS * t, d...  8.71 us

profile of v7, /device:TPU:4, one launch (start us, length us, event | category | flops | bytes accessed | tf_op | source)
XLA Modules:
  0.0 284.2 jit_solution(3026319089170633502)
XLA Ops:
  0.6 54.5 %attn_fwd.1 = (bf16[2,576,1024]{2,1,0:T(8,128)(2,1)}, bf16[4,2,192,256]{3,2,1,0:T(8,128)(2,1)}, bf16[2,192,192]{2,1,0:T(8,128)(2,1)}, bf16[2,192,192]{2,1,0:T(8,...) custom-call(s32[2]{0:T(128)} %len_ref.5, ...), custom_call_target="tpu_custom_call" | custom-call | flops 8000000000 | bytes 30000000 | tf_op jit(solution)/shard_map/attn_fwd/pallas_call | solution.py:432
  55.2 39.9 %ffn.1 = (bf16[2,4,256,768]{3,2,1,0:T(8,128)(2,1)}, f32[2,256,768]{2,1,0:T(8,128)}, bf16[4,2,192,256]{3,2,1,0:T(8,128)(2,1)}, bf16[4,2,2,216,768]{4,3,2,1,0:T(8,128)(2,1)}, f32[8,768]{1,0:T(8,128)}) custom-call(s32[2]{0:T(128)} %len_ref.5, bf16[2,1024,768]{2,1,0:T(8,128)(2,1)} %x_hbm.5, bf16[2,1024,768]{2,1,0:T(8,128)(2,1)} %cot_hbm.1, ...), custom_call_target="tpu_custom_call" | custom-call | flops 17999998976 | bytes 40000000 | tf_op jit(solution)/shard_map/ffn/pallas_call | solution.py:666
  95.1 180.2 %attn_bwd.1 = (bf16[576,768]{1,0:T(8,128)(2,1)}, bf16[2,8,128,768]{3,2,1,0:T(8,128)(2,1)}, f32[3,512]{1,0:T(4,128)}, bf16[8,216,768]{2,1,0:T(8,128)(2,1)}, f32[8...) custom-call(s32[2]{0:T(128)} %len_ref.5, bf16[2,1024,768]{2,1,0:T(8,128)(2,1)} %x_hbm.5, ...), custom_call_target="tpu_custom_call", output_to_operand_aliasing={{5}: (18, {})} | custom-call | flops 12000000000 | bytes 30000000 | tf_op jit(solution)/shard_map/attn_bwd/pallas_call | solution.py:1186
  275.3 8.7 %finish.1 = (f32[192,768]{1,0:T(8,128)}, f32[768,768]{1,0:T(8,128)}, f32[768,768]{1,0:T(8,128)}, f32[576,768]{1,0:T(8,128)}, bf16[2,1024,768]{2,1,0:T(8,128)(2,1...) custom-call(bf16[8,216,768]{2,1,0:T(8,128)(2,1)} %get-tuple-element., ...), custom_call_target="tpu_custom_call" | custom-call | tf_op jit(solution)/shard_map/finish/pallas_call | solution.py:1265
